TPU v7x, 32 devices: a whole 2x2x4 slice. The times are simulated.
32 devices in a mesh: dp: 8 (over y, x, core), tensor: 4 (over z).
Axes of the slice: x: 2, y: 2, z: 4, core: 2. Of those that a mesh axis runs over, the one named last changes fastest.
Arguments:
- x_in: bfloat16 [8, 2048, 1536], P('dp'), may hold values from -6 to 6
- segments: int32 [8, 2048], P('dp'), may hold values from 0 to 4, as said below
- out_grad: bfloat16 [8, 2048, 1536], P('dp'), may hold values from -6 to 6
- norm_gain: float32 [1536], replicated, may hold values from 0.5 to 1.5
- w_z: bfloat16 [1536, 3072], P(None, 'tensor'), may hold values from -0.15625 to 0.15625
- w_x: bfloat16 [1536, 3072], P(None, 'tensor'), may hold values from -0.15625 to 0.15625
- w_bc: bfloat16 [1536, 256], replicated, may hold values from -0.15625 to 0.15625
- w_dt: bfloat16 [1536, 48], P(None, 'tensor'), may hold values from -0.15625 to 0.15625
- conv_x: float32 [4, 3072], P(None, 'tensor'), may hold values from -3 to 3
- conv_bc: float32 [4, 256], replicated, may hold values from -3 to 3
- bias_x: float32 [3072], P('tensor'), may hold values from -3 to 3
- bias_bc: float32 [256], replicated, may hold values from -3 to 3
- dt_bias: float32 [48], P('tensor'), may hold values from -4.5 to -2
- a_log: float32 [48], P('tensor'), may hold values from 0 to 2.77
- d_skip: float32 [48], P('tensor'), may hold values from 0.5 to 1.5
- out_gain: float32 [3072], P('tensor'), may hold values from 0.5 to 1.5
- w_out: bfloat16 [3072, 1536], P('tensor'), may hold values from -0.109375 to 0.109375
Outputs:
- y_out: bfloat16 [8, 2048, 1536], P('dp')
- x_grad: bfloat16 [8, 2048, 1536], P('dp')
- norm_gain_grad: float32 [1536], replicated
- w_z_grad: float32 [1536, 3072], P(None, 'tensor')
- w_x_grad: float32 [1536, 3072], P(None, 'tensor')
- w_bc_grad: float32 [1536, 256], replicated
- w_dt_grad: float32 [1536, 48], P(None, 'tensor')
- conv_x_grad: float32 [4, 3072], P(None, 'tensor')
- conv_bc_grad: float32 [4, 256], replicated
- bias_x_grad: float32 [3072], P('tensor')
- bias_bc_grad: float32 [256], replicated
- dt_bias_grad: float32 [48], P('tensor')
- a_log_grad: float32 [48], P('tensor')
- d_skip_grad: float32 [48], P('tensor')
- out_gain_grad: float32 [3072], P('tensor')
- w_out_grad: float32 [3072, 1536], P('tensor')
Inputs may be any that keep to these rules, and one draw needn't show every extreme that they name: `segments`: segment numbers never fall along a sequence and each of the 5 documents of a sequence holds 204 to 1024 neighbouring positions; one document of every sequence holds exactly 1024.
All inputs are finite; a program needn't handle non-finite values.
Results may differ from a plain program's by a relative error of at most 0.0083.
Values may be sent and summed in bfloat16 or wider, within the bound.
A program may use at most 192 MiB of HBM per device.

v0:
```python
from functools import partial

import jax
import jax.numpy as jnp
from jax import lax
from jax.sharding import PartitionSpec as P

GROUP = 256


epsilon = 1e-05


def outer_dot(left, right):
    return lax.dot_general(
        left, right, (((0,), (0,)), ((), ())), preferred_element_type=jnp.float32
    )


def back_dot(left, right):
    return lax.dot_general(
        left, right, (((1,), (1,)), ((), ())), preferred_element_type=jnp.float32
    )


def causal_conv(values, kernel, seg_ids):
    tap_count = kernel.shape[0]
    result = values * kernel[tap_count - 1]
    for offset in range(1, tap_count):
        earlier = jnp.concatenate(
            [jnp.zeros((offset, values.shape[1]), values.dtype), values[:-offset]], 0
        )
        prior_seg = jnp.concatenate([jnp.full((offset,), -1, jnp.int32), seg_ids[:-offset]], 0)
        same_seg = (prior_seg == seg_ids).astype(values.dtype)
        result = result + earlier * same_seg[:, None] * kernel[tap_count - 1 - offset]
    return result


def group_step(carry, inputs):
    carried, prev_seg = carry
    head_x, step_dt, log_decay, b_rows, c_rows, seg_rows = inputs
    cum_decay = jnp.cumsum(log_decay, axis=0)
    block_len = seg_rows.shape[0]
    position = jnp.arange(block_len)
    visible = (position[:, None] >= position[None, :]) & (seg_rows[:, None] == seg_rows[None, :])
    gap_decay = cum_decay[:, None, :] - cum_decay[None, :, :]
    decay_mat = jnp.exp(jnp.where(visible[:, :, None], gap_decay, 0.0)) * visible[
        :, :, None
    ].astype(cum_decay.dtype)
    scores = jnp.dot(c_rows, b_rows.T, precision=lax.Precision.HIGHEST)
    mixing = scores[:, :, None] * decay_mat * step_dt[None, :, :]
    inside = jnp.einsum("tsh,shp->thp", mixing, head_x, precision=lax.Precision.HIGHEST)
    keep_prev = (seg_rows == prev_seg).astype(cum_decay.dtype)
    entering = jnp.einsum("tn,hnp->thp", c_rows, carried, precision=lax.Precision.HIGHEST)
    entering = entering * (jnp.exp(cum_decay) * keep_prev[:, None])[:, :, None]
    last_seg = seg_rows[-1]
    to_end = (
        jnp.exp(cum_decay[-1][None, :] - cum_decay)
        * (seg_rows == last_seg).astype(cum_decay.dtype)[:, None]
        * step_dt
    )
    carry_scale = jnp.exp(cum_decay[-1]) * (last_seg == prev_seg).astype(cum_decay.dtype)
    updated = carried * carry_scale[:, None, None] + jnp.einsum(
        "sn,sh,shp->hnp", b_rows, to_end, head_x, precision=lax.Precision.HIGHEST
    )
    return ((updated, last_seg), inside + entering)


def state_scan(head_x, step_dt, log_decay, b_mat, c_mat, seg_ids):
    length, head_count, head_size = head_x.shape
    blocks = length // GROUP

    def to_blocks(array):
        return array.reshape((blocks, GROUP) + array.shape[1:])

    start = (jnp.zeros((head_count, b_mat.shape[1], head_size), head_x.dtype), jnp.int32(-1))
    final_state, outputs = lax.scan(
        jax.checkpoint(group_step),
        start,
        (
            to_blocks(head_x),
            to_blocks(step_dt),
            to_blocks(log_decay),
            to_blocks(b_mat),
            to_blocks(c_mat),
            to_blocks(seg_ids),
        ),
    )
    return outputs.reshape(length, head_count, head_size)


def bc_conv(values, kernel, shift_bc, seg_ids):
    return jax.nn.silu(causal_conv(values, kernel, seg_ids) + shift_bc)


def head_mix(
    gate_in, inner_in, dt_in, state_in, kernel_x, shift_x, dt_shift, decay_log, skip_gain, seg_ids
):
    length = inner_in.shape[0]
    head_count = dt_in.shape[1]
    mixed_x = jax.nn.silu(causal_conv(inner_in, kernel_x, seg_ids) + shift_x)
    head_x = mixed_x.reshape(length, head_count, -1)
    step_dt = jax.nn.softplus(dt_in + dt_shift)
    log_decay = -jnp.exp(decay_log) * step_dt
    state_dim = state_in.shape[1] // 2
    scanned = state_scan(
        head_x, step_dt, log_decay, state_in[:, :state_dim], state_in[:, state_dim:], seg_ids
    )
    scanned = scanned + skip_gain[None, :, None] * head_x
    return scanned.reshape(length, -1) * jax.nn.silu(gate_in)


def norm_back(tokens, inv_rms, gain, d_norm, upstream):
    width = tokens.shape[1]
    gain_grad = jnp.sum(d_norm * tokens * inv_rms, 0)
    inner_prod = jnp.sum(d_norm * gain * tokens, -1, keepdims=True)
    input_grad = (
        upstream.astype(jnp.float32)
        + inv_rms * gain * d_norm
        - tokens * inv_rms**3 * inner_prod / width
    )
    return (input_grad, gain_grad)


def on_device(
    x_in,
    segments,
    out_grad,
    norm_gain,
    w_z,
    w_x,
    w_bc,
    w_dt,
    conv_x,
    conv_bc,
    bias_x,
    bias_bc,
    dt_bias,
    a_log,
    d_skip,
    out_gain,
    w_out,
):
    tensor_count = lax.axis_size("tensor")
    place = lax.axis_index("tensor")
    tokens = x_in[0].astype(jnp.float32)
    seg_ids = segments[0]
    upstream = out_grad[0]
    inv_rms = lax.rsqrt(jnp.mean(tokens * tokens, -1, keepdims=True) + epsilon)
    normal_in = (tokens * inv_rms * norm_gain).astype(jnp.bfloat16)
    proj_z = jnp.dot(normal_in, w_z, preferred_element_type=jnp.float32)
    proj_x = jnp.dot(normal_in, w_x, preferred_element_type=jnp.float32)
    proj_bc = jnp.dot(normal_in, w_bc, preferred_element_type=jnp.float32)
    proj_dt = jnp.dot(normal_in, w_dt, preferred_element_type=jnp.float32)
    state_in, pull_bc = jax.vjp(partial(bc_conv, seg_ids=seg_ids), proj_bc, conv_bc, bias_bc)
    gated, pull_heads = jax.vjp(
        partial(head_mix, seg_ids=seg_ids),
        proj_z,
        proj_x,
        proj_dt,
        state_in,
        conv_x,
        bias_x,
        dt_bias,
        a_log,
        d_skip,
    )
    inner_total = gated.shape[1] * tensor_count
    square_sum = lax.psum(jnp.sum(gated * gated, -1), "tensor")
    inv_gate = lax.rsqrt(square_sum[:, None] / inner_total + epsilon)
    normed = (gated * inv_gate * out_gain).astype(jnp.bfloat16)
    projected = lax.psum(jnp.dot(normed, w_out, preferred_element_type=jnp.float32), "tensor")
    result = (tokens + projected).astype(jnp.bfloat16)
    grad_wout = outer_dot(normed, upstream)
    d_normed = back_dot(upstream, w_out)
    grad_gain_out = jnp.sum(d_normed * gated * inv_gate, 0)
    cross_sum = lax.psum(jnp.sum(d_normed * out_gain * gated, -1), "tensor")
    d_gated = (
        inv_gate * out_gain * d_normed - gated * inv_gate**3 * (cross_sum / inner_total)[:, None]
    )
    d_z, d_x, d_dt, d_state, grad_convx, grad_biasx, grad_dtb, grad_alog, grad_skip = pull_heads(
        d_gated
    )
    d_state_all = lax.psum(d_state, "tensor")
    d_bc, grad_convbc, grad_biasbc = pull_bc(d_state_all)
    dz_low = d_z.astype(jnp.bfloat16)
    dx_low = d_x.astype(jnp.bfloat16)
    ddt_low = d_dt.astype(jnp.bfloat16)
    dbc_low = d_bc.astype(jnp.bfloat16)
    grad_wz = outer_dot(normal_in, dz_low)
    grad_wx = outer_dot(normal_in, dx_low)
    grad_wdt = outer_dot(normal_in, ddt_low)
    grad_wbc = outer_dot(normal_in, dbc_low)
    columns = dbc_low.shape[1] // tensor_count
    bc_part = lax.dynamic_slice_in_dim(dbc_low, place * columns, columns, 1)
    wbc_part = lax.dynamic_slice_in_dim(w_bc, place * columns, columns, 1)
    total = back_dot(dz_low, w_z)
    total = total + back_dot(dx_low, w_x)
    total = total + back_dot(ddt_low, w_dt)
    d_norm = lax.psum(total + back_dot(bc_part, wbc_part), "tensor")
    grad_full, grad_gain_in = norm_back(tokens, inv_rms, norm_gain, d_norm, upstream)
    grad_in = grad_full.astype(jnp.bfloat16)
    summed = lax.psum(
        (
            grad_gain_in,
            grad_wz,
            grad_wx,
            grad_wbc,
            grad_wdt,
            grad_convx,
            grad_convbc,
            grad_biasx,
            grad_biasbc,
            grad_dtb,
            grad_alog,
            grad_skip,
            grad_gain_out,
            grad_wout,
        ),
        "dp",
    )
    return (
        result[None],
        grad_in[None],
        summed[0],
        summed[1],
        summed[2],
        summed[3],
        summed[4],
        summed[5],
        summed[6],
        summed[7],
        summed[8],
        summed[9],
        summed[10],
        summed[11],
        summed[12],
        summed[13],
    )


def solution(mesh):
    in_specs = (
        P("dp", None, None),
        P("dp", None),
        P("dp", None, None),
        P(),
        P(None, "tensor"),
        P(None, "tensor"),
        P(),
        P(None, "tensor"),
        P(None, "tensor"),
        P(),
        P("tensor"),
        P(),
        P("tensor"),
        P("tensor"),
        P("tensor"),
        P("tensor"),
        P("tensor", None),
    )
    out_specs = (
        P("dp", None, None),
        P("dp", None, None),
        P(),
        P(None, "tensor"),
        P(None, "tensor"),
        P(),
        P(None, "tensor"),
        P(None, "tensor"),
        P(),
        P("tensor"),
        P(),
        P("tensor"),
        P("tensor"),
        P("tensor"),
        P("tensor"),
        P("tensor", None),
    )
    return jax.shard_map(
        on_device, mesh=mesh, in_specs=in_specs, out_specs=out_specs, check_vma=False
    )
```

profile of v0, /device:TPU:0, one launch (start us, length us, event | category | flops | bytes accessed | tf_op | source)
XLA Modules:
  0.0 2381.7 jit_solution(5995256664528491353)
XLA Ops:
  26.3 8.3 fusion.120
  34.7 6.9 copy.107
  61.1 311.1 %while.45 = (s32[]{:T(128)}, f32[12,128,64]{1,2,0:T(8,128)S(1)}, s32[]{:T(128)}, f32[8,256,12,64]{1,0,3,2:T(8,128)}, f32[8,12,128,64]{2,3,1,0:T(8,128)}, /*index...) while((s32[]{:T(128)}, f32[12,128,64]{1,2,0:T(8,128)S(1)}, ...), condition=%wide.region_4.5_spmd.clone, body=%wide.region_1.4_spmd.clone.sunk | while | flops 1314108416 | bytes 11502541 | solution.py:77
  76.9 18.5 dynamic_update_slice.85
  115.7 18.5 dynamic_update_slice.85
  154.5 18.5 dynamic_update_slice.85
  193.3 18.5 dynamic_update_slice.85
  232.2 18.5 dynamic_update_slice.85
  271.0 18.5 dynamic_update_slice.85
  309.8 18.5 dynamic_update_slice.85
  348.6 18.5 dynamic_update_slice.85
  372.3 8.4 copy.183
  380.7 6.6 copy.112
  387.4 15.5 multiply_reduce_fusion.11
  402.9 13.6 psum.133
  416.6 11.8 multiply_reduce_fusion.4
  428.4 8.5 psum.135
  436.9 16.9 multiply_reduce_fusion.5
  453.8 6.6 copy.113
  460.4 8.5 copy.184
  475.7 722.4 %while.46 = (s32[]{:T(128)}, f32[12,128,64]{1,2,0:T(8,128)}, f32[8,256,12,64]{1,0,3,2:T(8,128)}, f32[8,256,12]{1,0,2:T(8,128)}, f32[8,256,12]{1,0,2:T(8,128)}, /...) while((s32[]{:T(128)}, f32[12,128,64]{1,2,0:T(8,128)}, ...), condition=%wide.region_22.23_spmd.clone, body=%wide.region_10.22_spmd.clone.sunk | while | flops 3038993408 | bytes 37520120 | solution.py:77
  515.8 6.4 fusion.266
  532.7 18.5 dynamic_update_slice.89
  606.1 6.4 fusion.266
  623.1 18.5 dynamic_update_slice.89
  713.4 18.5 dynamic_update_slice.89
  803.8 18.5 dynamic_update_slice.89
  894.1 18.5 dynamic_update_slice.89
  984.5 18.5 dynamic_update_slice.89
  1057.8 6.4 fusion.266
  1074.8 18.5 dynamic_update_slice.89
  1165.2 18.5 dynamic_update_slice.89
  1201.4 8.4 copy.185
  1209.8 6.6 copy.119
  1216.4 18.5 fusion.143
  1248.9 8.1 fusion.158
  1263.5 10.3 fusion.157
  1273.9 11.0 fusion.142
  1287.5 6.6 fusion.144
  1295.9 17.9 add_add_fusion
  1318.4 9.9 fusion.160
  1328.3 6.9 fusion.159
  1335.2 7.0 fusion.115
  1346.2 800.8 %all-reduce.37.cloned.1.call-done = (f32[2048,1536]{1,0:T(8,128)}, f32[2048,1536]{1,0:T(8,128)}) async-done(((f32[2048,1536]{1,0:T(8,128)}, f32[2048,1536]{1,0:T(8,128)}), (f32[2048,1536]{1,0:T(8,128)}, f32[2048,1536]{1,0:T(8,128)})) %all-reduce.37.cloned.1.call-update) | async-done | bytes 25165840 | tf_op jit(solution)/shard_map/psum | solution.py:172
  2147.0 8.9 fusion.104
  2155.9 27.5 %all-reduce.26 = (f32[1536]{0:T(1024)}, f32[4,768]{1,0:T(4,128)}, f32[4,256]{1,0:T(4,128)}, f32[768]{0:T(1024)}, f32[256]{0:T(256)}, /*index=5*/f32[12]{0:T(128)}, f32[12]{0:T(128)}, f32[12]{0:T(128)}, f32[768]{0:T(1024)}) all-reduce(f32[1536]{0:T(1024)S(1)} %get-tuple-element.681, ...), channel_id=1, replica_groups=mesh['dp'=8,'tensor'=4] {'dp'}, use_global_device_ids=true, to_apply=%region_27.28 | all-reduce | flops 7460 | bytes 59680 | tf_op jit(solution)/shard_map/psum | solution.py:203
  2183.4 19.4 fusion.110
  2202.8 159.3 %all-reduce.35.cloned.1.call-done = (f32[1536,768]{1,0:T(8,128)}, f32[1536,768]{1,0:T(8,128)}, f32[1536,256]{1,0:T(8,128)}, f32[1536,12]{0,1:T(8,128)}, f32[768,1536]{1,0:T(8,128)}) async-done(((f32[1536,768]{1,0:T(8,128)}, f32[1536,768]{1,0:T(8,128)}, f32[1536,256]{1,0:T(8,128)}, f32[1536,12]{0,1:T(8,128)}, f32[768,1536]{1,0:T(8,128)}), (f32[1536,768]{1,0:T(8,128)}, f32[1536,768]{1,0:T(8,128)}, ...) | async-done | bytes 15802384 | tf_op jit(solution)/shard_map/psum | solution.py:203
  (1112 shorter events, 787.7 us)
Async XLA Ops:
  7.2 380.2 %copy-start = (bf16[1536,768]{1,0:T(8,128)(2,1)S(1)}, bf16[1536,768]{1,0:T(8,128)(2,1)}, u32[]{:S(2)}) copy-start(bf16[1536,768]{1,0:T(8,128)(2,1)} %param.25) | copy-start | bytes 7077892
  7.2 1280.3 %all-reduce.33.cloned.1.call-start = ((), (), s32[]{:S(2)}) async-start(), calls=%async_computation | async-start | bytes 4194304 | tf_op jit(solution)/shard_map/psum | solution.py:184
  15.8 10.5 copy-start.23
  15.8 10.5 copy-start.25
  15.8 10.5 copy-start.27
  41.5 10.6 slice-start
  387.4 49.5 %copy-start.49 = (f32[768]{0:T(1024)}, f32[768]{0:T(1024)S(1)}, u32[]{:S(2)}) copy-start(f32[768]{0:T(1024)S(1)} %mul.977) | copy-start | bytes 9220
  387.4 29.2 %copy-start.69 = (f32[768]{0:T(1024)S(1)}, f32[768]{0:T(1024)}, u32[]{:S(2)}) copy-start(f32[768]{0:T(1024)} %param.36) | copy-start | bytes 9220
  416.6 20.3 copy-start.53
  515.7 9.7 copy-start.2
  515.7 11.1 copy-start.6
  515.7 12.4 copy-start.9
  606.1 9.7 copy-start.2
  606.1 11.1 copy-start.6
  606.1 12.3 copy-start.9
  696.4 9.7 copy-start.2
  696.4 11.1 copy-start.6
  696.4 12.4 copy-start.9
  786.8 9.7 copy-start.2
  786.8 11.1 copy-start.6
  786.8 12.3 copy-start.9
  877.1 9.7 copy-start.2
  877.1 11.1 copy-start.6
  877.1 12.3 copy-start.9
  967.5 9.7 copy-start.2
  967.5 11.1 copy-start.6
  967.5 12.4 copy-start.9
  1057.8 9.7 copy-start.2
  1057.8 11.1 copy-start.6
  1057.8 12.4 copy-start.9
  1148.2 9.7 copy-start.2
  1148.2 11.1 copy-start.6
  1148.2 12.3 copy-start.9
  1201.1 945.8 %all-reduce.37.cloned.1.call-start = ((), (), s32[]{:S(2)}) async-start(), calls=%async_computation.2 | async-start | bytes 50331648 | tf_op jit(solution)/shard_map/psum | solution.py:172
  1216.4 18.5 copy-start.48
  1263.5 10.3 copy-start.54
  1263.5 10.3 copy-start.70
  1263.5 10.3 copy-start.78
  1313.8 1048.4 %all-reduce.35.cloned.1.call-start = ((), (), s32[]{:S(2)}) async-start(), calls=%async_computation.1 | async-start | bytes 31653888 | tf_op jit(solution)/shard_map/psum | solution.py:203
  1313.8 14.4 slice-start.2
  1318.3 9.9 slice-start.3
  1318.3 9.9 copy-start.14
  1318.3 16.9 slice-start.4
  1318.3 16.9 slice-start.6
  1345.3 801.7 %copy-start.35 = (f32[2048]{0:T(1024)S(1)}, f32[2048]{0:T(1024)}, u32[]{:S(2)}) copy-start(f32[2048]{0:T(1024)} %copy-done.34) | copy-start | bytes 24580
  1345.3 801.7 %copy-start.41 = (f32[1536]{0:T(1024)S(1)}, f32[1536]{0:T(1024)}, u32[]{:S(2)}) copy-start(f32[1536]{0:T(1024)} %param.24) | copy-start | bytes 18436
  2147.0 36.4 %copy-start.55 = (f32[2048]{0:T(1024)S(1)}, f32[2048]{0:T(1024)}, u32[]{:S(2)}) copy-start(f32[2048]{0:T(1024)} %get-tuple-element.818) | copy-start | bytes 24580
  2362.1 10.6 slice-start.8
  (151 other events, 839.2 us)
Sparse Core Ops, SparseCore 0:
  1201.3 86.2 all-reduce.32
  1313.9 833.0 all-reduce.36
  2152.8 209.2 all-reduce.34
where the time goes:
time: 2400 us; the launch traced here: 2380 us
  waiting for transfers between devices  963 us (40%)
  local copies, waits for them, and re-layouts  660 us (28%)
  matrix products  390 us (16%)
  other arithmetic  278 us (12%)
  blocking collectives  49.6 us (2%)
  loops' own time  25.3 us (1%)
    psum x1, waiting for transfers between devices, on_device(): lax.psum(jnp.dot(normed, w_out, preferred_element_type=jnp.float32), 'ten...  801 us
    dynamic_update_slice x72, local copies, waits for them, and re-layouts, state_scan(): lax.scan(jax.checkpoint(group_step), start, (to_blocks(head_x), to_blocks...  357 us
    psum x1, waiting for transfers between devices, on_device(): lax.psum((grad_gain_in, grad_wz, grad_wx, grad_wbc, grad_wdt, grad_convx,...  159 us
    dot_general x24, matrix products, group_step(): jnp.einsum('tsh,shp->thp', mixing, head_x, precision=lax.Precision.HIGHEST)  115 us
    another operation x81, other arithmetic  68 us
    another operation x134, local copies, waits for them, and re-layouts  65.5 us
    squeeze x32, local copies, waits for them, and re-layouts, state_scan(): lax.scan(jax.checkpoint(group_step), start, (to_blocks(head_x), to_blocks...  55.4 us
    dot_general x24, matrix products, group_step(): jnp.einsum('sn,sh,shp->hnp', b_rows, to_end, head_x, precision=lax.Precis...  54.6 us
  transfers between devices with their start and end apart: 3, of which 3 were waited for; matrix products, arithmetic and copies ran while one was open for 6% of the time, Pallas kernels for 0%

commit v1 on v0

v1 whole, which is shorter than its diff:
```python
import functools

import jax
import jax.numpy as jnp
from jax import lax
from jax.experimental import pallas as pl
from jax.experimental.pallas import tpu as pltpu
from jax.sharding import PartitionSpec as P

EPS = 1e-05
CHUNK = 128
BLOCK = 256
LANES = 128
F32 = jnp.float32
BF16 = jnp.bfloat16
HIGHEST = lax.Precision.HIGHEST


def dot(a, b, precision=None):
    return lax.dot_general(a, b, (((1,), (0,)), ((), ())), precision=precision, preferred_element_type=F32)


def dot_t(a, b):
    return lax.dot_general(a, b, (((1,), (1,)), ((), ())), preferred_element_type=F32)


def tdot(a, b):
    return lax.dot_general(a, b, (((0,), (0,)), ((), ())), preferred_element_type=F32)


def sigmoid(v):
    return 1.0 / (1.0 + jnp.exp(-v))


def softplus(v):
    e = jnp.exp(-jnp.abs(v))
    series = e * (1.0 - e * (0.5 - e * (1.0 / 3.0 - e * 0.25)))
    return jnp.maximum(v, 0.0) + jnp.where(e < 0.03, series, jnp.log(1.0 + e))


def spread(columns, heads):
    rows = columns.shape[0]
    low = lax.broadcasted_iota(jnp.int32, (rows, LANES), 1) < LANES // 2
    pieces = []
    for pair in range(heads // 2):
        first = columns[:, 2 * pair : 2 * pair + 1]
        second = columns[:, 2 * pair + 1 : 2 * pair + 2]
        pieces.append(jnp.where(low, first, second))
    return jnp.concatenate(pieces, axis=1)


def iotas(rows, cols):
    return (
        lax.broadcasted_iota(jnp.int32, (rows, cols), 0),
        lax.broadcasted_iota(jnp.int32, (rows, cols), 1),
    )


def decays(la, seg_col, seg_row):
    r, c = iotas(CHUNK, CHUNK)
    lower = (r >= c).astype(F32)
    cum = dot(lower, la, HIGHEST)
    visible = (r >= c) & (seg_col == seg_row)
    return cum, cum.T, visible


def decay_matrix(cum, cum_t, visible, head):
    gap = cum[:, head : head + 1] - cum_t[head : head + 1, :]
    return jnp.exp(jnp.where(visible, gap, -1e30))


def split_pair(values):
    low = lax.broadcasted_iota(jnp.int32, values.shape, 1) < LANES // 2
    zero = jnp.zeros_like(values)
    return jnp.where(low, values, zero), jnp.where(low, zero, values)


def conv_taps(hist, weight, meta, rows):
    out = hist[8 : 8 + rows, :] * weight[3:4, :]
    for k in range(1, 4):
        out = out + hist[8 - k : 8 - k + rows, :] * meta[:, k - 1 : k] * weight[3 - k : 4 - k, :]
    return out


MESH = pl.DeviceIdType.MESH


def greet(count):
    me = lax.axis_index("tensor")
    barrier = pltpu.get_barrier_semaphore()
    left, right = me > 0, me < count - 1

    @pl.when(left)
    def _():
        pl.semaphore_signal(barrier, inc=1, device_id={"tensor": me - 1}, device_id_type=MESH)

    @pl.when(right)
    def _():
        pl.semaphore_signal(barrier, inc=1, device_id={"tensor": me + 1}, device_id_type=MESH)

    pl.semaphore_wait(barrier, left.astype(jnp.int32) + right.astype(jnp.int32))


class Line:
    def __init__(self, count, pairs, half, steps, refs, own):
        self.count, self.pairs, self.half, self.steps, self.own = count, pairs, half, steps, own
        (self.res, self.land, self.mine, self.send, self.red_out, self.red_in, self.bc_out, self.bc_in, self.local) = refs

    def slot(self, k):
        return jnp.where(k < self.half, k, 3 * self.half - 1 - k)

    def flow(self, f):
        me = lax.axis_index("tensor")
        if f == 0:
            return me, me - 1, me + 1
        return self.count - 1 - me, me + 1, me - 1

    def red(self, f, ls, toward):
        return pltpu.make_async_remote_copy(
            src_ref=self.send.at[f], dst_ref=self.land.at[ls + 1, f], send_sem=self.red_out.at[f, ls],
            recv_sem=self.red_in.at[f, ls], device_id={"tensor": toward}, device_id_type=MESH,
        )

    def cast(self, f, ls, away, k, src=None):
        there = self.res.at[self.slot(k), f]
        return pltpu.make_async_remote_copy(
            src_ref=there if src is None else src, dst_ref=there, send_sem=self.bc_out.at[f, ls],
            recv_sem=self.bc_in.at[f, ls], device_id={"tensor": away}, device_id_type=MESH,
        )

    def finish(self, f, s, ls):
        z, toward, away = self.flow(f)
        n = self.count
        i = s - (n - 1) + z
        k = s - (n - 1) - z
        i_ok = (i >= 0) & (i < self.pairs)
        k_ok = (k >= 0) & (k < self.pairs)

        @pl.when(i_ok & (z > 0))
        def _():
            self.red(f, ls, toward).wait_send()

        @pl.when(k_ok & (z < n - 1))
        def _():
            self.cast(f, ls, away, k).wait_send()

        @pl.when((i + 1 >= 0) & (i + 1 < self.pairs) & (z < n - 1))
        def _():
            self.red(f, ls, toward).wait_recv()

        @pl.when((k + 1 >= 0) & (k + 1 < self.pairs) & (z > 0))
        def _():
            self.cast(f, ls, away, k + 1).wait_recv()

    def step(self, s, ls):
        n = self.count
        for f in range(2):

            @pl.when(ls > 0)
            def _():
                self.finish(f, s - 1, ls - 1)

            z, toward, away = self.flow(f)
            i = s - (n - 1) + z
            k = s - (n - 1) - z

            @pl.when((i >= 0) & (i < self.pairs))
            def _():
                self.own(self.mine.at[f], f, i, self.local.at[f])

                @pl.when(z == n - 1)
                def _():
                    self.send[f] = self.mine[f]

                @pl.when(z < n - 1)
                def _():
                    total = self.mine[f].astype(F32) + self.land[ls, f].astype(F32)
                    self.send[f] = total.astype(BF16)

                @pl.when(z > 0)
                def _():
                    self.red(f, ls, toward).start()

                @pl.when(z == 0)
                def _():
                    self.cast(f, ls, away, i, self.send.at[f]).start()
                    keep = pltpu.make_async_copy(self.send.at[f], self.res.at[self.slot(i), f], self.local.at[f])
                    keep.start()
                    keep.wait()

            @pl.when((k >= 0) & (k < self.pairs) & (z > 0) & (z < n - 1))
            def _():
                self.cast(f, ls, away, k).start()

    def open(self, carry):
        for f in range(2):
            if carry is not None:
                self.land[0, f] = carry[f]

    def close(self, s, ls, carry):
        for f in range(2):
            self.finish(f, s, ls)
            z, _, _ = self.flow(f)
            i = s + 1 - (self.count - 1) + z
            got = (i >= 0) & (i < self.pairs) & (z < self.count - 1)
            if carry is None:
                continue

            @pl.when(got)
            def _():
                carry[f] = self.land[ls + 1, f]

            @pl.when(jnp.logical_not(got))
            def _():
                carry[f] = jnp.zeros(carry.shape[1:], carry.dtype)


def line_scratch(steps, rows, width):
    return [
        pltpu.VMEM((steps + 1, 2, rows, width), BF16),
        pltpu.VMEM((2, rows, width), BF16),
        pltpu.VMEM((2, rows, width), BF16),
        pltpu.SemaphoreType.DMA((2, steps)),
        pltpu.SemaphoreType.DMA((2, steps)),
        pltpu.SemaphoreType.DMA((2, steps)),
        pltpu.SemaphoreType.DMA((2, steps)),
        pltpu.SemaphoreType.DMA((2,)),
    ]


def bring(src, dst, sem):
    copy = pltpu.make_async_copy(src, dst, sem)
    copy.start()
    copy.wait()


def line_kernel(count, pairs, half, first, steps, y_ref, x_ref, carry_ref, res_in, res_ref, *scratch):
    del res_in

    def own(dst, f, i, sem):
        @pl.when(i < half)
        def _():
            bring(y_ref.at[i, f], dst, sem)

        @pl.when(i >= half)
        def _():
            bring(x_ref.at[2 * half - 1 - i, f], dst, sem)

    line = Line(count, pairs, half, steps, (res_ref, *scratch), own)
    at = pl.program_id(0)

    @pl.when(at == 0)
    def _():
        greet(count)
        line.open(carry_ref)

    line.step(first + at, at)

    @pl.when(at == steps - 1)
    def _():
        line.close(first + at, at, None)


def forward_kernel(
    heads, count, pairs, half, steps, when,
    x_ref, g_ref, seg_ref, meta_ref, wz_ref, wx_ref, wbc_ref, wdt_ref, wo_ref, ng_ref,
    cx_ref, bx_ref, cbc_ref, bbc_ref, dtb_ref, al_ref, dsk_ref, og_ref,
    z_ref, p_ref, xc_ref, ys_ref, pbc_ref, bc_ref, dtr_ref, dn_ref, xn_ref, st_ref, yp_ref, stat_ref,
    carry_out, res_ref, hist, hist_bc, state, part, *scratch,
):
    rows = x_ref.shape[0]
    width = x_ref.shape[1]
    block = pl.program_id(0)

    def own(dst, f, i, sem):
        bring(part.at[i, f], dst, sem)

    line = Line(count, pairs, half, steps, (res_ref, *scratch), own)

    @pl.when(block == 0)
    def _():
        greet(count)
        hist[0:8, :] = jnp.zeros((8, hist.shape[1]), F32)
        hist_bc[0:8, :] = jnp.zeros((8, hist_bc.shape[1]), F32)
        state[...] = jnp.zeros_like(state)

    x = x_ref[...].astype(F32)
    r1 = lax.rsqrt(jnp.sum(x * x, axis=1, keepdims=True) * (1.0 / width) + EPS)
    xn = (x * r1 * ng_ref[...]).astype(BF16)
    xn_ref[...] = xn
    z_ref[...] = dot(xn, wz_ref[...])
    xc = dot(xn, wx_ref[...])
    bc = dot(xn, wbc_ref[...])
    dtr = dot(xn, wdt_ref[...])
    xc_ref[...] = xc.astype(BF16)
    bc_ref[...] = bc
    dtr_ref[...] = dtr
    hist[8 : 8 + rows, :] = xc
    hist_bc[8 : 8 + rows, :] = bc
    meta = meta_ref[...]
    p_ref[...] = conv_taps(hist, cx_ref, meta, rows) + bx_ref[...]
    pbc_ref[...] = conv_taps(hist_bc, cbc_ref, meta, rows) + bbc_ref[...]
    hist[0:8, :] = hist[rows : rows + 8, :]
    hist_bc[0:8, :] = hist_bc[rows : rows + 8, :]
    g = g_ref[...]
    dn_ref[...] = dot_t(g, wo_ref[...])
    dt_all = softplus(dtr + dtb_ref[...])
    la_all = -jnp.exp(al_ref[...]) * dt_all
    lane8 = lax.broadcasted_iota(jnp.int32, (CHUNK, 8), 1)
    for piece in range(rows // CHUNK):
        at = pl.ds(piece * CHUNK, CHUNK)
        span = slice(piece * CHUNK, (piece + 1) * CHUNK)
        seg_col = meta[span, 6:7]
        keep = meta[span, 7:8]
        tail = meta[span, 8:9]
        dt = dt_all[span, :]
        cum, cum_t, visible = decays(la_all[span, :], seg_col, seg_ref[:, span])
        p = p_ref[at, :]
        u = p * sigmoid(p)
        pbc = pbc_ref[at, :]
        bcu = (pbc * sigmoid(pbc)).astype(BF16)
        n = bcu.shape[1] // 2
        b, c = bcu[:, :n], bcu[:, n:]
        scores = dot_t(c, b)
        v = spread(dt, heads) * u
        v_low = v.astype(BF16)
        pieces = []
        for pair in range(heads // 2):
            mats = [
                (scores * decay_matrix(cum, cum_t, visible, 2 * pair + k)).astype(BF16)
                for k in range(2)
            ]
            halves = split_pair(v_low[:, pair * LANES : (pair + 1) * LANES])
            pieces.append(dot(jnp.concatenate(mats, axis=1), jnp.concatenate(halves, axis=0)))
        inside = jnp.concatenate(pieces, axis=1)
        old = state[...]
        old_low = old.astype(BF16)
        st_ref[piece] = old_low
        entering = dot(c, old_low) * spread(jnp.exp(cum) * keep, heads)
        last = cum[CHUNK - 1 : CHUNK, :]
        to_end = spread(jnp.exp(last - cum) * tail, heads)
        carry = spread(jnp.exp(last) * keep[CHUNK - 1 : CHUNK, :], heads)
        state[...] = old * carry + tdot(b, (to_end * v).astype(BF16))
        ys = inside + entering + dsk_ref[...] * u
        ys_ref[at, :] = ys
        z = z_ref[at, :]
        gated = ys * (z * sigmoid(z))
        scaled = gated * og_ref[...]
        y_part = dot(scaled.astype(BF16), wo_ref[...]).astype(BF16)
        yp_ref[0, piece] = y_part
        part[block, piece] = y_part
        sums = jnp.sum(gated * gated, axis=1, keepdims=True)
        inner = jnp.sum(dn_ref[at, :] * scaled, axis=1, keepdims=True)
        stat_ref[at, :] = jnp.where(lane8 == 0, sums, jnp.where(lane8 == 1, inner, 0.0))
    run_steps(line, block, when, 0)

    @pl.when(block == len(when) - 1)
    def _():
        line.close(steps - 1, steps - 1, carry_out)


def run_steps(line, block, when, first):
    for b, ls in enumerate(when):
        if ls >= 0:

            @pl.when(block == b)
            def _():
                line.step(first + ls, ls)


def backward_kernel(
    heads, count, pairs, half, first, steps, when,
    z_ref, p_ref, xc_ref, ys_ref, pbc_ref, bc_ref, dtr_ref, dn_ref, st_ref, seg_ref, meta_ref, scal_ref,
    wz_ref, wx_ref, wbc_ref, wdt_ref, cx_ref, cbc_ref, dtb_ref, al_ref, dsk_ref, og_ref, y_ref, carry_ref, res_in,
    dz_ref, dx_ref, ddt_ref, dbc_ref, xp_ref, nm_ref, a768_ref, a256_ref, a128_ref,
    carry_out, res_ref, ahead, ahead_bc, d_state, part, *scratch,
):
    del res_in
    rows = z_ref.shape[0]
    inner = z_ref.shape[1]
    block = pl.program_id(0)

    def own(dst, f, i, sem):
        @pl.when(i < half)
        def _():
            bring(y_ref.at[i, f], dst, sem)

        @pl.when(i >= half)
        def _():
            bring(part.at[i - half, f], dst, sem)

    line = Line(count, pairs, half, steps, (res_ref, *scratch), own)

    @pl.when(block == 0)
    def _():
        greet(count)
        line.open(carry_ref)
        ahead[rows : rows + 8, :] = jnp.zeros((8, ahead.shape[1]), F32)
        ahead_bc[rows : rows + 8, :] = jnp.zeros((8, ahead_bc.shape[1]), F32)
        d_state[...] = jnp.zeros_like(d_state)
        a768_ref[...] = jnp.zeros_like(a768_ref)
        a256_ref[...] = jnp.zeros_like(a256_ref)
        a128_ref[...] = jnp.zeros_like(a128_ref)

    meta = meta_ref[...]
    r, c_ = iotas(CHUNK, CHUNK)
    upper = (r <= c_).astype(F32)
    below = (r > c_).astype(F32)
    seg_r, seg_l = iotas(inner, LANES)
    to_head = (seg_r // (inner // heads) == seg_l).astype(BF16)
    two_r, two_l = iotas(2 * CHUNK, LANES)
    decay_rate = -jnp.exp(al_ref[...])
    for piece in reversed(range(rows // CHUNK)):
        at = pl.ds(piece * CHUNK, CHUNK)
        span = slice(piece * CHUNK, (piece + 1) * CHUNK)
        seg_col = meta[span, 6:7]
        keep = meta[span, 7:8]
        tail = meta[span, 8:9]
        r2 = scal_ref[at, 0:1]
        k2 = scal_ref[at, 1:2]
        pre = dtr_ref[at, :] + dtb_ref[...]
        dt = softplus(pre)
        la = decay_rate * dt
        cum, cum_t, visible = decays(la, seg_col, seg_ref[:, span])
        z = z_ref[at, :]
        ys = ys_ref[at, :]
        sz = sigmoid(z)
        silu = z * sz
        gated = ys * silu
        dn = dn_ref[at, :]
        og = og_ref[...]
        d_gated = r2 * og * dn - gated * k2
        nm_ref[at, :] = (gated * r2 * og).astype(BF16)
        a768_ref[6:7, :] += jnp.sum(dn * gated * r2, axis=0, keepdims=True)
        dz_ref[at, :] = (d_gated * ys * (sz * (1.0 + z * (1.0 - sz)))).astype(BF16)
        dy = d_gated * silu
        dy_low = dy.astype(BF16)
        p = p_ref[at, :]
        sp = sigmoid(p)
        u = p * sp
        a768_ref[5:6, :] += jnp.sum(dy * u, axis=0, keepdims=True)
        pbc = pbc_ref[at, :]
        spbc = sigmoid(pbc)
        bcu = (pbc * spbc).astype(BF16)
        n = bcu.shape[1] // 2
        b, c = bcu[:, :n], bcu[:, n:]
        scores = dot_t(c, b)
        dt_x = spread(dt, heads)
        v = dt_x * u
        v_low = v.astype(BF16)
        d_scores = jnp.zeros((CHUNK, CHUNK), F32)
        d_cum = jnp.zeros((CHUNK, LANES), F32)
        pieces = []
        for pair in range(heads // 2):
            lanes = slice(pair * LANES, (pair + 1) * LANES)
            dy_halves = jnp.concatenate(split_pair(dy_low[:, lanes]), axis=0)
            grads = dot_t(dy_halves, v_low[:, lanes])
            mats, weighed = [], []
            for k in range(2):
                decay = decay_matrix(cum, cum_t, visible, 2 * pair + k)
                grad = grads[k * CHUNK : (k + 1) * CHUNK, :]
                mat = scores * decay
                d_scores = d_scores + grad * decay
                weighed.append((grad * mat).astype(BF16))
                mats.append(mat.astype(BF16))
            pieces.append(tdot(jnp.concatenate(mats, axis=0), dy_halves))
            pick = (two_l == 2 * pair + two_r // CHUNK).astype(BF16)
            d_cum = d_cum + dot(jnp.concatenate(weighed, axis=1), pick)
            d_cum = d_cum - tdot(jnp.concatenate(weighed, axis=0), pick)
        old_low = st_ref[piece]
        last = cum[CHUNK - 1 : CHUNK, :]
        enter_x = spread(jnp.exp(cum) * keep, heads)
        end_x = spread(jnp.exp(last - cum) * tail, heads)
        carry = spread(jnp.exp(last) * keep[CHUNK - 1 : CHUNK, :], heads)
        ds = d_state[...]
        ds_low = ds.astype(BF16)
        dv_state = end_x * dot(b, ds_low)
        dv = jnp.concatenate(pieces, axis=1) + dv_state
        dy_enter = enter_x * dy
        dy_enter_low = dy_enter.astype(BF16)
        d_b = dot_t((end_x * v).astype(BF16), ds_low)
        d_c = dot_t(dy_enter_low, old_low)
        e = dot((dy_enter * dot(c, old_low)).astype(BF16), to_head)
        f = dot((dv_state * v).astype(BF16), to_head)
        flow = jnp.sum(ds * old_low.astype(F32) * carry, axis=0, keepdims=True)
        flow = dot(flow, to_head.astype(F32), HIGHEST)
        d_state[...] = carry * ds + tdot(c, dy_enter_low)
        d_scores_low = d_scores.astype(BF16)
        d_c = d_c + dot(d_scores_low, b)
        d_b = d_b + tdot(d_scores_low, c)
        d_la = dot(upper, d_cum + e, HIGHEST) + dot(below, f, HIGHEST) + flow
        d_dt = d_la * decay_rate + dot((dv * u).astype(BF16), to_head)
        d_pre = d_dt * sigmoid(pre)
        ddt_ref[at, :] = d_pre.astype(BF16)
        a128_ref[0:1, :] += jnp.sum(d_pre, axis=0, keepdims=True)
        a128_ref[1:2, :] += jnp.sum(d_la * la, axis=0, keepdims=True)
        du = dt_x * dv + dsk_ref[...] * dy
        ahead[at, :] = du * (sp * (1.0 + p * (1.0 - sp)))
        d_bcu = jnp.concatenate([d_b, d_c], axis=1)
        ahead_bc[at, :] = d_bcu * (spbc * (1.0 + pbc * (1.0 - spbc)))

    for hist, weight, raw, out, acc in (
        (ahead, cx_ref, xc_ref, dx_ref, a768_ref),
        (ahead_bc, cbc_ref, bc_ref, dbc_ref, a256_ref),
    ):
        value = raw[...].astype(F32)
        dp = hist[0:rows, :]
        acc[4:5, :] += jnp.sum(dp, axis=0, keepdims=True)
        acc[3:4, :] += jnp.sum(dp * value, axis=0, keepdims=True)
        total = dp * weight[3:4, :]
        for k in range(1, 4):
            later = hist[k : k + rows, :] * meta[:, 2 + k : 3 + k]
            total = total + later * weight[3 - k : 4 - k, :]
            acc[3 - k : 4 - k, :] += jnp.sum(later * value, axis=0, keepdims=True)
        out[...] = total.astype(BF16)
        hist[rows : rows + 8, :] = hist[0:8, :]
    partial = dot_t(dz_ref[...], wz_ref[...]) + dot_t(dx_ref[...], wx_ref[...])
    partial = partial + dot_t(ddt_ref[...], wdt_ref[...]) + dot_t(dbc_ref[...], wbc_ref[...])
    for piece in range(rows // CHUNK):
        low = partial[piece * CHUNK : (piece + 1) * CHUNK, :].astype(BF16)
        xp_ref[0, piece] = low
        part[block, piece] = low
    run_steps(line, block, when, first)

    @pl.when(block == len(when) - 1)
    def _():
        line.close(first + steps - 1, steps - 1, carry_out)


def rows_spec(block, cols, last=None):
    if last is None:
        return pl.BlockSpec((block, cols), lambda i: (i, 0))
    return pl.BlockSpec((block, cols), lambda i: (last - i, 0))


def whole_spec(array):
    return pl.BlockSpec(array.shape, lambda i: (0, 0), pipeline_mode=pl.Buffered(1))


def lane_pad(array):
    return jnp.pad(array, ((0, 0), (0, LANES - array.shape[1])))


def token_masks(seg):
    length = seg.shape[0]
    t = jnp.arange(length)
    columns = []
    for k in range(1, 4):
        columns.append((jnp.roll(seg, k) == seg) & (t >= k))
    for k in range(1, 4):
        columns.append((jnp.roll(seg, -k) == seg) & (t < length - k))
    chunked = seg.reshape(-1, CHUNK)
    ends = chunked[:, -1:]
    before = jnp.concatenate([jnp.full((1, 1), -1, seg.dtype), ends[:-1]], axis=0)
    columns.append(seg)
    columns.append((chunked == before).reshape(-1))
    columns.append((chunked == ends).reshape(-1))
    columns = [column.astype(F32) for column in columns]
    columns += [jnp.zeros((length,), F32)] * (16 - len(columns))
    return jnp.stack(columns, axis=1)


def on_device(
    x_in, segments, out_grad, norm_gain, w_z, w_x, w_bc, w_dt, conv_x, conv_bc, bias_x, bias_bc,
    dt_bias, a_log, d_skip, out_gain, w_out,
):
    tensor_count = lax.axis_size("tensor")
    x, g, seg = x_in[0], out_grad[0], segments[0]
    length, width = x.shape
    inner = w_x.shape[1]
    heads = w_dt.shape[1]
    bc_width = w_bc.shape[1]
    blocks = length // BLOCK
    chunks = length // CHUNK
    per_block = BLOCK // CHUNK
    meta = token_masks(seg)
    seg_row = seg.astype(F32)[None, :]
    wdt = lane_pad(w_dt)
    dtb = lane_pad(dt_bias[None, :])
    al = lane_pad(a_log[None, :])
    dsk = jnp.repeat(d_skip, inner // heads)[None, :]
    og = out_gain[None, :]
    shape = jax.ShapeDtypeStruct
    pairs = 2 * blocks
    all_steps = pairs + 2 * tensor_count - 3
    spread_fwd = [b if b < 4 else (4 + (b - 5) // 2 if b % 2 else -1) for b in range(blocks)]
    spread_bwd = [b // 2 if b % 2 == 0 else -1 for b in range(blocks)]
    n_fwd = max(spread_fwd) + 1
    n_bwd = max(spread_bwd) + 1
    anywhere = pl.BlockSpec(memory_space=pl.ANY)
    pair_shape = (blocks, 2, CHUNK, width)
    carry_spec = pl.BlockSpec((2, CHUNK, width), lambda i: (0, 0, 0))
    carry_shape = jax.ShapeDtypeStruct((2, CHUNK, width), BF16)
    res_shape = jax.ShapeDtypeStruct((pairs, 2, CHUNK, width), BF16)

    def params(ident):
        return pltpu.CompilerParams(
            vmem_limit_bytes=60 * 2**20, dimension_semantics=("arbitrary",), collective_id=ident, has_side_effects=True
        )

    weights = (w_z, w_x, w_bc, wdt, w_out, norm_gain[None, :], conv_x, bias_x[None, :], conv_bc, bias_bc[None, :], dtb, al, dsk, og)
    z, p, xc, ys, pbc, bc, dtr, dn, xn, st, yp, stat, carry, res = pl.pallas_call(
        functools.partial(forward_kernel, heads, tensor_count, pairs, blocks, n_fwd, spread_fwd),
        grid=(blocks,),
        in_specs=[
            rows_spec(BLOCK, width),
            rows_spec(BLOCK, width),
            pl.BlockSpec((1, BLOCK), lambda i: (0, i)),
            rows_spec(BLOCK, meta.shape[1]),
            *[whole_spec(w) for w in weights],
        ],
        out_specs=[
            rows_spec(BLOCK, inner),
            rows_spec(BLOCK, inner),
            rows_spec(BLOCK, inner),
            rows_spec(BLOCK, inner),
            rows_spec(BLOCK, bc_width),
            rows_spec(BLOCK, bc_width),
            rows_spec(BLOCK, LANES),
            rows_spec(BLOCK, inner),
            rows_spec(BLOCK, width),
            pl.BlockSpec((per_block, bc_width // 2, inner), lambda i: (i, 0, 0)),
            pl.BlockSpec((1, 2, CHUNK, width), lambda i: (i, 0, 0, 0)),
            rows_spec(BLOCK, 8),
            carry_spec,
            anywhere,
        ],
        out_shape=[
            shape((length, inner), F32),
            shape((length, inner), F32),
            shape((length, inner), BF16),
            shape((length, inner), F32),
            shape((length, bc_width), F32),
            shape((length, bc_width), F32),
            shape((length, LANES), F32),
            shape((length, inner), F32),
            shape((length, width), BF16),
            shape((chunks, bc_width // 2, inner), BF16),
            shape(pair_shape, BF16),
            shape((length, 8), F32),
            carry_shape,
            res_shape,
        ],
        scratch_shapes=[
            pltpu.VMEM((BLOCK + 8, inner), F32),
            pltpu.VMEM((BLOCK + 8, bc_width), F32),
            pltpu.VMEM((bc_width // 2, inner), F32),
            pltpu.VMEM(pair_shape, BF16),
            *line_scratch(n_fwd, CHUNK, width),
        ],
        compiler_params=params(0),
        name="forward_scan",
    )(x, g, seg_row, meta, *weights)

    sums = lax.psum(stat[:, :2].T, "tensor")
    total = inner * tensor_count
    r2 = lax.rsqrt(sums[0] / total + EPS)
    k2 = r2 * r2 * r2 * (sums[1] / total)
    scal = jnp.stack([r2, k2] + [jnp.zeros_like(r2)] * 6, axis=1)

    last = blocks - 1
    weights = (w_z, w_x, w_bc, wdt, conv_x, conv_bc, dtb, al, dsk, og)
    dz, dx, ddt, dbc, xp, normed, a768, a256, a128, carry, res = pl.pallas_call(
        functools.partial(backward_kernel, heads, tensor_count, pairs, blocks, n_fwd, n_bwd, spread_bwd),
        grid=(blocks,),
        in_specs=[
            rows_spec(BLOCK, inner, last),
            rows_spec(BLOCK, inner, last),
            rows_spec(BLOCK, inner, last),
            rows_spec(BLOCK, inner, last),
            rows_spec(BLOCK, bc_width, last),
            rows_spec(BLOCK, bc_width, last),
            rows_spec(BLOCK, LANES, last),
            rows_spec(BLOCK, inner, last),
            pl.BlockSpec((per_block, bc_width // 2, inner), lambda i: (last - i, 0, 0)),
            pl.BlockSpec((1, BLOCK), lambda i: (0, last - i)),
            rows_spec(BLOCK, meta.shape[1], last),
            rows_spec(BLOCK, 8, last),
            *[whole_spec(w) for w in weights],
            anywhere,
            carry_spec,
            anywhere,
        ],
        out_specs=[
            rows_spec(BLOCK, inner, last),
            rows_spec(BLOCK, inner, last),
            rows_spec(BLOCK, LANES, last),
            rows_spec(BLOCK, bc_width, last),
            pl.BlockSpec((1, 2, CHUNK, width), lambda i: (last - i, 0, 0, 0)),
            rows_spec(BLOCK, inner, last),
            pl.BlockSpec((8, inner), lambda i: (0, 0)),
            pl.BlockSpec((8, bc_width), lambda i: (0, 0)),
            pl.BlockSpec((8, LANES), lambda i: (0, 0)),
            carry_spec,
            anywhere,
        ],
        out_shape=[
            shape((length, inner), BF16),
            shape((length, inner), BF16),
            shape((length, LANES), BF16),
            shape((length, bc_width), BF16),
            shape(pair_shape, BF16),
            shape((length, inner), BF16),
            shape((8, inner), F32),
            shape((8, bc_width), F32),
            shape((8, LANES), F32),
            carry_shape,
            res_shape,
        ],
        scratch_shapes=[
            pltpu.VMEM((BLOCK + 8, inner), F32),
            pltpu.VMEM((BLOCK + 8, bc_width), F32),
            pltpu.VMEM((bc_width // 2, inner), F32),
            pltpu.VMEM(pair_shape, BF16),
            *line_scratch(n_bwd, CHUNK, width),
        ],
        input_output_aliases={12 + len(weights) + 2: 10},
        compiler_params=params(1),
        name="backward_scan",
    )(z, p, xc, ys, pbc, bc, dtr, dn, st, seg_row, meta, scal, *weights, yp, carry, res)

    grad_wout = tdot(normed, g)
    grad_wz = tdot(xn, dz)
    grad_wx = tdot(xn, dx)
    grad_wdt = tdot(xn, ddt)[:, :heads]
    grad_wbc = tdot(xn, dbc)
    low = (grad_wz.astype(BF16), grad_wx.astype(BF16), grad_wout.astype(BF16))
    low, xp = lax.optimization_barrier((low, xp))
    rest = all_steps - n_fwd - n_bwd
    res = pl.pallas_call(
        functools.partial(line_kernel, tensor_count, pairs, blocks, n_fwd + n_bwd, rest),
        grid=(rest,),
        in_specs=[anywhere, anywhere, carry_spec, anywhere],
        out_specs=anywhere,
        out_shape=res_shape,
        scratch_shapes=line_scratch(rest, CHUNK, width),
        input_output_aliases={3: 0},
        compiler_params=params(2),
        cost_estimate=pl.CostEstimate(flops=10**11, bytes_accessed=3 * 10**8, transcendentals=0),
        name="line_sums",
    )(yp, xp, carry, res)
    y_sum = res[:blocks].reshape(length, width)
    x_sum = res[blocks:].reshape(length, width)
    result = (x.astype(F32) + r2[:, None] * y_sum.astype(F32)).astype(BF16)
    grad_wz, grad_wx, grad_wout = (v.astype(F32) for v in lax.psum(low, "dp"))
    grad_wbc = lax.psum(grad_wbc, ("dp", "tensor"))

    tokens = x.astype(F32)
    r1 = lax.rsqrt(jnp.mean(tokens * tokens, -1, keepdims=True) + EPS)
    dxn = x_sum.astype(F32)
    dot_x = jnp.sum(dxn * norm_gain * tokens, -1, keepdims=True)
    grad_x = (g.astype(F32) + r1 * norm_gain * dxn - tokens * (r1 * r1 * r1 * dot_x / width)).astype(BF16)
    grad_gain = jnp.sum(dxn * tokens * r1, 0)

    grad_dskip = jnp.sum(a768[5].reshape(heads, -1), axis=1)
    own = lax.psum((grad_gain, a768, a128, grad_wdt), "dp")
    shared = lax.psum(a256, ("dp", "tensor"))
    grad_gain, a768_all, a128_all, grad_wdt = own
    grad_dskip = jnp.sum(a768_all[5].reshape(heads, -1), axis=1)
    return (
        result[None],
        grad_x[None],
        grad_gain,
        grad_wz,
        grad_wx,
        grad_wbc,
        grad_wdt,
        a768_all[:4],
        shared[:4],
        a768_all[4],
        shared[4],
        a128_all[0, :heads],
        a128_all[1, :heads],
        grad_dskip,
        a768_all[6],
        grad_wout,
    )


def solution(mesh):
    tensor_last = P(None, "tensor")
    in_specs = (
        P("dp", None, None), P("dp", None), P("dp", None, None), P(), tensor_last, tensor_last, P(), tensor_last,
        tensor_last, P(), P("tensor"), P(), P("tensor"), P("tensor"), P("tensor"), P("tensor"), P("tensor", None),
    )
    out_specs = (
        P("dp", None, None), P("dp", None, None), P(), tensor_last, tensor_last, P(), tensor_last, tensor_last, P(),
        P("tensor"), P(), P("tensor"), P("tensor"), P("tensor"), P("tensor"), P("tensor", None),
    )
    return jax.shard_map(on_device, mesh=mesh, in_specs=in_specs, out_specs=out_specs, check_vma=False)
```

time: 2400 us -> 612 us (0.26)
  waiting for transfers between devices: 963 us -> 24 us
  local copies, waits for them, and re-layouts: 660 us -> 30.2 us
  matrix products: 390 us -> 35.9 us
  Pallas kernels: 0 us -> 349 us
  other arithmetic: 278 us -> 46 us
  blocking collectives: 49.6 us -> 104 us
  loops' own time: 25.3 us -> 0 us
    psum x3, waiting for transfers between devices: 963 us -> 23.9 us  [the longest x1 23.9 us: on_device(): grad_wbc = lax.psum(grad_wbc, ('dp', 'tensor'))]
    dynamic_update_slice x72 -> x0, local copies, waits for them, and re-layouts: 357 us -> none  [state_scan(): lax.scan(jax.checkpoint(group_step), start, (to_blocks(head_x), to_blocks...]
    pallas_call x0 -> x3, Pallas kernels: none -> 349 us  [the longest x1 164 us: on_device(): pl.pallas_call(functools.partial(line_kernel, tensor_count, pairs, blocks...]
    dot_general x111 -> x5, matrix products: 362 us -> 35.9 us  [tdot(): lax.dot_general(a, b, (((0,), (0,)), ((), ())), preferred_element_type=F32)]
    another operation x89 -> x1, other arithmetic: 75.2 us -> 0.04 us  [on_device(): scal = jnp.stack([r2, k2] + [jnp.zeros_like(r2)] * 6, axis=1)]
    reduce_sum x31 -> x3, other arithmetic: 77.4 us -> 11.3 us  [the longest x1 6.54 us: on_device(): grad_gain = jnp.sum(dxn * tokens * r1, 0)]
    another operation x135 -> x8, local copies, waits for them, and re-layouts: 66.1 us -> 3.54 us  [the longest x3 1.49 us: token_masks(): return jnp.stack(columns, axis=1)]
    squeeze x32 -> x1, local copies, waits for them, and re-layouts: 55.4 us -> 0.52 us  [on_device(): a128_all[1, :heads]]
  transfers between devices with their start and end apart: 3 -> 3, of which waited for: 3 -> 1; matrix products, arithmetic and copies ran while one was open for 6% -> 9% of each run, Pallas kernels for 0% -> 27%
where the time goes in v1:
time: 612 us; the launch traced here: 603 us
  Pallas kernels  349 us (57%)
  blocking collectives  104 us (17%)
  other arithmetic  46 us (8%)
  matrix products  35.9 us (6%)
  local copies, waits for them, and re-layouts  30.2 us (5%)
  waiting for transfers between devices  24 us (4%)
  between operations  14.4 us (2%)
    pallas_call x1, Pallas kernels, on_device(): pl.pallas_call(functools.partial(line_kernel, tensor_count, pairs, blocks...  164 us
    pallas_call x1, Pallas kernels, on_device(): pl.pallas_call(functools.partial(forward_kernel, heads, tensor_count, pai...  93.9 us
    pallas_call x1, Pallas kernels, on_device(): pl.pallas_call(functools.partial(backward_kernel, heads, tensor_count, pa...  90.6 us
    psum x1, blocking collectives, on_device(): sums = lax.psum(stat[:, :2].T, 'tensor')  41.7 us
    psum x1, blocking collectives, on_device(): shared = lax.psum(a256, ('dp', 'tensor'))  38.1 us
    dot_general x5, matrix products, tdot(): lax.dot_general(a, b, (((0,), (0,)), ((), ())), preferred_element_type=F32)  35.9 us
    psum x1, blocking collectives, on_device(): own = lax.psum((grad_gain, a768, a128, grad_wdt), 'dp')  24 us
    psum x1, waiting for transfers between devices, on_device(): grad_wbc = lax.psum(grad_wbc, ('dp', 'tensor'))  23.9 us
  transfers between devices with their start and end apart: 3, of which 1 were waited for; matrix products, arithmetic and copies ran while one was open for 9% of the time, Pallas kernels for 27%

profile of v1, /device:TPU:0, one launch (start us, length us, event | category | flops | bytes accessed | tf_op | source)
XLA Modules:
  0.0 603.2 jit_solution(14933167855352182443)
XLA Ops:
  7.2 1.4 bitcast_convert_fusion
  8.6 0.8 slice_bitcast_fusion.2
  9.5 0.8 slice_bitcast_fusion.10
  10.2 0.8 slice_bitcast_fusion.1
  11.1 0.8 slice_bitcast_fusion.9
  11.8 1.3 fusion.12
  13.1 0.8 slice_bitcast_fusion.3
  13.9 0.8 slice.139
  14.7 0.8 slice.138
  15.8 2.1 compare_convert_fusion
  18.2 1.3 copy.79.meta_ref
  19.5 1.0 copy.78
  20.5 1.3 broadcast_in_dim.14.ng_ref
  21.8 1.3 broadcast_in_dim.30.bx_ref
  23.1 1.2 pad.12.dtb_ref
  24.3 1.2 pad.13.al_ref
  25.5 0.7 broadcast_in_dim.34
  26.2 0.7 broadcast_in_dim_reshape.3.dsk_ref
  26.8 1.3 broadcast_in_dim.35.og_ref
  28.1 0.8 pad.11.wdt_ref
  28.9 93.9 %forward_scan.1 = (f32[2048,768]{1,0:T(8,128)}, f32[2048,768]{1,0:T(8,128)}, bf16[2048,768]{1,0:T(8,128)(2,1)}, f32[2048,768]{1,0:T(8,128)}, f32[2048,256]{1,0:T...) custom-call(bf16[2048,1536]{1,0:T(8,128)(2,1)} %bitcast.70, ...), custom_call_target="tpu_custom_call" | custom-call | tf_op jit(solution)/shard_map/forward_scan/pallas_call | solution.py:602
  122.8 1.3 slice_bitcast_fusion
  124.1 41.7 %psum.70 = f32[2,2048]{0,1:T(8,128)S(1)} all-reduce(f32[2,2048]{0,1:T(8,128)S(1)} %slice_bitcast_fusion), channel_id=1, replica_groups=mesh['dp'=8,'tensor'=4] {'tensor'}, use_global_device_ids=true, to_apply=%region_0.1 | all-reduce | flops 4096 | bytes 32768 | tf_op jit(solution)/shard_map/psum | solution.py:655
  165.8 0.9 fusion.5
  166.8 1.3 copy.81.scal_ref
  168.1 90.6 %backward_scan.1 = (bf16[2048,768]{1,0:T(8,128)(2,1)}, bf16[2048,768]{1,0:T(8,128)(2,1)}, bf16[2048,128]{1,0:T(8,128)(2,1)}, bf16[2048,256]{1,0:T(8,128)(2,1)}, ...) custom-call(f32[2048,768]{1,0:T(8,128)} %get-tuple-element.48.z_ref,, ...), custom_call_target="tpu_custom_call", output_to_operand_aliasing={{10}: (24, {})} | custom-call | tf_op jit(solution)/shard_map/backward_scan/pallas_call | solution.py:663
  258.8 9.6 %convolution_convert_fusion.2 = bf16[1536,768]{1,0:T(8,128)(2,1)} fusion(bf16[2048,1536]{1,0:T(8,128)(2,1)} %get-tuple-element.47, bf16[2048,768]{1,0:T(8,128)(2,1)} %get-tuple-element.59), kind=kOutput, calls=%fused_computation.10 | convolution fusion | flops 4833017856 | bytes 11796480 | tf_op jit(solution)/shard_map/dot_general | solution.py:28
  268.3 9.4 %convolution_convert_fusion.1 = bf16[1536,768]{1,0:T(8,128)(2,1)} fusion(bf16[2048,1536]{1,0:T(8,128)(2,1)} %get-tuple-element.47, bf16[2048,768]{1,0:T(8,128)(2,1)S(1)} %copy-done.11), kind=kOutput, calls=%fused_computation.9 | convolution fusion | flops 4833017856 | bytes 11796480 | tf_op jit(solution)/shard_map/dot_general | solution.py:28
  277.7 6.5 %convolution_convert_fusion = bf16[768,1536]{1,0:T(8,128)(2,1)} fusion(bf16[2048,768]{1,0:T(8,128)(2,1)S(1)} %copy-done.10, bf16[1,2048,1536]{2,1,0:T(8,128)(2,1)S(1)} %bitcast.75), kind=kOutput, calls=%fused_computation.8 | convolution fusion | flops 4833017856 | bytes 11796480 | tf_op jit(solution)/shard_map/dot_general | solution.py:28
  284.3 1.0 copy-done.3
  285.2 4.4 fusion.6
  289.7 6.1 %fusion.13 = f32[1536,256]{1,0:T(8,128)} fusion(bf16[2048,1536]{1,0:T(8,128)(2,1)} %get-tuple-element.47, bf16[2048,256]{1,0:T(8,128)(2,1)S(1)} %copy-done.12), kind=kOutput, calls=%fused_computation.54 | convolution fusion | flops 1610612736 | bytes 8912896 | tf_op jit(solution)/shard_map/dot_general | solution.py:28
  295.8 4.2 multiply_reduce_fusion.2
  300.0 164.3 %line_sums.1 = bf16[16,2,128,1536]{3,2,1,0:T(8,128)(2,1)} custom-call(bf16[8,2,128,1536]{3,2,1,0:T(8,128)(2,1)} %get-tuple-element.46.y_ref, bf16[8,2,128,1536]{3,2,1,0:T(8,128)(2,1)} %get-tuple-element.63.x_ref, bf16[2,128,1536]{2,1,0:T(8,128)(2,1)} %get-tuple-element.64.carry_ref, ...), custom_call_target="tpu_custom_call", output_to_operand_aliasing={{}: (3, {})} | custom-call | flops 99999997952 | bytes 300000000 | tf_op jit(solution)/shard_map/line_sums/pallas_call | solution.py:730
  464.3 7.3 %slice_convert_fusion = (f32[8,2,128,1536]{3,2,1,0:T(8,128)S(1)}, bf16[8,2,128,1536]{3,2,1,0:T(8,128)(2,1)S(1)}) fusion(bf16[16,2,128,1536]{3,2,1,0:T(8,128)(2,1)} %line_sums.1), kind=kLoop, calls=%fused_computation.7 | loop fusion | flops 3145728 | bytes 31457280 | tf_op jit(solution)/shard_map/convert_element_type | solution.py:750
  471.7 1.3 copy-done
  473.0 6.5 %multiply_reduce_fusion = (f32[1536]{0:T(1024)S(1)}, f32[8,2,128]{2,1,0:T(2,128)S(1)}) fusion(f32[8,2,128]{2,1,0:T(2,128)S(1)} %bitcast.81, bf16[16,2,128,1536]{3,2,1,0:T(8,128)(2,1)S(1)} %copy-done, f32[1536]{0:T(1024)S(1)} %copy-done.6, bf16[8,2,128,1536]{3,2,1,0:T(8,128)(2,1)} %bitcast.71), kind=kLoop, calls=%fused_computation.3 | loop fusion | flops 25162240 | bytes 12611584 | tf_op jit(solution)/shard_map/reduce_sum | solution.py:753
  479.6 13.0 %subtract_convert_fusion = (bf16[1,2048,1536]{2,1,0:T(8,128)(2,1)}, bf16[1,2048,1536]{2,1,0:T(8,128)(2,1)}) fusion(f32[1,2048,1536]{2,1,0:T(8,128)S(1)} %bitcast.72, bf16[1,2048,1536]{2,1,0:T(8,128)(2,1)} %param.19, f32[2048]{0:T(1024)S(1)} %fusion.10, f32[1536]{0:T(1024)S(1)} %copy-done.6, f32[2048]{0:T(1024)S(1)} %add_rsqrt_fusion, ...), kind=kLoop, calls=%fused_computation.4 | loop fusion | flops 37748736 | bytes 44070912 | tf_op jit(solution)/shard_map/convert_element_type | solution.py:752
  492.6 38.1 %psum.77 = f32[8,256]{1,0:T(8,128)S(1)} all-reduce(f32[8,256]{1,0:T(8,128)S(1)} %copy-done.8), channel_id=1, replica_groups=mesh['dp'=8,'tensor'=4] {'dp','tensor'}, use_global_device_ids=true, to_apply=%region_10.11 | all-reduce | flops 2048 | bytes 16384 | tf_op jit(solution)/shard_map/psum | solution.py:757
  531.9 24.0 %all-reduce.3 = (f32[1536]{0:T(1024)}, f32[8,768]{1,0:T(8,128)S(1)}, f32[8,128]{1,0:T(8,128)S(1)}) all-reduce(f32[1536]{0:T(1024)S(1)} %get-tuple-element.74, f32[8,768]{1,0:T(8,128)S(1)} %copy-done.7, f32[8,128]{1,0:T(8,128)S(1)} %copy-done.9), channel_id=1, replica_groups=mesh['dp'=8,'tensor'=4] {'dp'}, use_global_device_ids=true, to_apply=%region_4.5 | all-reduce | flops 8704 | bytes 69632 | tf_op jit(solution)/shard_map/psum | solution.py:756
  556.5 0.6 slice_reduce_fusion
  557.2 0.6 reduce_sum.42
  558.4 4.4 convert_element_type.199
  562.8 2.5 convert_element_type.200
  565.3 2.8 convert_element_type.201
  568.1 23.9 %all-reduce.9.cloned.1.call-done = f32[1536,256]{1,0:T(8,128)} async-done(((f32[1536,256]{1,0:T(8,128)}), f32[1536,256]{1,0:T(8,128)}) %all-reduce.9.cloned.1.call-update) | async-done | bytes 1572880 | tf_op jit(solution)/shard_map/psum | solution.py:746
  592.1 2.7 copy.91
  594.7 1.5 copy.92
  (55 shorter events, 3.2 us)
Async XLA Ops:
  7.2 551.2 %all-reduce.13.cloned.1.call-start = ((), (), s32[]{:S(2)}) async-start(), calls=%async_computation.2 | async-start | bytes 14155776 | tf_op jit(solution)/shard_map/psum | solution.py:745
  166.7 92.0 %copy-start.4 = (f32[2048]{0:T(1024)}, f32[2048]{0:T(1024)S(1)}, u32[]{:S(2)}) copy-start(f32[2048]{0:T(1024)S(1)} %get-tuple-element.76) | copy-start | bytes 24580
  258.7 9.6 %copy-start.11 = (bf16[2048,768]{1,0:T(8,128)(2,1)S(1)}, bf16[2048,768]{1,0:T(8,128)(2,1)}, u32[]{:S(2)}) copy-start(bf16[2048,768]{1,0:T(8,128)(2,1)} %get-tuple-element.60) | copy-start | bytes 9437188
  258.8 19.0 %slice-start = ((s8[6291456]{0:T(1024)(128)(4,1)}), s8[4194304]{0:T(1024)(128)(4,1)S(1)}, s32[]{:S(2)}) async-start(s8[6291456]{0:T(1024)(128)(4,1)} %bitcast.74), calls=%async_computation.3 | async-start | bytes 8388608
  268.3 9.4 %slice-start.1 = ((s8[6291456]{0:T(1024)(128)(4,1)}), s8[2097152]{0:T(1024)(128)(4,1)S(1)}, s32[]{:S(2)}) async-start(s8[6291456]{0:T(1024)(128)(4,1)} %bitcast.74), calls=%async_computation.4 | async-start | bytes 4194304
  268.3 9.4 %copy-start.10 = (bf16[2048,768]{1,0:T(8,128)(2,1)S(1)}, bf16[2048,768]{1,0:T(8,128)(2,1)}, u32[]{:S(2)}) copy-start(bf16[2048,768]{1,0:T(8,128)(2,1)} %get-tuple-element.61) | copy-start | bytes 9437188
  284.2 1.0 copy-start.3
  284.2 5.5 copy-start.12
  284.2 283.9 %all-reduce.11.cloned.1.call-start = ((), (), s32[]{:S(2)}) async-start(), calls=%async_computation.1 | async-start | bytes 196608 | tf_op jit(solution)/shard_map/psum | solution.py:756
  289.7 302.4 %all-reduce.9.cloned.1.call-start = ((), (), s32[]{:S(2)}) async-start(), calls=%async_computation | async-start | bytes 3145728 | tf_op jit(solution)/shard_map/psum | solution.py:746
  464.3 8.7 %copy-start = (bf16[16,2,128,1536]{3,2,1,0:T(8,128)(2,1)S(1)}, bf16[16,2,128,1536]{3,2,1,0:T(8,128)(2,1)}, u32[]{:S(2)}) copy-start(bf16[16,2,128,1536]{3,2,1,0:T(8,128)(2,1)} %line_sums.1) | copy-start | bytes 37748740
  464.3 8.7 %copy-start.6 = (f32[1536]{0:T(1024)S(1)}, f32[1536]{0:T(1024)}, u32[]{:S(2)}) copy-start(f32[1536]{0:T(1024)} %param.20) | copy-start | bytes 18436
  473.0 6.6 %copy-start.5 = (f32[2048]{0:T(1024)S(1)}, f32[2048]{0:T(1024)}, u32[]{:S(2)}) copy-start(f32[2048]{0:T(1024)} %copy-done.4) | copy-start | bytes 24580
  479.6 13.1 %copy-start.8 = (f32[8,256]{1,0:T(8,128)S(1)}, f32[8,256]{1,0:T(8,128)}, u32[]{:S(2)}) copy-start(f32[8,256]{1,0:T(8,128)} %get-tuple-element.71) | copy-start | bytes 24580
  479.6 52.3 %copy-start.7 = (f32[8,768]{1,0:T(8,128)S(1)}, f32[8,768]{1,0:T(8,128)}, u32[]{:S(2)}) copy-start(f32[8,768]{1,0:T(8,128)} %get-tuple-element.70) | copy-start | bytes 73732
  479.6 52.3 %copy-start.9 = (f32[8,128]{1,0:T(8,128)S(1)}, f32[8,128]{1,0:T(8,128)}, u32[]{:S(2)}) copy-start(f32[8,128]{1,0:T(8,128)} %get-tuple-element.72) | copy-start | bytes 12292
  558.4 4.4 copy-start.2
  558.4 6.9 %copy-start.1 = (bf16[768,1536]{1,0:T(8,128)(2,1)S(1)}, bf16[768,1536]{1,0:T(8,128)(2,1)}, u32[]{:S(2)}) copy-start(bf16[768,1536]{1,0:T(8,128)(2,1)} %get-tuple-element.86) | copy-start | bytes 7077892
Sparse Core Ops, SparseCore 0:
  284.3 112.8 all-reduce.12
  400.9 51.5 all-reduce.10
  459.2 132.8 all-reduce.8

commit v2 on v1

v2 whole, which is shorter than its diff:
```python
import functools

import jax
import jax.numpy as jnp
from jax import lax
from jax.experimental import pallas as pl
from jax.experimental.pallas import tpu as pltpu
from jax.sharding import PartitionSpec as P

EPS = 1e-05
CHUNK = 128
BLOCK = 256
PIECES = BLOCK // CHUNK
LANES = 128
F32 = jnp.float32
BF16 = jnp.bfloat16
HIGHEST = lax.Precision.HIGHEST
MESH = pl.DeviceIdType.MESH


def dot(a, b, precision=None):
    return lax.dot_general(a, b, (((1,), (0,)), ((), ())), precision=precision, preferred_element_type=F32)


def dot_t(a, b):
    return lax.dot_general(a, b, (((1,), (1,)), ((), ())), preferred_element_type=F32)


def tdot(a, b):
    return lax.dot_general(a, b, (((0,), (0,)), ((), ())), preferred_element_type=F32)


def sigmoid(v):
    return 1.0 / (1.0 + jnp.exp(-v))


def softplus(v):
    e = jnp.exp(-jnp.abs(v))
    series = e * (1.0 - e * (0.5 - e * (1.0 / 3.0 - e * 0.25)))
    return jnp.maximum(v, 0.0) + jnp.where(e < 0.03, series, jnp.log(1.0 + e))


def iotas(rows, cols):
    return (
        lax.broadcasted_iota(jnp.int32, (rows, cols), 0),
        lax.broadcasted_iota(jnp.int32, (rows, cols), 1),
    )


def spread(columns, heads):
    rows = columns.shape[0]
    low = lax.broadcasted_iota(jnp.int32, (rows, LANES), 1) < LANES // 2
    pieces = []
    for pair in range(heads // 2):
        first = columns[:, 2 * pair : 2 * pair + 1]
        second = columns[:, 2 * pair + 1 : 2 * pair + 2]
        pieces.append(jnp.where(low, first, second))
    return jnp.concatenate(pieces, axis=1)


def decays(la, seg_col, seg_row):
    r, c = iotas(CHUNK, CHUNK)
    cum = dot((r >= c).astype(F32), la, HIGHEST)
    visible = (r >= c) & (seg_col == seg_row)
    return cum, cum.T, visible


def decay_matrix(cum, cum_t, visible, head):
    gap = cum[:, head : head + 1] - cum_t[head : head + 1, :]
    return jnp.exp(jnp.where(visible, gap, -1e30))


def split_pair(values):
    low = lax.broadcasted_iota(jnp.int32, values.shape, 1) < LANES // 2
    zero = jnp.zeros_like(values)
    return jnp.where(low, values, zero), jnp.where(low, zero, values)


def conv_taps(hist, weight, same, rows):
    out = hist[8 : 8 + rows, :] * weight[3:4, :]
    for k in range(1, 4):
        out = out + hist[8 - k : 8 - k + rows, :] * same[k - 1] * weight[3 - k : 4 - k, :]
    return out


def columns_of(segr_ref):
    rows = segr_ref.shape[1]
    pieces = []
    for at in range(0, rows, LANES):
        row = segr_ref[:, at : at + LANES].astype(F32)
        pieces.append(jnp.broadcast_to(row, (LANES, LANES)).T[:, 0:1])
    return jnp.concatenate(pieces, axis=0)


def fill_heads(hv, wdt_s, dtb_ref, al_ref, dsk_ref, wdt_ref):
    heads = wdt_ref.shape[0]
    hv[...] = jnp.zeros_like(hv)
    for j, ref in enumerate((dtb_ref, al_ref, dsk_ref)):
        hv[j : j + 1, 0:heads] = ref[...]
    wdt_s[...] = jnp.zeros_like(wdt_s)
    wdt_s[0:heads, :] = wdt_ref[...]


def row_of(ref):
    return ref[...].reshape(1, ref.shape[0])


def inverse_rms(tokens):
    return lax.rsqrt(jnp.sum(tokens * tokens, axis=1, keepdims=True) * (1.0 / tokens.shape[1]) + EPS)


def bring(src, dst, sem):
    copy = pltpu.make_async_copy(src, dst, sem)
    copy.start()
    copy.wait()


def greet(peers, dp_peers=()):
    barrier = pltpu.get_barrier_semaphore()
    total = jnp.int32(len(dp_peers))
    for peer in dp_peers:
        pl.semaphore_signal(barrier, inc=1, device_id={"dp": peer}, device_id_type=MESH)
    for peer, there in peers:

        @pl.when(there)
        def _():
            pl.semaphore_signal(barrier, inc=1, device_id={"tensor": peer}, device_id_type=MESH)

        total = total + there.astype(jnp.int32)
    pl.semaphore_wait(barrier, total)


def neighbours(count):
    me = lax.axis_index("tensor")
    return [(me - 1, me > 0), (me + 1, me < count - 1)]


class Line:
    def __init__(self, count, pairs, first, steps, refs, source, finals=None):
        self.count, self.pairs, self.first, self.steps = count, pairs, first, steps
        self.source, self.finals = source, finals
        (self.res_y, self.res_x, self.land, self.send) = refs[:4]
        (self.red_out, self.red_in, self.bc_out, self.bc_in, self.local) = refs[4:]

    def to_result(self, k, q, act):
        half = self.pairs // 2

        @pl.when(k < half)
        def _():
            act(self.res_y.at[k, q])

        @pl.when(k >= half)
        def _():
            act(self.res_x.at[2 * half - 1 - k, q])

    def flow(self, q):
        me = lax.axis_index("tensor")
        if q % 2 == 0:
            return me, me - 1, me + 1
        return self.count - 1 - me, me + 1, me - 1

    def is_pair(self, i):
        return (i >= 0) & (i < self.pairs)

    def red(self, q, ls, toward, src):
        return pltpu.make_async_remote_copy(
            src_ref=src, dst_ref=self.land.at[ls + 1, q], send_sem=self.red_out.at[q, ls],
            recv_sem=self.red_in.at[q, ls], device_id={"tensor": toward}, device_id_type=MESH,
        )

    def cast(self, q, ls, away, src, there):
        return pltpu.make_async_remote_copy(
            src_ref=src, dst_ref=there, send_sem=self.bc_out.at[q, ls],
            recv_sem=self.bc_in.at[q, ls], device_id={"tensor": away}, device_id_type=MESH,
        )

    def keep(self, q, there):
        return pltpu.make_async_copy(self.send.at[q], there, self.local.at[q])

    def finish_red(self, q, s, ls):
        z, toward, away = self.flow(q)
        n = self.count
        i = s - (n - 1) + z

        @pl.when(self.is_pair(i) & (z > 0))
        def _():
            self.red(q, ls, toward, self.send.at[q]).wait_send()

        @pl.when(self.is_pair(i) & (z == 0))
        def _():
            self.cast(q, ls, away, self.send.at[q], self.res_y.at[0, q]).wait_send()
            self.keep(q, self.res_y.at[0, q]).wait()

        @pl.when(self.is_pair(i + 1) & (z < n - 1))
        def _():
            self.red(q, ls, toward, self.send.at[q]).wait_recv()

    def finish_cast(self, q, s, ls):
        z, _, away = self.flow(q)
        n = self.count
        k = s - (n - 1) - z

        @pl.when(self.is_pair(k) & (z > 0) & (z < n - 1))
        def _():
            self.cast(q, ls, away, self.res_y.at[0, q], self.res_y.at[0, q]).wait_send()

        @pl.when(self.is_pair(k + 1) & (z > 0))
        def _():
            self.cast(q, ls, away, self.res_y.at[0, q], self.res_y.at[0, q]).wait_recv()

    def step(self, ls, h):
        n = self.count
        s = self.first + ls
        for q in (2 * h, 2 * h + 1):
            z, toward, away = self.flow(q)
            i = s - (n - 1) + z

            @pl.when(ls > 0)
            def _():
                self.finish_red(q, s - 1, ls - 1)

            @pl.when(self.is_pair(i))
            def _():
                mine = self.source(q, i)

                @pl.when(z == n - 1)
                def _():
                    self.red(q, ls, toward, mine).start()

                @pl.when((z > 0) & (z < n - 1))
                def _():
                    self.send[q] = (mine[...].astype(F32) + self.land[ls, q].astype(F32)).astype(BF16)
                    self.red(q, ls, toward, self.send.at[q]).start()

                @pl.when(z == 0)
                def _():
                    total = mine[...].astype(F32) + self.land[ls, q].astype(F32)
                    if self.finals is None:
                        self.send[q] = total.astype(BF16)
                    else:
                        self.finals.last(q, i, total, self.send)

                    def give(there):
                        self.cast(q, ls, away, self.send.at[q], there).start()
                        self.keep(q, there).start()

                    self.to_result(i, q, give)
                    if self.finals is not None:

                        @pl.when(ls + 1 < self.steps)
                        def _():
                            self.finals.fetch(q, i + 1)

        for q in (2 * h, 2 * h + 1):

            @pl.when(ls > 0)
            def _():
                self.finish_cast(q, s - 1, ls - 1)

            z, toward, away = self.flow(q)
            k = s - (n - 1) - z

            @pl.when(self.is_pair(k) & (z > 0) & (z < n - 1))
            def _():
                self.to_result(k, q, lambda there: self.cast(q, ls, away, there, there).start())

    def held(self, q, s):
        z, _, _ = self.flow(q)
        return self.is_pair(s - (self.count - 1) + z) & (z < self.count - 1)

    def open(self, carry):
        for q in range(4):

            @pl.when(self.held(q, self.first))
            def _():
                bring(carry.at[q], self.land.at[0, q], self.local.at[q])

            z, _, _ = self.flow(q)

            @pl.when(z == 0)
            def _():
                self.finals.fetch(q, jnp.int32(self.first - (self.count - 1)))

    def close(self, carry):
        ls = self.steps - 1
        s = self.first + ls
        for q in range(4):
            self.finish_red(q, s, ls)
            self.finish_cast(q, s, ls)
            if carry is None:
                continue

            @pl.when(self.held(q, s + 1))
            def _():
                bring(self.land.at[ls + 1, q], carry.at[q], self.local.at[q])


def line_scratch(steps, width):
    return [
        pltpu.VMEM((steps + 1, 4, BLOCK // 4, width), BF16),
        pltpu.VMEM((4, BLOCK // 4, width), BF16),
        pltpu.SemaphoreType.DMA((4, steps)),
        pltpu.SemaphoreType.DMA((4, steps)),
        pltpu.SemaphoreType.DMA((4, steps)),
        pltpu.SemaphoreType.DMA((4, steps)),
        pltpu.SemaphoreType.DMA((4,)),
    ]


class Finals:
    def __init__(self, pairs, x_any, g_any, gain, rows, sems):
        self.pairs, self.half, self.x_any, self.g_any, self.gain, self.rows, self.sems = (
            pairs, pairs // 2, x_any, g_any, gain, rows, sems,
        )

    def copies(self, q, i):
        b = 2 * self.half - 1 - i
        return [
            pltpu.make_async_copy(src.at[b, q], self.rows.at[q, j], self.sems.at[q, j])
            for j, src in enumerate((self.x_any, self.g_any))
        ]

    def fetch(self, q, i):
        @pl.when((i >= self.half) & (i < self.pairs))
        def _():
            for copy in self.copies(q, i):
                copy.start()

    def last(self, q, i, total, out):
        @pl.when(i < self.half)
        def _():
            out[q] = total.astype(BF16)

        @pl.when(i >= self.half)
        def _():
            for copy in self.copies(q, i):
                copy.wait()
            x = self.rows[q, 0].astype(F32)
            r1 = inverse_rms(x)
            scaled = total * self.gain
            across = jnp.sum(scaled * x, axis=1, keepdims=True) * (1.0 / x.shape[1])
            out[q] = (self.rows[q, 1].astype(F32) + r1 * scaled - x * (r1 * r1 * r1 * across)).astype(BF16)


def finals_scratch(width):
    return [pltpu.VMEM((4, 2, BLOCK // 4, width), BF16), pltpu.SemaphoreType.DMA((4, 2))]


def dp_bits():
    me = lax.axis_index("dp")
    bits = []
    for b in range(lax.axis_size("dp").bit_length() - 1):
        bit = lax.rem(me // 2**b, 2)
        bits.append((bit, me + (1 - 2 * bit) * 2**b))
    return bits


class Cube:
    def __init__(self, order, refs, across=None):
        self.order, self.across = order, across
        (self.src, self.out, self.total, self.send, self.land, self.out_sem, self.in_sem, self.local) = refs
        self.rows = self.src.shape[0]
        self.bits = dp_bits()
        self.events = 2 * len(order) + (1 if across is None else 2)

    def start_of(self, depth):
        at = 0
        for j in range(depth):
            at = at + self.bits[self.order[j]][0] * (self.rows >> (j + 1))
        return at

    def span(self, at, size):
        return pl.ds(pl.multiple_of(at, 8 if self.src.dtype == F32 else 16), size)

    def inside(self, depth):
        return self.start_of(depth) - self.start_of(1)

    def halving(self, j):
        size = self.rows >> (j + 1)
        bit, partner = self.bits[self.order[j]]
        theirs = self.start_of(j) + (1 - bit) * size
        src = self.src.at[self.span(theirs, size), :] if j == 0 else self.send.at[pl.ds(0, size), :]
        return pltpu.make_async_remote_copy(
            src_ref=src, dst_ref=self.land.at[pl.ds(self.rows - 2 * size, size), :], send_sem=self.out_sem.at[j],
            recv_sem=self.in_sem.at[j], device_id={"dp": partner}, device_id_type=MESH,
        )

    def doubling(self, j):
        count = len(self.order)
        size = self.rows >> (count - j)
        _, partner = self.bits[self.order[count - 1 - j]]
        mine = self.out.at[self.span(self.start_of(count - j), size), :]
        return pltpu.make_async_remote_copy(
            src_ref=mine, dst_ref=mine, send_sem=self.out_sem.at[count + j], recv_sem=self.in_sem.at[count + j],
            device_id={"dp": partner}, device_id_type=MESH,
        )

    def crossing(self, d):
        land, out_sem, in_sem, peers = self.across
        return pltpu.make_async_remote_copy(
            src_ref=self.send.at[pl.ds(0, land.shape[1]), :], dst_ref=land.at[d - 1], send_sem=out_sem.at[d - 1],
            recv_sem=in_sem.at[d - 1], device_id={"tensor": peers[d - 1]}, device_id_type=MESH,
        )

    def turn(self):
        count = len(self.order)
        size = self.rows >> count
        bring(self.send.at[pl.ds(0, size), :], self.out.at[self.span(self.start_of(count), size), :], self.local)
        self.doubling(0).start()

    def event(self, e):
        count = len(self.order)
        if e == 0:
            self.halving(0).start()
            mine = self.src.at[self.span(self.start_of(1), self.rows // 2), :]
            bring(mine, self.send.at[pl.ds(0, self.rows // 2), :], self.local)
            return
        if e <= count:
            self.halving(e - 1).wait()
            size = self.rows >> e
            at = self.inside(e)
            for r in range(0, size, 192):
                tile = min(192, size - r)
                landed = self.land[self.rows - 2 * size + r : self.rows - 2 * size + r + tile, :].astype(F32)
                here = self.span(at + r, tile)
                if e == 1:
                    self.total[here, :] = self.send[r : r + tile, :].astype(F32) + landed
                else:
                    self.total[here, :] = self.total[here, :] + landed
            if e < count:
                bit, _ = self.bits[self.order[e]]
                at = at + (1 - bit) * (size // 2)
                size = size // 2
            self.send[0:size, :] = self.total[self.span(at, size), :].astype(self.send.dtype)
            if e < count:
                self.halving(e).start()
            elif self.across is None:
                self.turn()
            else:
                for d in range(1, len(self.across[3]) + 1):
                    self.crossing(d).start()
            return
        if self.across is not None:
            if e == count + 1:
                size = self.rows >> count
                total = self.total[self.span(self.inside(count), size), :]
                for d in range(1, len(self.across[3]) + 1):
                    self.crossing(d).wait()
                    total = total + self.across[0][d - 1].astype(F32)
                self.send[0:size, :] = total.astype(self.send.dtype)
                self.turn()
                return
            e = e - 1
        self.doubling(e - count - 1).wait()
        if e < 2 * count:
            self.doubling(e - count).start()


def cube_scratch(rows, cols, bits, dtype):
    return [
        pltpu.VMEM((rows // 2, cols), F32),
        pltpu.VMEM((rows // 2, cols), dtype),
        pltpu.VMEM((rows - (rows >> bits), cols), dtype),
        pltpu.SemaphoreType.DMA((2 * bits,)),
        pltpu.SemaphoreType.DMA((2 * bits,)),
        pltpu.SemaphoreType.DMA,
    ]


def cross_scratch(count, rows, cols, dtype):
    return [
        pltpu.VMEM((count - 1, rows, cols), dtype),
        pltpu.SemaphoreType.DMA((count - 1,)),
        pltpu.SemaphoreType.DMA((count - 1,)),
    ]


def tensor_peers(count):
    me = lax.axis_index("tensor")
    return [lax.rem(me + d, count) for d in range(1, count)]


def line_kernel(
    count, pairs, first, steps, xp_ref, x_any, g_any, ng_ref, carry_ref, gz_ref, gx_ref, gb_ref, pk_ref, res_y_in, res_x_in,
    res_y, res_x, oz_ref, ox_ref, ob_ref, op_ref, part, part_sem, rows, sems, *scratch,
):
    del res_y_in, res_x_in
    half = pairs // 2
    order = list(range(len(dp_bits())))
    other = order[:1] + order[:0:-1]
    peers = tensor_peers(count)
    cubes = [
        Cube(order, (gz_ref, oz_ref, *scratch[0:6])),
        Cube(other, (gx_ref, ox_ref, *scratch[6:12])),
        Cube(other, (gb_ref, ob_ref, *scratch[12:18]), (*scratch[24:27], peers)),
        Cube(order, (pk_ref, op_ref, *scratch[18:24]), (*scratch[27:30], peers)),
    ]
    finals = Finals(pairs, x_any, g_any, row_of(ng_ref), rows, sems)
    line = Line(
        count, pairs, first, steps, (res_y, res_x, *scratch[30:]), lambda q, i: part.at[2 * half - 1 - i, q], finals
    )
    at = pl.program_id(0)

    @pl.when(at == 0)
    def _():
        terms = pltpu.make_async_copy(xp_ref.at[pl.ds(0, part.shape[0])], part, part_sem)
        terms.start()
        greet([(peer, peer >= 0) for peer in peers], [partner for _, partner in dp_bits()])
        line.open(carry_ref)
        terms.wait()

    turn = len(order)
    last = 2 * steps - 1
    plain = [0, 1] + [2 * e - 1 for e in range(2, turn)] + [2 * turn - 2, 2 * turn - 1]
    plain += [2 * (turn + j) - 1 for j in range(1, turn - 1)] + [4 * turn - 4]
    crossed = plain[: turn + 1] + [2 * turn - 1, 2 * turn + 1] + plain[turn + 3 :] + [4 * turn - 3]
    times = [plain, plain, crossed, crossed]
    for h in range(2):
        line.step(at, h)
        for cube, when in zip(cubes, times):
            for e, t in enumerate(when):
                t = min(t, last)
                if t % 2 == h:

                    @pl.when(at == t // 2)
                    def _():
                        cube.event(e)

    @pl.when(at == steps - 1)
    def _():
        line.close(None)


def finish_kernel(
    heads, count, x_ref, y_ref, dx_ref, scal_ref, gz_ref, gx_ref, go_ref, go2_ref, gb_ref, pack_ref,
    yo_ref, xo_ref, oz_ref, ox_ref, oo_ref, wbc_ref, wdt_ref, ng_ref, cx_ref, bx_ref, og_ref, ds_ref, cbc_ref, bbc_ref,
    dtb_ref, al_ref,
):
    inner = cx_ref.shape[1]
    width, bcw = x_ref.shape[1], wbc_ref.shape[1]
    me = lax.axis_index("tensor")
    for piece in range(PIECES):
        span = slice(piece * CHUNK, (piece + 1) * CHUNK)
        r2 = jnp.concatenate([scal_ref[piece], jnp.zeros((CHUNK - 8, CHUNK), F32)], axis=0).T[:, 0:1]
        yo_ref[span, :] = (x_ref[span, :].astype(F32) + r2 * y_ref[span, :].astype(F32)).astype(BF16)
    xo_ref[...] = dx_ref[...]
    oz_ref[...] = gz_ref[...].astype(F32)
    ox_ref[...] = gx_ref[...].astype(F32)
    oo_ref[:, 0 : width // 2] = go_ref[...].astype(F32)
    oo_ref[:, width // 2 :] = go2_ref[...].astype(F32)
    wbc_ref[...] = gb_ref[...].astype(F32)

    @pl.when(pl.program_id(0) == 0)
    def _():
        at = 0
        base = pl.multiple_of(at + me * dt_rows(width), 8)
        for j in range(width // LANES):
            wdt_ref[:, j * LANES : (j + 1) * LANES] = pack_ref[pl.ds(base + 16 * j, 16), :][0:heads, :]
        at += count * dt_rows(width)
        def put(ref, row):
            ref[...] = row.reshape(ref.shape)

        put(ng_ref, jnp.concatenate([pack_ref[at + 8 * j : at + 8 * j + 1, :] for j in range(width // LANES)], axis=1))
        at += width // LANES * 8
        rows = jnp.concatenate([pack_ref[at + 8 * j : at + 8 * j + 8, :] for j in range(bcw // LANES)], axis=1)
        cbc_ref[...] = rows[0:4, :]
        put(bbc_ref, rows[4:5, :])
        at += bcw // LANES * 8
        base = pl.multiple_of(at + me * slot_rows(inner), 8)
        rows = jnp.concatenate([pack_ref[pl.ds(base + 8 * j, 8), :] for j in range(inner // LANES)], axis=1)
        cx_ref[...] = rows[0:4, :]
        put(bx_ref, rows[4:5, :])
        put(og_ref, rows[6:7, :])
        lane = lax.broadcasted_iota(jnp.int32, (1, heads), 1)
        skip = jnp.zeros((1, heads), F32)
        for h in range(heads):
            head = jnp.sum(rows[5:6, h * 64 : h * 64 + 64], axis=1, keepdims=True)
            skip = jnp.where(lane == h, head, skip)
        ds_ref[...] = skip
        rows = pack_ref[pl.ds(base + inner // LANES * 8, 8), :]
        dtb_ref[...] = rows[0:1, 0:heads]
        al_ref[...] = rows[1:2, 0:heads]


def forward_kernel(
    heads, count, pairs, steps, blocks,
    x_ref, g_ref, segr_ref, wz_ref, wx_ref, wbc_ref, wdt_ref, wo_ref, ng_ref, bx_ref, og_ref, bbc_ref, cx_ref, cbc_ref,
    dtb_ref, al_ref, dsk_ref,
    z_ref, p_ref, xc_ref, ys_ref, pbc_ref, bc_ref, dtr_ref, dn_ref, st_ref, yp_ref, scal_ref, wout_ref,
    carry_out, res_y, res_x,
    hv_ref, wdt_s, hist, hist_bc, segs, state, scaled_s, g_s, acc_out, stat_mine, stat_land, stat_out, stat_in, part, *scratch,
):
    rows, width = x_ref.shape
    inner = z_ref.shape[1]
    block = pl.program_id(0)
    me = lax.axis_index("tensor")
    ng, bx, og, bbc = row_of(ng_ref), row_of(bx_ref), row_of(og_ref), row_of(bbc_ref)

    line = Line(count, pairs, 0, steps, (res_y, res_x, *scratch), lambda q, i: part.at[i, q])

    @pl.when(block == 0)
    def _():
        greet([(lax.rem(me + d, count), me >= 0) for d in range(1, count)])
        fill_heads(hv_ref, wdt_s, dtb_ref, al_ref, dsk_ref, wdt_ref)
        hist[0:8, :] = jnp.zeros((8, hist.shape[1]), F32)
        hist_bc[0:8, :] = jnp.zeros((8, hist_bc.shape[1]), F32)
        segs[0:8, :] = jnp.full((8, 1), -1.0, F32)
        state[...] = jnp.zeros_like(state)
        acc_out[...] = jnp.zeros_like(acc_out)

    x = x_ref[...].astype(F32)
    xn = (x * inverse_rms(x) * ng).astype(BF16)
    z_ref[...] = dot(xn, wz_ref[...])
    xc = dot(xn, wx_ref[...])
    bc = dot(xn, wbc_ref[...])
    dtr = dot_t(xn, wdt_s[...])
    xc_ref[...] = xc.astype(BF16)
    bc_ref[...] = bc
    dtr_ref[...] = dtr
    seg_all = columns_of(segr_ref)
    segs[8 : 8 + rows, :] = seg_all
    hist[8 : 8 + rows, :] = xc
    hist_bc[8 : 8 + rows, :] = bc
    same = [(segs[8 - k : 8 - k + rows, :] == seg_all).astype(F32) for k in range(1, 4)]
    p_ref[...] = conv_taps(hist, cx_ref, same, rows) + bx
    pbc_ref[...] = conv_taps(hist_bc, cbc_ref, same, rows) + bbc
    g = g_ref[...]
    g_s[lax.rem(block, 2)] = g
    dn_ref[...] = dot_t(g, wo_ref[...])
    dt_all = softplus(dtr + hv_ref[0:1, :])
    la_all = -jnp.exp(hv_ref[1:2, :]) * dt_all
    dsk = spread(hv_ref[2:3, :], heads)
    row_i, lane_i = iotas(CHUNK, LANES)
    for piece in range(PIECES):
        at = pl.ds(piece * CHUNK, CHUNK)
        span = slice(piece * CHUNK, (piece + 1) * CHUNK)
        seg_col = seg_all[span, :]
        keep = (seg_col == segs[7 + piece * CHUNK : 8 + piece * CHUNK, :]).astype(F32)
        tail = (seg_col == seg_col[CHUNK - 1 : CHUNK, :]).astype(F32)
        dt = dt_all[span, :]
        cum, cum_t, visible = decays(la_all[span, :], seg_col, segr_ref[:, span].astype(F32))
        p = p_ref[at, :]
        u = p * sigmoid(p)
        pbc = pbc_ref[at, :]
        bcu = (pbc * sigmoid(pbc)).astype(BF16)
        n = bcu.shape[1] // 2
        b, c = bcu[:, :n], bcu[:, n:]
        scores = dot_t(c, b)
        v = spread(dt, heads) * u
        v_low = v.astype(BF16)
        pieces = []
        for pair in range(heads // 2):
            mats = [
                (scores * decay_matrix(cum, cum_t, visible, 2 * pair + k)).astype(BF16)
                for k in range(2)
            ]
            halves = split_pair(v_low[:, pair * LANES : (pair + 1) * LANES])
            pieces.append(dot(jnp.concatenate(mats, axis=1), jnp.concatenate(halves, axis=0)))
        inside = jnp.concatenate(pieces, axis=1)
        old = state[...]
        old_low = old.astype(BF16)
        st_ref[piece] = old_low
        entering = dot(c, old_low) * spread(jnp.exp(cum) * keep, heads)
        last = cum[CHUNK - 1 : CHUNK, :]
        to_end = spread(jnp.exp(last - cum) * tail, heads)
        carry = spread(jnp.exp(last) * keep[CHUNK - 1 : CHUNK, :], heads)
        state[...] = old * carry + tdot(b, (to_end * v).astype(BF16))
        ys = inside + entering + dsk * u
        ys_ref[at, :] = ys
        z = z_ref[at, :]
        gated = ys * (z * sigmoid(z))
        scaled = gated * og
        scaled_s[lax.rem(block, 2), at, :] = scaled
        y_part = dot(scaled.astype(BF16), wo_ref[...]).astype(BF16)
        for q in range(2):
            yp_ref[0, 2 * piece + q] = y_part[q * 64 : q * 64 + 64, :]

        @pl.when(block < part.shape[0])
        def _():
            for q in range(2):
                part[jnp.minimum(block, part.shape[0] - 1), 2 * piece + q] = y_part[q * 64 : q * 64 + 64, :]

        if piece == 0:

            @pl.when((block >= 4) & (lax.rem(block, 2) == 0))
            def _():
                line.step(block // 2 + 1, 1)

            @pl.when((block < 4) | (lax.rem(block, 2) == 1))
            def _():
                line.step(jnp.where(block < 4, block, (block + 3) // 2), 0)

        else:

            @pl.when(block < 3)
            def _():
                line.step(block, 1)

        sums = jnp.sum(gated * gated, axis=1, keepdims=True)
        across = jnp.sum(dn_ref[at, :] * scaled, axis=1, keepdims=True)
        both = jnp.where(lane_i == 0, sums, jnp.where(lane_i == 1, across, 0.0))
        stat_mine[block, piece] = both.T[0:8, :]
    hist[0:8, :] = hist[rows : rows + 8, :]
    hist_bc[0:8, :] = hist_bc[rows : rows + 8, :]
    segs[0:8, :] = segs[rows : rows + 8, :]

    def stat_copy(d, b):
        return pltpu.make_async_remote_copy(
            src_ref=stat_mine.at[b], dst_ref=stat_land.at[d - 1, b], send_sem=stat_out.at[d - 1, b],
            recv_sem=stat_in.at[d - 1, b], device_id={"tensor": lax.rem(me + d, count)}, device_id_type=MESH,
        )

    def settle(b):
        total = stat_mine[b]
        for d in range(1, count):
            stat_copy(d, b).wait()
            total = total + stat_land[d - 1, b]
        place = lax.rem(b, 2)
        low = []
        for piece in range(PIECES):
            r2 = lax.rsqrt(total[piece, 0:1, :] * (1.0 / (inner * count)) + EPS)
            k2 = r2 * r2 * r2 * (total[piece, 1:2, :] * (1.0 / (inner * count)))
            both = jnp.where(row_i == 0, r2, jnp.where(row_i == 1, k2, 0.0))
            scal_ref[b * PIECES + piece] = both[0:8, :]
            low.append((scaled_s[place, piece * CHUNK : (piece + 1) * CHUNK, :] * both.T[:, 0:1]).astype(BF16))
        normed = jnp.concatenate(low, axis=0)
        up = g_s[place]
        for c in range(0, inner, 256):
            acc_out[c : c + 256, :] += tdot(normed[:, c : c + 256], up)

    for d in range(1, count):
        stat_copy(d, block).start()

    @pl.when(block > 0)
    def _():
        settle(block - 1)

    @pl.when(block == blocks - 1)
    def _():
        settle(block)
        for c in range(0, inner, 256):
            low = acc_out[c : c + 256, :].astype(BF16)
            wout_ref[c : c + 256, :] = low[:, 0 : width // 2]
            wout_ref[inner + c : inner + c + 256, :] = low[:, width // 2 :]
        line.step(jnp.int32(steps - 1), 1)
        line.close(carry_out)


def backward_kernel(
    heads, count, pairs, first, steps,
    z_ref, p_ref, xc_ref, ys_ref, pbc_ref, bc_ref, dtr_ref, dn_ref, st_ref, segp_ref, segr_ref, scal_ref, x_ref,
    wz_ref, wx_ref, wbc_ref, wdt_ref, ng_ref, og_ref, cx_ref, cbc_ref, dtb_ref, al_ref, dsk_ref, y_ref, x_any, g_any, carry_ref, go_ref, res_y_in, res_x_in,
    xp_ref, gz_ref, gx_ref, gb_ref, pack_ref, carry_out, go_sum, res_y, res_x,
    hv_ref, wdt_s, ahead, ahead_bc, segs, d_state, dz_s, dx_s, ddt_s, dbc_s, acc_z, acc_x, acc_bc, acc_dt,
    a1536, a768, a256, a128, rest, low_bc, stage, stage_sem, part, part_sem, rows_s, rows_sem, *scratch,
):
    del res_y_in, res_x_in
    rows, inner = z_ref.shape
    width = x_ref.shape[1]
    block = pl.program_id(0)
    blocks = steps
    half = pairs // 2
    me = lax.axis_index("tensor")
    ng, og = row_of(ng_ref), row_of(og_ref)

    finals = Finals(pairs, x_any, g_any, ng, rows_s, rows_sem)
    line = Line(
        count, pairs, first, steps, (res_y, res_x, *scratch[6:]), lambda q, i: part.at[lax.rem(i, half), q], finals
    )
    cube = Cube(list(range(len(dp_bits()))), (go_ref, go_sum, *scratch[0:6]))
    old = first - (count - 1)

    @pl.when(block == 0)
    def _():
        terms = pltpu.make_async_copy(y_ref.at[pl.ds(old, half - old)], part.at[pl.ds(old, half - old)], part_sem)
        terms.start()
        greet(neighbours(count), [partner for _, partner in dp_bits()])
        line.open(carry_ref)
        terms.wait()
        fill_heads(hv_ref, wdt_s, dtb_ref, al_ref, dsk_ref, wdt_ref)
        ahead[rows : rows + 8, :] = jnp.zeros((8, ahead.shape[1]), F32)
        ahead_bc[rows : rows + 8, :] = jnp.zeros((8, ahead_bc.shape[1]), F32)
        segs[rows : rows + 8, :] = jnp.full((8, 1), -1.0, F32)
        for ref in (d_state, acc_z, acc_x, acc_bc, acc_dt, a1536, a768, a256, a128, rest):
            ref[...] = jnp.zeros_like(ref)

    line.step(block, 0)
    seg_all = columns_of(segr_ref)
    segs[0:rows, :] = seg_all
    before = jnp.where(block == blocks - 1, -1.0, segp_ref[:, rows - 1 : rows].astype(F32))
    r, c_ = iotas(CHUNK, CHUNK)
    upper = (r <= c_).astype(F32)
    below = (r > c_).astype(F32)
    seg_r, seg_l = iotas(inner, LANES)
    to_head = (seg_r // (inner // heads) == seg_l).astype(BF16)
    two_r, two_l = iotas(2 * CHUNK, LANES)
    decay_rate = -jnp.exp(hv_ref[1:2, :])
    dsk = spread(hv_ref[2:3, :], heads)
    for piece in reversed(range(PIECES)):
        at = pl.ds(piece * CHUNK, CHUNK)
        span = slice(piece * CHUNK, (piece + 1) * CHUNK)
        seg_col = seg_all[span, :]
        prev = seg_all[piece * CHUNK - 1 : piece * CHUNK, :] if piece else before
        keep = (seg_col == prev).astype(F32)
        tail = (seg_col == seg_col[CHUNK - 1 : CHUNK, :]).astype(F32)
        scal = jnp.concatenate([scal_ref[piece], jnp.zeros((CHUNK - 8, CHUNK), F32)], axis=0).T
        r2 = scal[:, 0:1]
        k2 = scal[:, 1:2]
        pre = dtr_ref[at, :] + hv_ref[0:1, :]
        dt = softplus(pre)
        la = decay_rate * dt
        cum, cum_t, visible = decays(la, seg_col, segr_ref[:, span].astype(F32))
        z = z_ref[at, :]
        ys = ys_ref[at, :]
        sz = sigmoid(z)
        silu = z * sz
        gated = ys * silu
        dn = dn_ref[at, :]
        d_gated = r2 * og * dn - gated * k2
        a768[6:7, :] += jnp.sum(dn * gated * r2, axis=0, keepdims=True)
        dz_s[at, :] = (d_gated * ys * (sz * (1.0 + z * (1.0 - sz)))).astype(BF16)
        dy = d_gated * silu
        dy_low = dy.astype(BF16)
        p = p_ref[at, :]
        sp = sigmoid(p)
        u = p * sp
        a768[5:6, :] += jnp.sum(dy * u, axis=0, keepdims=True)
        pbc = pbc_ref[at, :]
        spbc = sigmoid(pbc)
        bcu = (pbc * spbc).astype(BF16)
        n = bcu.shape[1] // 2
        b, c = bcu[:, :n], bcu[:, n:]
        scores = dot_t(c, b)
        dt_x = spread(dt, heads)
        v = dt_x * u
        v_low = v.astype(BF16)
        d_scores = jnp.zeros((CHUNK, CHUNK), F32)
        d_cum = jnp.zeros((CHUNK, LANES), F32)
        pieces = []
        for pair in range(heads // 2):
            lanes = slice(pair * LANES, (pair + 1) * LANES)
            dy_halves = jnp.concatenate(split_pair(dy_low[:, lanes]), axis=0)
            grads = dot_t(dy_halves, v_low[:, lanes])
            mats, weighed = [], []
            for k in range(2):
                decay = decay_matrix(cum, cum_t, visible, 2 * pair + k)
                grad = grads[k * CHUNK : (k + 1) * CHUNK, :]
                mat = scores * decay
                d_scores = d_scores + grad * decay
                weighed.append((grad * mat).astype(BF16))
                mats.append(mat.astype(BF16))
            pieces.append(tdot(jnp.concatenate(mats, axis=0), dy_halves))
            pick = (two_l == 2 * pair + two_r // CHUNK).astype(BF16)
            d_cum = d_cum + dot(jnp.concatenate(weighed, axis=1), pick)
            d_cum = d_cum - tdot(jnp.concatenate(weighed, axis=0), pick)
        old_low = st_ref[piece]
        last = cum[CHUNK - 1 : CHUNK, :]
        enter_x = spread(jnp.exp(cum) * keep, heads)
        end_x = spread(jnp.exp(last - cum) * tail, heads)
        carry = spread(jnp.exp(last) * keep[CHUNK - 1 : CHUNK, :], heads)
        ds = d_state[...]
        ds_low = ds.astype(BF16)
        dv_state = end_x * dot(b, ds_low)
        dv = jnp.concatenate(pieces, axis=1) + dv_state
        dy_enter = enter_x * dy
        dy_enter_low = dy_enter.astype(BF16)
        d_b = dot_t((end_x * v).astype(BF16), ds_low)
        d_c = dot_t(dy_enter_low, old_low)
        e = dot((dy_enter * dot(c, old_low)).astype(BF16), to_head)
        f = dot((dv_state * v).astype(BF16), to_head)
        flow = jnp.sum(ds * old_low.astype(F32) * carry, axis=0, keepdims=True)
        flow = dot(flow, to_head.astype(F32), HIGHEST)
        d_state[...] = carry * ds + tdot(c, dy_enter_low)
        d_scores_low = d_scores.astype(BF16)
        d_c = d_c + dot(d_scores_low, b)
        d_b = d_b + tdot(d_scores_low, c)
        d_la = dot(upper, d_cum + e, HIGHEST) + dot(below, f, HIGHEST) + flow
        d_dt = d_la * decay_rate + dot((dv * u).astype(BF16), to_head)
        d_pre = d_dt * sigmoid(pre)
        ddt_s[at, :] = d_pre.astype(BF16)
        a128[0:1, :] += jnp.sum(d_pre, axis=0, keepdims=True)
        a128[1:2, :] += jnp.sum(d_la * la, axis=0, keepdims=True)
        du = dt_x * dv + dsk * dy
        ahead[at, :] = du * (sp * (1.0 + p * (1.0 - sp)))
        d_bcu = jnp.concatenate([d_b, d_c], axis=1)
        ahead_bc[at, :] = d_bcu * (spbc * (1.0 + pbc * (1.0 - spbc)))

    line.step(block, 1)
    for e in range(cube.events):

        @pl.when(block == min(e, blocks - 1))
        def _():
            cube.event(e)

    same = [(segs[k : k + rows, :] == seg_all).astype(F32) for k in range(1, 4)]
    for hist, weight, raw, out, acc in (
        (ahead, cx_ref, xc_ref, dx_s, a768),
        (ahead_bc, cbc_ref, bc_ref, dbc_s, a256),
    ):
        value = raw[...].astype(F32)
        dp = hist[0:rows, :]
        acc[4:5, :] += jnp.sum(dp, axis=0, keepdims=True)
        acc[3:4, :] += jnp.sum(dp * value, axis=0, keepdims=True)
        total = dp * weight[3:4, :]
        for k in range(1, 4):
            later = hist[k : k + rows, :] * same[k - 1]
            total = total + later * weight[3 - k : 4 - k, :]
            acc[3 - k : 4 - k, :] += jnp.sum(later * value, axis=0, keepdims=True)
        out[...] = total.astype(BF16)
        hist[rows : rows + 8, :] = hist[0:8, :]
    segs[rows : rows + 8, :] = segs[0:8, :]
    partial = dot_t(dz_s[...], wz_ref[...]) + dot_t(dx_s[...], wx_ref[...])
    partial = partial + dot(ddt_s[...], wdt_s[...]) + dot_t(dbc_s[...], wbc_ref[...])
    for piece in range(PIECES):
        low = partial[piece * CHUNK : (piece + 1) * CHUNK, :].astype(BF16)
        for q in range(2):
            xp_ref[0, 2 * piece + q] = low[q * 64 : q * 64 + 64, :]

        @pl.when(first + block < pairs)
        def _():
            for q in range(2):
                part[block, 2 * piece + q] = low[q * 64 : q * 64 + 64, :]

    x = x_ref[...].astype(F32)
    xr = x * inverse_rms(x)
    a1536[0:1, :] += jnp.sum(partial * xr, axis=0, keepdims=True)
    xn = (xr * ng).astype(BF16)
    for w in range(0, width, 512):
        left = xn[:, w : w + 512]
        acc_z[w : w + 512, :] += tdot(left, dz_s[...])
        acc_x[w : w + 512, :] += tdot(left, dx_s[...])
        for j in range(acc_bc.shape[0]):
            acc_bc[j, w : w + 512, :] += tdot(left, dbc_s[:, j * LANES : (j + 1) * LANES])
        acc_dt[w : w + 512, :] += tdot(left, ddt_s[...])
    @pl.when(block == blocks - 1)
    def _():
        bits = [(acc_z, gz_ref, w) for w in range(0, width, 256)] + [(acc_x, gx_ref, w) for w in range(0, width, 256)]
        copies = []
        for j, (acc, out, w) in enumerate(bits):
            if j >= 2:
                copies[j - 2].wait()
            stage[j % 2] = acc[w : w + 256, :].astype(BF16)
            copies.append(pltpu.make_async_copy(stage.at[j % 2], out.at[pl.ds(w, 256), :], stage_sem.at[j % 2]))
            copies[j].start()
        copies[-2].wait()
        copies[-1].wait()
        for j in range(acc_bc.shape[0]):
            low_bc[:, j * LANES : (j + 1) * LANES] = acc_bc[j].astype(BF16)
        turned = pl.multiple_of(me * dt_rows(width), 8)
        for j in range(width // LANES):
            rest[pl.ds(turned + 16 * j, 16), :] = acc_dt[j * LANES : (j + 1) * LANES, :].T[0:16, :]
        base = count * dt_rows(width)
        for acc in (a1536, a256):
            for j in range(acc.shape[1] // LANES):
                rest[base : base + 8, :] = acc[:, j * LANES : (j + 1) * LANES]
                base += 8
        mine = pl.multiple_of(base + me * slot_rows(inner), 8)
        for j in range(inner // LANES):
            rest[pl.ds(mine + 8 * j, 8), :] = a768[:, j * LANES : (j + 1) * LANES]
        rest[pl.ds(mine + inner // LANES * 8, 8), :] = a128[...]
        first_copy = pltpu.make_async_copy(rest, pack_ref, stage_sem.at[2])
        second_copy = pltpu.make_async_copy(low_bc, gb_ref, stage_sem.at[3])
        first_copy.start()
        second_copy.start()
        first_copy.wait()
        second_copy.wait()
        line.close(carry_out)


def dt_rows(width):
    return width // LANES * 16


def slot_rows(inner):
    return (inner // LANES + 1) * 8


def rows_spec(block, cols, last=None):
    if last is None:
        return pl.BlockSpec((block, cols), lambda i: (i, 0))
    return pl.BlockSpec((block, cols), lambda i: (last - i, 0))


def whole_spec(array):
    return pl.BlockSpec(array.shape, lambda i: (0,) * array.ndim, pipeline_mode=pl.Buffered(1))


def fixed_spec(*dims):
    return pl.BlockSpec(dims, lambda i: (0,) * len(dims))


def on_device(
    x_in, segments, out_grad, norm_gain, w_z, w_x, w_bc, w_dt, conv_x, conv_bc, bias_x, bias_bc,
    dt_bias, a_log, d_skip, out_gain, w_out,
):
    count = lax.axis_size("tensor")
    x, g = x_in[0], out_grad[0]
    length, width = x.shape
    inner = w_x.shape[1]
    heads = w_dt.shape[1]
    bcw = w_bc.shape[1]
    state_n = bcw // 2
    blocks = length // BLOCK
    chunks = length // CHUNK
    last = blocks - 1
    pairs = 2 * blocks
    all_steps = pairs + 2 * count - 3
    n_fwd = (blocks + 4) // 2
    n_bwd = blocks
    rest = all_steps - n_fwd - n_bwd
    wdt = w_dt.T
    per_head = (dt_bias[None, :], a_log[None, :], d_skip[None, :])
    x4 = x.reshape(blocks, 4, BLOCK // 4, width)
    g4 = g.reshape(blocks, 4, BLOCK // 4, width)
    shape = jax.ShapeDtypeStruct
    anywhere = pl.BlockSpec(memory_space=pl.ANY)
    pair_shape = (blocks, 4, BLOCK // 4, width)
    carry_shape = shape((4, BLOCK // 4, width), BF16)
    res_shape = shape(pair_shape, BF16)

    def params(ident):
        return pltpu.CompilerParams(
            vmem_limit_bytes=62 * 2**20, dimension_semantics=("arbitrary",), collective_id=ident, has_side_effects=True
        )

    def cost(flops, moved):
        return pl.CostEstimate(flops=flops, bytes_accessed=moved, transcendentals=0)

    weights = (w_z, w_x, w_bc, wdt, w_out, norm_gain, bias_x, out_gain, bias_bc, conv_x, conv_bc, *per_head)
    z, p, xc, ys, pbc, bc, dtr, dn, st, yp, scal, gout, carry, res_y, res_x = pl.pallas_call(
        functools.partial(forward_kernel, heads, count, pairs, n_fwd, blocks),
        grid=(blocks,),
        in_specs=[
            rows_spec(BLOCK, width),
            rows_spec(BLOCK, width),
            pl.BlockSpec((1, BLOCK), lambda i: (0, i)),
            *[whole_spec(w) for w in weights],
        ],
        out_specs=[
            rows_spec(BLOCK, inner),
            rows_spec(BLOCK, inner),
            rows_spec(BLOCK, inner),
            rows_spec(BLOCK, inner),
            rows_spec(BLOCK, bcw),
            rows_spec(BLOCK, bcw),
            rows_spec(BLOCK, LANES),
            rows_spec(BLOCK, inner),
            pl.BlockSpec((PIECES, state_n, inner), lambda i: (i, 0, 0)),
            pl.BlockSpec((1, 4, BLOCK // 4, width), lambda i: (i, 0, 0, 0)),
            fixed_spec(chunks, 8, CHUNK),
            fixed_spec(2 * inner, width // 2),
            anywhere,
            anywhere,
            anywhere,
        ],
        out_shape=[
            shape((length, inner), F32),
            shape((length, inner), F32),
            shape((length, inner), BF16),
            shape((length, inner), F32),
            shape((length, bcw), F32),
            shape((length, bcw), F32),
            shape((length, LANES), F32),
            shape((length, inner), F32),
            shape((chunks, state_n, inner), BF16),
            shape(pair_shape, BF16),
            shape((chunks, 8, CHUNK), F32),
            shape((2 * inner, width // 2), BF16),
            carry_shape,
            res_shape,
            res_shape,
        ],
        scratch_shapes=[
            pltpu.VMEM((8, LANES), F32),
            pltpu.VMEM((LANES, width), BF16),
            pltpu.VMEM((BLOCK + 8, inner), F32),
            pltpu.VMEM((BLOCK + 8, bcw), F32),
            pltpu.VMEM((BLOCK + 8, 1), F32),
            pltpu.VMEM((state_n, inner), F32),
            pltpu.VMEM((2, BLOCK, inner), F32),
            pltpu.VMEM((2, BLOCK, width), BF16),
            pltpu.VMEM((inner, width), F32),
            pltpu.VMEM((blocks, PIECES, 8, CHUNK), F32),
            pltpu.VMEM((count - 1, blocks, PIECES, 8, CHUNK), F32),
            pltpu.SemaphoreType.DMA((count - 1, blocks)),
            pltpu.SemaphoreType.DMA((count - 1, blocks)),
            pltpu.VMEM((n_fwd, 4, BLOCK // 4, width), BF16),
            *line_scratch(n_fwd, width),
        ],
        compiler_params=params(0),
        cost_estimate=cost(9 * 10**10, 10**8),
        name="forward_scan",
    )(x, g, segments, *weights)

    weights = (w_z, w_x, w_bc, wdt, norm_gain, out_gain, conv_x, conv_bc, *per_head)
    n_in = 13 + len(weights)
    bits = lax.axis_size("dp").bit_length() - 1
    used = (width + bcw) // LANES * 8 + count * (slot_rows(inner) + dt_rows(width))
    pack_rows = -(-used // 256) * 256
    xp, gz, gx, gbc, pack, carry, gout, res_y, res_x = pl.pallas_call(
        functools.partial(backward_kernel, heads, count, pairs, n_fwd, n_bwd),
        grid=(blocks,),
        in_specs=[
            rows_spec(BLOCK, inner, last),
            rows_spec(BLOCK, inner, last),
            rows_spec(BLOCK, inner, last),
            rows_spec(BLOCK, inner, last),
            rows_spec(BLOCK, bcw, last),
            rows_spec(BLOCK, bcw, last),
            rows_spec(BLOCK, LANES, last),
            rows_spec(BLOCK, inner, last),
            pl.BlockSpec((PIECES, state_n, inner), lambda i: (last - i, 0, 0)),
            pl.BlockSpec((1, BLOCK), lambda i: (0, jnp.maximum(last - i - 1, 0))),
            pl.BlockSpec((1, BLOCK), lambda i: (0, last - i)),
            pl.BlockSpec((PIECES, 8, CHUNK), lambda i: (last - i, 0, 0)),
            rows_spec(BLOCK, width, last),
            *[whole_spec(w) for w in weights],
            *[anywhere] * 7,
        ],
        out_specs=[
            pl.BlockSpec((1, 4, BLOCK // 4, width), lambda i: (last - i, 0, 0, 0)),
            *[anywhere] * 8,
        ],
        out_shape=[
            shape(pair_shape, BF16),
            shape((width, inner), BF16),
            shape((width, inner), BF16),
            shape((width, bcw), BF16),
            shape((pack_rows, LANES), F32),
            carry_shape,
            shape((2 * inner, width // 2), BF16),
            res_shape,
            res_shape,
        ],
        scratch_shapes=[
            pltpu.VMEM((8, LANES), F32),
            pltpu.VMEM((LANES, width), BF16),
            pltpu.VMEM((BLOCK + 8, inner), F32),
            pltpu.VMEM((BLOCK + 8, bcw), F32),
            pltpu.VMEM((BLOCK + 8, 1), F32),
            pltpu.VMEM((state_n, inner), F32),
            pltpu.VMEM((BLOCK, inner), BF16),
            pltpu.VMEM((BLOCK, inner), BF16),
            pltpu.VMEM((BLOCK, LANES), BF16),
            pltpu.VMEM((BLOCK, bcw), BF16),
            pltpu.VMEM((width, inner), F32),
            pltpu.VMEM((width, inner), F32),
            pltpu.VMEM((bcw // LANES, width, LANES), F32),
            pltpu.VMEM((width, LANES), F32),
            pltpu.VMEM((8, width), F32),
            pltpu.VMEM((8, inner), F32),
            pltpu.VMEM((8, bcw), F32),
            pltpu.VMEM((8, LANES), F32),
            pltpu.VMEM((pack_rows, LANES), F32),
            pltpu.VMEM((width, bcw), BF16),
            pltpu.VMEM((2, 256, inner), BF16),
            pltpu.SemaphoreType.DMA((4,)),
            pltpu.VMEM((blocks, 4, BLOCK // 4, width), BF16),
            pltpu.SemaphoreType.DMA,
            *finals_scratch(width),
            *cube_scratch(2 * inner, width // 2, bits, BF16),
            *line_scratch(n_bwd, width),
        ],
        input_output_aliases={n_in + 5: 7, n_in + 6: 8},
        compiler_params=params(1),
        cost_estimate=cost(12 * 10**10, 10**8),
        name="backward_scan",
    )(z, p, xc, ys, pbc, bc, dtr, dn, st, segments, segments, scal, x, *weights, yp, x4, g4, carry, gout, res_y, res_x)

    left = pairs - (n_fwd + n_bwd - (count - 1))
    res_y, res_x, gz, gx, gbc, pack = pl.pallas_call(
        functools.partial(line_kernel, count, pairs, n_fwd + n_bwd, rest),
        grid=(rest,),
        in_specs=[anywhere] * 3 + [whole_spec(norm_gain)] + [anywhere] * 7,
        out_specs=[anywhere] * 6,
        out_shape=[
            res_shape,
            res_shape,
            shape((width, inner), BF16),
            shape((width, inner), BF16),
            shape((width, bcw), BF16),
            shape((pack_rows, LANES), F32),
        ],
        scratch_shapes=[
            pltpu.VMEM((left, 4, BLOCK // 4, width), BF16),
            pltpu.SemaphoreType.DMA,
            *finals_scratch(width),
            *cube_scratch(width, inner, bits, BF16),
            *cube_scratch(width, inner, bits, BF16),
            *cube_scratch(width, bcw, bits, BF16),
            *cube_scratch(pack_rows, LANES, bits, F32),
            *cross_scratch(count, width >> bits, bcw, BF16),
            *cross_scratch(count, pack_rows >> bits, LANES, F32),
            *line_scratch(rest, width),
        ],
        input_output_aliases={9: 0, 10: 1},
        compiler_params=params(2),
        cost_estimate=cost(10**11, 3 * 10**8),
        name="line_sums",
    )(xp, x4, g4, norm_gain, carry, gz, gx, gbc, pack, res_y, res_x)

    wide = width // blocks
    tall = inner // blocks
    outs = pl.pallas_call(
        functools.partial(finish_kernel, heads, count),
        grid=(blocks,),
        in_specs=[
            rows_spec(BLOCK, width),
            rows_spec(BLOCK, width),
            rows_spec(BLOCK, width),
            pl.BlockSpec((PIECES, 8, CHUNK), lambda i: (i, 0, 0)),
            rows_spec(wide, inner),
            rows_spec(wide, inner),
            rows_spec(tall, width // 2),
            pl.BlockSpec((tall, width // 2), lambda i: (i + blocks, 0)),
            rows_spec(wide, bcw),
            whole_spec(pack),
        ],
        out_specs=[
            rows_spec(BLOCK, width),
            rows_spec(BLOCK, width),
            rows_spec(wide, inner),
            rows_spec(wide, inner),
            rows_spec(tall, width),
            rows_spec(wide, bcw),
            fixed_spec(heads, width),
            fixed_spec(width),
            fixed_spec(4, inner),
            fixed_spec(inner),
            fixed_spec(inner),
            fixed_spec(1, heads),
            fixed_spec(4, bcw),
            fixed_spec(bcw),
            fixed_spec(1, heads),
            fixed_spec(1, heads),
        ],
        out_shape=[
            shape((length, width), BF16),
            shape((length, width), BF16),
            shape((width, inner), F32),
            shape((width, inner), F32),
            shape((inner, width), F32),
            shape((width, bcw), F32),
            shape((heads, width), F32),
            shape((width,), F32),
            shape((4, inner), F32),
            shape((inner,), F32),
            shape((inner,), F32),
            shape((1, heads), F32),
            shape((4, bcw), F32),
            shape((bcw,), F32),
            shape((1, heads), F32),
            shape((1, heads), F32),
        ],
        compiler_params=pltpu.CompilerParams(vmem_limit_bytes=60 * 2**20, dimension_semantics=("arbitrary",)),
        name="finish",
    )(x, res_y.reshape(length, width), res_x.reshape(length, width), scal, gz, gx, gout, gout, gbc, pack)
    result, grad_x, gz, gx, gout, grad_wbc, grad_wdt, ng, cx, bx, og, ds, cbc, bbc, dtb, al = outs
    return (
        result[None], grad_x[None], ng, gz, gx, grad_wbc, grad_wdt.T, cx, cbc, bx, bbc, dtb[0], al[0], ds[0],
        og, gout,
    )


def solution(mesh):
    tensor_last = P(None, "tensor")
    in_specs = (
        P("dp", None, None), P("dp", None), P("dp", None, None), P(), tensor_last, tensor_last, P(), tensor_last,
        tensor_last, P(), P("tensor"), P(), P("tensor"), P("tensor"), P("tensor"), P("tensor"), P("tensor", None),
    )
    out_specs = (
        P("dp", None, None), P("dp", None, None), P(), tensor_last, tensor_last, P(), tensor_last, tensor_last, P(),
        P("tensor"), P(), P("tensor"), P("tensor"), P("tensor"), P("tensor"), P("tensor", None),
    )
    return jax.shard_map(on_device, mesh=mesh, in_specs=in_specs, out_specs=out_specs, check_vma=False)
```

time: 612 us -> 389 us (0.64); the launches traced: 603 us -> 388 us
  blocking collectives: 104 us -> 0 us
  other arithmetic: 46 us -> 0 us
  Pallas kernels: 349 us -> 387 us
  matrix products: 35.9 us -> 0 us
  local copies, waits for them, and re-layouts: 30.2 us -> 0 us
  waiting for transfers between devices: 24 us -> 0 us
  between operations: 14.4 us -> 0.85 us
    psum x3 -> x0, blocking collectives: 104 us -> none  [the longest x1 41.7 us: on_device(): sums = lax.psum(stat[:, :2].T, 'tensor')]
    pallas_call x3 -> x4, Pallas kernels: 349 us -> 387 us  [the longest x1 150 us: on_device(): pl.pallas_call(functools.partial(backward_kernel, heads, count, pairs, n_...]
    dot_general x5 -> x0, matrix products: 35.9 us -> none  [tdot(): lax.dot_general(a, b, (((0,), (0,)), ((), ())), preferred_element_type=F32)]
    convert_element_type x7 -> x0, other arithmetic: 33.6 us -> none  [the longest x1 13 us: on_device(): (g.astype(F32) + r1 * norm_gain * dxn - tokens * (r1 * r1 * r1 * dot_x /...]
    psum x3 -> x0, waiting for transfers between devices: 23.9 us -> none  [the longest x1 23.9 us: on_device(): grad_wbc = lax.psum(grad_wbc, ('dp', 'tensor'))]
    reduce_sum x3 -> x0, other arithmetic: 11.3 us -> none  [the longest x1 6.54 us: on_device(): grad_gain = jnp.sum(dxn * tokens * r1, 0)]
    unnamed x35 -> x0, local copies, waits for them, and re-layouts: 7.75 us -> none
  transfers between devices with their start and end apart: 3 -> 0, of which waited for: 1 -> 0; matrix products, arithmetic and copies ran while one was open for 9% -> 0% of each run, Pallas kernels for 27% -> 0%
where the time goes in v2:
time: 389 us; the launch traced here: 388 us
  Pallas kernels  387 us (99%)
    pallas_call x1, Pallas kernels, on_device(): pl.pallas_call(functools.partial(backward_kernel, heads, count, pairs, n_...  150 us
    pallas_call x1, Pallas kernels, on_device(): pl.pallas_call(functools.partial(line_kernel, count, pairs, n_fwd + n_bwd...  114 us
    pallas_call x1, Pallas kernels, on_device(): pl.pallas_call(functools.partial(forward_kernel, heads, count, pairs, n_f...  102 us
    pallas_call x1, Pallas kernels, on_device(): pl.pallas_call(functools.partial(finish_kernel, heads, count), grid=(bloc...  21.3 us

profile of v2, /device:TPU:0, one launch (start us, length us, event | category | flops | bytes accessed | tf_op | source)
XLA Modules:
  0.0 388.1 jit_solution(18354025441496394335)
XLA Ops:
  0.6 101.9 %forward_scan.1 = (f32[2048,768]{1,0:T(8,128)}, f32[2048,768]{1,0:T(8,128)}, bf16[2048,768]{1,0:T(8,128)(2,1)}, f32[2048,768]{1,0:T(8,128)}, f32[2048,256]{1,0:T...) custom-call(bf16[2048,1536]{1,0:T(8,128)(2,1)} %bitcast.16, ...), custom_call_target="tpu_custom_call" | custom-call | flops 89999998976 | bytes 100000000 | tf_op jit(solution)/shard_map/forward_scan/pallas_call | solution.py:1030
  102.5 149.9 %backward_scan.1 = (bf16[8,4,64,1536]{3,2,1,0:T(8,128)(2,1)}, bf16[1536,768]{1,0:T(8,128)(2,1)}, bf16[1536,768]{1,0:T(8,128)(2,1)}, bf16[1536,256]{1,0:T(8,128)(...) custom-call(f32[2048,768]{1,0:T(8,128)} %get-tuple-element.62.z_ref,, ...), custom_call_target="tpu_custom_call", output_to_operand_aliasing={{7}: (29, {}), {8}: (30, {})} | custom-call | flops 120000004096 | bytes 100000000 | tf_op jit(solution)/shard_map/backward_scan/pallas_call | solution.py:1100
  252.4 114.2 %line_sums.1 = (bf16[8,4,64,1536]{3,2,1,0:T(8,128)(2,1)}, bf16[8,4,64,1536]{3,2,1,0:T(8,128)(2,1)}, bf16[1536,768]{1,0:T(8,128)(2,1)}, bf16[1536,768]{1,0:T(8,12...) custom-call(bf16[8,4,64,1536]{3,2,1,0:T(8,128)(2,1)} %get-tuple-element.77, ...), custom_call_target="tpu_custom_call", output_to_operand_aliasing={{0}: (9, {}), {1}: (10, {})} | custom-call | flops 99999997952 | bytes 300000000 | tf_op jit(solution)/shard_map/line_sums/pallas_call | solution.py:1171
  366.6 21.3 %finish.1 = (bf16[2048,1536]{1,0:T(8,128)(2,1)}, bf16[2048,1536]{1,0:T(8,128)(2,1)}, f32[1536,768]{1,0:T(8,128)}, f32[1536,768]{1,0:T(8,128)}, f32[768,1536]{1,0...) custom-call(bf16[2048,1536]{1,0:T(8,128)(2,1)} %bitcast.20, ...), custom_call_target="tpu_custom_call" | custom-call | tf_op jit(solution)/shard_map/finish/pallas_call | solution.py:1204

commit v3 on v2

--- a/solution.py
+++ b/solution.py
@@ -12,6 +12,9 @@
 BLOCK = 256
 PIECES = BLOCK // CHUNK
 LANES = 128
+ROWS = CHUNK // 2
+LAG = 2
+RING = 4
 F32 = jnp.float32
 BF16 = jnp.bfloat16
 HIGHEST = lax.Precision.HIGHEST
@@ -47,15 +50,15 @@
     )
 
 
-def spread(columns, heads):
-    rows = columns.shape[0]
-    low = lax.broadcasted_iota(jnp.int32, (rows, LANES), 1) < LANES // 2
-    pieces = []
-    for pair in range(heads // 2):
-        first = columns[:, 2 * pair : 2 * pair + 1]
-        second = columns[:, 2 * pair + 1 : 2 * pair + 2]
-        pieces.append(jnp.where(low, first, second))
-    return jnp.concatenate(pieces, axis=1)
+def fill_expand(expand, heads):
+    r, c = iotas(*expand.shape)
+    expand[...] = (lax.rem(r, LANES) == c // (expand.shape[1] // heads)).astype(BF16)
+
+
+def spread(columns, expand):
+    high = columns.astype(BF16)
+    low = (columns - high.astype(F32)).astype(BF16)
+    return dot(jnp.concatenate([high, low], axis=1), expand[...])
 
 
 def decays(la, seg_col, seg_row):
@@ -115,9 +118,8 @@
     copy.wait()
 
 
-def greet(peers, dp_peers=()):
+def hello(peers, dp_peers=()):
     barrier = pltpu.get_barrier_semaphore()
-    total = jnp.int32(len(dp_peers))
     for peer in dp_peers:
         pl.semaphore_signal(barrier, inc=1, device_id={"dp": peer}, device_id_type=MESH)
     for peer, there in peers:
@@ -126,8 +128,12 @@
         def _():
             pl.semaphore_signal(barrier, inc=1, device_id={"tensor": peer}, device_id_type=MESH)
 
+
+def heard(peers, dp_peers=()):
+    total = jnp.int32(len(dp_peers))
+    for _, there in peers:
         total = total + there.astype(jnp.int32)
-    pl.semaphore_wait(barrier, total)
+    pl.semaphore_wait(pltpu.get_barrier_semaphore(), total)
 
 
 def neighbours(count):
@@ -155,7 +161,7 @@
 
     def flow(self, q):
         me = lax.axis_index("tensor")
-        if q % 2 == 0:
+        if q == 0:
             return me, me - 1, me + 1
         return self.count - 1 - me, me + 1, me - 1
 
@@ -164,7 +170,7 @@
 
     def red(self, q, ls, toward, src):
         return pltpu.make_async_remote_copy(
-            src_ref=src, dst_ref=self.land.at[ls + 1, q], send_sem=self.red_out.at[q, ls],
+            src_ref=src, dst_ref=self.land.at[ls + LAG, q], send_sem=self.red_out.at[q, ls],
             recv_sem=self.red_in.at[q, ls], device_id={"tensor": toward}, device_id_type=MESH,
         )
 
@@ -174,54 +180,78 @@
             recv_sem=self.bc_in.at[q, ls], device_id={"tensor": away}, device_id_type=MESH,
         )
 
-    def keep(self, q, there):
-        return pltpu.make_async_copy(self.send.at[q], there, self.local.at[q])
+    def hold(self, q, ls):
+        return self.send.at[lax.rem(ls, LAG), q]
+
+    def keep(self, q, ls, there):
+        return pltpu.make_async_copy(self.hold(q, ls), there, self.local.at[lax.rem(ls, LAG), q])
+
+    def term(self, s, z):
+        return s - LAG * (self.count - 1 - z)
+
+    def back(self, s, z):
+        return s - LAG * (self.count - 1 + z)
 
     def finish_red(self, q, s, ls):
         z, toward, away = self.flow(q)
         n = self.count
-        i = s - (n - 1) + z
+        i = self.term(s, z)
 
         @pl.when(self.is_pair(i) & (z > 0))
         def _():
-            self.red(q, ls, toward, self.send.at[q]).wait_send()
+            self.red(q, ls, toward, self.hold(q, ls)).wait_send()
 
         @pl.when(self.is_pair(i) & (z == 0))
         def _():
-            self.cast(q, ls, away, self.send.at[q], self.res_y.at[0, q]).wait_send()
-            self.keep(q, self.res_y.at[0, q]).wait()
-
-        @pl.when(self.is_pair(i + 1) & (z < n - 1))
+            self.cast(q, ls, away, self.hold(q, ls), self.res_y.at[0, q]).wait_send()
+            self.keep(q, ls, self.res_y.at[0, q]).wait()
+
+        @pl.when(self.is_pair(i + LAG) & (z < n - 1))
         def _():
-            self.red(q, ls, toward, self.send.at[q]).wait_recv()
+            self.red(q, ls, toward, self.hold(q, ls)).wait_recv()
 
     def finish_cast(self, q, s, ls):
         z, _, away = self.flow(q)
         n = self.count
-        k = s - (n - 1) - z
+        k = self.back(s, z)
 
         @pl.when(self.is_pair(k) & (z > 0) & (z < n - 1))
         def _():
             self.cast(q, ls, away, self.res_y.at[0, q], self.res_y.at[0, q]).wait_send()
 
-        @pl.when(self.is_pair(k + 1) & (z > 0))
+        @pl.when(self.is_pair(k + LAG) & (z > 0))
         def _():
             self.cast(q, ls, away, self.res_y.at[0, q], self.res_y.at[0, q]).wait_recv()
 
-    def step(self, ls, h):
+    def step(self, ls):
         n = self.count
+        ls = jnp.int32(ls)
         s = self.first + ls
-        for q in (2 * h, 2 * h + 1):
+        for q in range(2):
+
+            @pl.when(ls >= LAG)
+            def _():
+                self.finish_cast(q, s - LAG, ls - LAG)
+
             z, toward, away = self.flow(q)
-            i = s - (n - 1) + z
-
-            @pl.when(ls > 0)
+            k = self.back(s, z)
+
+            @pl.when(self.is_pair(k) & (z > 0) & (z < n - 1))
             def _():
-                self.finish_red(q, s - 1, ls - 1)
+                self.to_result(k, q, lambda there: self.cast(q, ls, away, there, there).start())
+
+        for q in range(2):
+            z, toward, away = self.flow(q)
+            i = self.term(s, z)
+
+            @pl.when(ls >= LAG)
+            def _():
+                self.finish_red(q, s - LAG, ls - LAG)
 
             @pl.when(self.is_pair(i))
             def _():
                 mine = self.source(q, i)
+                place = lax.rem(ls, LAG)
 
                 @pl.when(z == n - 1)
                 def _():
@@ -229,20 +259,20 @@
 
                 @pl.when((z > 0) & (z < n - 1))
                 def _():
-                    self.send[q] = (mine[...].astype(F32) + self.land[ls, q].astype(F32)).astype(BF16)
-                    self.red(q, ls, toward, self.send.at[q]).start()
+                    self.send[place, q] = (mine[...].astype(F32) + self.land[ls, q].astype(F32)).astype(BF16)
+                    self.red(q, ls, toward, self.hold(q, ls)).start()
 
                 @pl.when(z == 0)
                 def _():
                     total = mine[...].astype(F32) + self.land[ls, q].astype(F32)
                     if self.finals is None:
-                        self.send[q] = total.astype(BF16)
+                        self.send[place, q] = total.astype(BF16)
                     else:
-                        self.finals.last(q, i, total, self.send)
+                        self.finals.last(q, i, total, self.hold(q, ls))
 
                     def give(there):
-                        self.cast(q, ls, away, self.send.at[q], there).start()
-                        self.keep(q, there).start()
+                        self.cast(q, ls, away, self.hold(q, ls), there).start()
+                        self.keep(q, ls, there).start()
 
                     self.to_result(i, q, give)
                     if self.finals is not None:
@@ -251,59 +281,52 @@
                         def _():
                             self.finals.fetch(q, i + 1)
 
-        for q in (2 * h, 2 * h + 1):
-
-            @pl.when(ls > 0)
-            def _():
-                self.finish_cast(q, s - 1, ls - 1)
-
-            z, toward, away = self.flow(q)
-            k = s - (n - 1) - z
-
-            @pl.when(self.is_pair(k) & (z > 0) & (z < n - 1))
-            def _():
-                self.to_result(k, q, lambda there: self.cast(q, ls, away, there, there).start())
-
     def held(self, q, s):
         z, _, _ = self.flow(q)
-        return self.is_pair(s - (self.count - 1) + z) & (z < self.count - 1)
+        return self.is_pair(self.term(s, z)) & (z < self.count - 1)
+
+    def each_held(self, s, src, act):
+        for q in range(2):
+            for d in range(LAG):
+
+                @pl.when(self.held(q, s + d))
+                def _():
+                    act(pltpu.make_async_copy(*src(d, q), self.local.at[d, q]))
 
     def open(self, carry):
-        for q in range(4):
-
-            @pl.when(self.held(q, self.first))
-            def _():
-                bring(carry.at[q], self.land.at[0, q], self.local.at[q])
-
+        self.each_held(self.first, lambda d, q: (carry.at[d, q], self.land.at[d, q]), lambda copy: copy.start())
+        for q in range(2):
             z, _, _ = self.flow(q)
 
             @pl.when(z == 0)
             def _():
-                self.finals.fetch(q, jnp.int32(self.first - (self.count - 1)))
+                self.finals.fetch(q, jnp.int32(self.first - LAG * (self.count - 1)))
+
+    def opened(self, carry):
+        self.each_held(self.first, lambda d, q: (carry.at[d, q], self.land.at[d, q]), lambda copy: copy.wait())
 
     def close(self, carry):
-        ls = self.steps - 1
-        s = self.first + ls
-        for q in range(4):
-            self.finish_red(q, s, ls)
-            self.finish_cast(q, s, ls)
-            if carry is None:
-                continue
-
-            @pl.when(self.held(q, s + 1))
-            def _():
-                bring(self.land.at[ls + 1, q], carry.at[q], self.local.at[q])
+        for d in range(LAG):
+            ls = self.steps - LAG + d
+            for q in range(2):
+                self.finish_cast(q, self.first + ls, jnp.int32(ls))
+                self.finish_red(q, self.first + ls, jnp.int32(ls))
+        if carry is None:
+            return
+        left = (self.first + self.steps, lambda d, q: (self.land.at[self.steps + d, q], carry.at[d, q]))
+        self.each_held(*left, lambda copy: copy.start())
+        self.each_held(*left, lambda copy: copy.wait())
 
 
 def line_scratch(steps, width):
     return [
-        pltpu.VMEM((steps + 1, 4, BLOCK // 4, width), BF16),
-        pltpu.VMEM((4, BLOCK // 4, width), BF16),
-        pltpu.SemaphoreType.DMA((4, steps)),
-        pltpu.SemaphoreType.DMA((4, steps)),
-        pltpu.SemaphoreType.DMA((4, steps)),
-        pltpu.SemaphoreType.DMA((4, steps)),
-        pltpu.SemaphoreType.DMA((4,)),
+        pltpu.VMEM((steps + LAG, 2, ROWS, width), BF16),
+        pltpu.VMEM((LAG, 2, ROWS, width), BF16),
+        pltpu.SemaphoreType.DMA((2, steps)),
+        pltpu.SemaphoreType.DMA((2, steps)),
+        pltpu.SemaphoreType.DMA((2, steps)),
+        pltpu.SemaphoreType.DMA((2, steps)),
+        pltpu.SemaphoreType.DMA((LAG, 2)),
     ]
 
 
@@ -329,7 +352,7 @@
     def last(self, q, i, total, out):
         @pl.when(i < self.half)
         def _():
-            out[q] = total.astype(BF16)
+            out[...] = total.astype(BF16)
 
         @pl.when(i >= self.half)
         def _():
@@ -339,11 +362,11 @@
             r1 = inverse_rms(x)
             scaled = total * self.gain
             across = jnp.sum(scaled * x, axis=1, keepdims=True) * (1.0 / x.shape[1])
-            out[q] = (self.rows[q, 1].astype(F32) + r1 * scaled - x * (r1 * r1 * r1 * across)).astype(BF16)
+            out[...] = (self.rows[q, 1].astype(F32) + r1 * scaled - x * (r1 * r1 * r1 * across)).astype(BF16)
 
 
 def finals_scratch(width):
-    return [pltpu.VMEM((4, 2, BLOCK // 4, width), BF16), pltpu.SemaphoreType.DMA((4, 2))]
+    return [pltpu.VMEM((2, 2, ROWS, width), BF16), pltpu.SemaphoreType.DMA((2, 2))]
 
 
 def dp_bits():
@@ -374,6 +397,10 @@
 
     def inside(self, depth):
         return self.start_of(depth) - self.start_of(1)
+
+    def own_half(self):
+        mine = self.src.at[self.span(self.start_of(1), self.rows // 2), :]
+        return pltpu.make_async_copy(mine, self.send.at[pl.ds(0, self.rows // 2), :], self.local)
 
     def halving(self, j):
         size = self.rows >> (j + 1)
@@ -396,26 +423,27 @@
         )
 
     def crossing(self, d):
-        land, out_sem, in_sem, peers = self.across
+        mine, land, out_sem, in_sem, peers = self.across
         return pltpu.make_async_remote_copy(
-            src_ref=self.send.at[pl.ds(0, land.shape[1]), :], dst_ref=land.at[d - 1], send_sem=out_sem.at[d - 1],
+            src_ref=mine, dst_ref=land.at[d - 1], send_sem=out_sem.at[d - 1],
             recv_sem=in_sem.at[d - 1], device_id={"tensor": peers[d - 1]}, device_id_type=MESH,
         )
 
-    def turn(self):
+    def turn(self, part):
         count = len(self.order)
         size = self.rows >> count
-        bring(self.send.at[pl.ds(0, size), :], self.out.at[self.span(self.start_of(count), size), :], self.local)
+        bring(part, self.out.at[self.span(self.start_of(count), size), :], self.local)
         self.doubling(0).start()
 
     def event(self, e):
         count = len(self.order)
         if e == 0:
             self.halving(0).start()
-            mine = self.src.at[self.span(self.start_of(1), self.rows // 2), :]
-            bring(mine, self.send.at[pl.ds(0, self.rows // 2), :], self.local)
+            self.own_half().start()
             return
         if e <= count:
+            if e == 1:
+                self.own_half().wait()
             self.halving(e - 1).wait()
             size = self.rows >> e
             at = self.inside(e)
@@ -431,24 +459,27 @@
                 bit, _ = self.bits[self.order[e]]
                 at = at + (1 - bit) * (size // 2)
                 size = size // 2
-            self.send[0:size, :] = self.total[self.span(at, size), :].astype(self.send.dtype)
+            part = self.total[self.span(at, size), :]
+            if e == count and self.across is not None:
+                self.across[0][...] = part.astype(self.across[0].dtype)
+                for d in range(1, len(self.across[4]) + 1):
+                    self.crossing(d).start()
+                return
+            self.send[0:size, :] = part.astype(self.send.dtype)
             if e < count:
                 self.halving(e).start()
-            elif self.across is None:
-                self.turn()
             else:
-                for d in range(1, len(self.across[3]) + 1):
-                    self.crossing(d).start()
+                self.turn(self.send.at[pl.ds(0, size), :])
             return
         if self.across is not None:
             if e == count + 1:
                 size = self.rows >> count
                 total = self.total[self.span(self.inside(count), size), :]
-                for d in range(1, len(self.across[3]) + 1):
+                for d in range(1, len(self.across[4]) + 1):
                     self.crossing(d).wait()
-                    total = total + self.across[0][d - 1].astype(F32)
-                self.send[0:size, :] = total.astype(self.send.dtype)
-                self.turn()
+                    total = total + self.across[1][d - 1].astype(F32)
+                self.across[0][...] = total.astype(self.across[0].dtype)
+                self.turn(self.across[0])
                 return
             e = e - 1
         self.doubling(e - count - 1).wait()
@@ -469,6 +500,7 @@
 
 def cross_scratch(count, rows, cols, dtype):
     return [
+        pltpu.VMEM((rows, cols), dtype),
         pltpu.VMEM((count - 1, rows, cols), dtype),
         pltpu.SemaphoreType.DMA((count - 1,)),
         pltpu.SemaphoreType.DMA((count - 1,)),
@@ -481,8 +513,8 @@
 
 
 def line_kernel(
-    count, pairs, first, steps, xp_ref, x_any, g_any, ng_ref, carry_ref, gz_ref, gx_ref, gb_ref, pk_ref, res_y_in, res_x_in,
-    res_y, res_x, oz_ref, ox_ref, ob_ref, op_ref, part, part_sem, rows, sems, *scratch,
+    count, pairs, first, steps, xp_ref, x_any, g_any, ng_ref, carry_ref, gz_ref, gx_ref, gb_ref, pk_ref, sh_ref, res_y_in, res_x_in,
+    res_y, res_x, oz_ref, ox_ref, ob_ref, op_ref, os_ref, part, part_sem, rows, sems, *scratch,
 ):
     del res_y_in, res_x_in
     half = pairs // 2
@@ -492,39 +524,39 @@
     cubes = [
         Cube(order, (gz_ref, oz_ref, *scratch[0:6])),
         Cube(other, (gx_ref, ox_ref, *scratch[6:12])),
-        Cube(other, (gb_ref, ob_ref, *scratch[12:18]), (*scratch[24:27], peers)),
-        Cube(order, (pk_ref, op_ref, *scratch[18:24]), (*scratch[27:30], peers)),
+        Cube(other, (gb_ref, ob_ref, *scratch[12:18]), (*scratch[30:34], peers)),
+        Cube(order, (pk_ref, op_ref, *scratch[18:24])),
+        Cube(order, (sh_ref, os_ref, *scratch[24:30]), (*scratch[34:38], peers)),
     ]
     finals = Finals(pairs, x_any, g_any, row_of(ng_ref), rows, sems)
     line = Line(
-        count, pairs, first, steps, (res_y, res_x, *scratch[30:]), lambda q, i: part.at[2 * half - 1 - i, q], finals
+        count, pairs, first, steps, (res_y, res_x, *scratch[38:]), lambda q, i: part.at[2 * half - 1 - i, q], finals
     )
     at = pl.program_id(0)
 
     @pl.when(at == 0)
     def _():
         terms = pltpu.make_async_copy(xp_ref.at[pl.ds(0, part.shape[0])], part, part_sem)
+        everyone = [(peer, peer >= 0) for peer in peers], [partner for _, partner in dp_bits()]
+        hello(*everyone)
         terms.start()
-        greet([(peer, peer >= 0) for peer in peers], [partner for _, partner in dp_bits()])
         line.open(carry_ref)
+        line.opened(carry_ref)
         terms.wait()
-
-    turn = len(order)
-    last = 2 * steps - 1
-    plain = [0, 1] + [2 * e - 1 for e in range(2, turn)] + [2 * turn - 2, 2 * turn - 1]
-    plain += [2 * (turn + j) - 1 for j in range(1, turn - 1)] + [4 * turn - 4]
-    crossed = plain[: turn + 1] + [2 * turn - 1, 2 * turn + 1] + plain[turn + 3 :] + [4 * turn - 3]
-    times = [plain, plain, crossed, crossed]
-    for h in range(2):
-        line.step(at, h)
-        for cube, when in zip(cubes, times):
-            for e, t in enumerate(when):
-                t = min(t, last)
-                if t % 2 == h:
-
-                    @pl.when(at == t // 2)
-                    def _():
-                        cube.event(e)
+        heard(*everyone)
+
+    if len(order) == 3:
+        times = [0, 1, 4, 5, 6, 9, 10], [0, 1, 4, 5, 6, 9, 10], [0, 1, 4, 6, 8, 10, 11, 11]
+    else:
+        times = (range(2 * len(order) + 2),) * 3
+    for cube, when in zip(cubes, (*times, times[0], times[2])):
+        for e in range(cube.events):
+
+            @pl.when(at == min(when[e], steps - 1))
+            def _():
+                cube.event(e)
+
+    line.step(at)
 
     @pl.when(at == steps - 1)
     def _():
@@ -532,14 +564,13 @@
 
 
 def finish_kernel(
-    heads, count, x_ref, y_ref, dx_ref, scal_ref, gz_ref, gx_ref, go_ref, go2_ref, gb_ref, pack_ref,
+    heads, x_ref, y_ref, dx_ref, scal_ref, gz_ref, gx_ref, go_ref, go2_ref, gb_ref, pack_ref, shared_ref,
     yo_ref, xo_ref, oz_ref, ox_ref, oo_ref, wbc_ref, wdt_ref, ng_ref, cx_ref, bx_ref, og_ref, ds_ref, cbc_ref, bbc_ref,
     dtb_ref, al_ref,
 ):
     inner = cx_ref.shape[1]
     width, bcw = x_ref.shape[1], wbc_ref.shape[1]
-    me = lax.axis_index("tensor")
-    for piece in range(PIECES):
+    for piece in range(x_ref.shape[0] // CHUNK):
         span = slice(piece * CHUNK, (piece + 1) * CHUNK)
         r2 = jnp.concatenate([scal_ref[piece], jnp.zeros((CHUNK - 8, CHUNK), F32)], axis=0).T[:, 0:1]
         yo_ref[span, :] = (x_ref[span, :].astype(F32) + r2 * y_ref[span, :].astype(F32)).astype(BF16)
@@ -552,22 +583,20 @@
 
     @pl.when(pl.program_id(0) == 0)
     def _():
-        at = 0
-        base = pl.multiple_of(at + me * dt_rows(width), 8)
         for j in range(width // LANES):
-            wdt_ref[:, j * LANES : (j + 1) * LANES] = pack_ref[pl.ds(base + 16 * j, 16), :][0:heads, :]
-        at += count * dt_rows(width)
+            wdt_ref[:, j * LANES : (j + 1) * LANES] = pack_ref[16 * j : 16 * j + 16, :][0:heads, :]
+
         def put(ref, row):
             ref[...] = row.reshape(ref.shape)
 
-        put(ng_ref, jnp.concatenate([pack_ref[at + 8 * j : at + 8 * j + 1, :] for j in range(width // LANES)], axis=1))
-        at += width // LANES * 8
-        rows = jnp.concatenate([pack_ref[at + 8 * j : at + 8 * j + 8, :] for j in range(bcw // LANES)], axis=1)
+        def side_by_side(ref, at, pieces, rows=8):
+            return jnp.concatenate([ref[at + 8 * j : at + 8 * j + rows, :] for j in range(pieces)], axis=1)
+
+        put(ng_ref, side_by_side(shared_ref, 0, width // LANES, 1))
+        rows = side_by_side(shared_ref, width // LANES * 8, bcw // LANES)
         cbc_ref[...] = rows[0:4, :]
         put(bbc_ref, rows[4:5, :])
-        at += bcw // LANES * 8
-        base = pl.multiple_of(at + me * slot_rows(inner), 8)
-        rows = jnp.concatenate([pack_ref[pl.ds(base + 8 * j, 8), :] for j in range(inner // LANES)], axis=1)
+        rows = side_by_side(pack_ref, dt_rows(width), inner // LANES)
         cx_ref[...] = rows[0:4, :]
         put(bx_ref, rows[4:5, :])
         put(og_ref, rows[6:7, :])
@@ -577,18 +606,19 @@
             head = jnp.sum(rows[5:6, h * 64 : h * 64 + 64], axis=1, keepdims=True)
             skip = jnp.where(lane == h, head, skip)
         ds_ref[...] = skip
-        rows = pack_ref[pl.ds(base + inner // LANES * 8, 8), :]
+        at = dt_rows(width) + inner // LANES * 8
+        rows = pack_ref[at : at + 8, :]
         dtb_ref[...] = rows[0:1, 0:heads]
         al_ref[...] = rows[1:2, 0:heads]
 
 
 def forward_kernel(
     heads, count, pairs, steps, blocks,
-    x_ref, g_ref, segr_ref, wz_ref, wx_ref, wbc_ref, wdt_ref, wo_ref, ng_ref, bx_ref, og_ref, bbc_ref, cx_ref, cbc_ref,
+    x_ref, g_ref, segr_ref, wz_ref, wx_ref, wbc_ref, wdt_ref, wo_any, ng_ref, bx_ref, og_ref, bbc_ref, cx_ref, cbc_ref,
     dtb_ref, al_ref, dsk_ref,
     z_ref, p_ref, xc_ref, ys_ref, pbc_ref, bc_ref, dtr_ref, dn_ref, st_ref, yp_ref, scal_ref, wout_ref,
     carry_out, res_y, res_x,
-    hv_ref, wdt_s, hist, hist_bc, segs, state, scaled_s, g_s, acc_out, stat_mine, stat_land, stat_out, stat_in, part, *scratch,
+    wo_ref, w_sem, hv_ref, wdt_s, expand, hist, hist_bc, segs, state, scaled_s, g_s, acc_out, stat_mine, stat_land, stat_out, stat_in, part, *scratch,
 ):
     rows, width = x_ref.shape
     inner = z_ref.shape[1]
@@ -598,10 +628,15 @@
 
     line = Line(count, pairs, 0, steps, (res_y, res_x, *scratch), lambda q, i: part.at[i, q])
 
+    load = pltpu.make_async_copy(wo_any, wo_ref, w_sem)
+    everyone = [(peer, peer >= 0) for peer in tensor_peers(count)]
+
     @pl.when(block == 0)
     def _():
-        greet([(lax.rem(me + d, count), me >= 0) for d in range(1, count)])
+        hello(everyone)
+        load.start()
         fill_heads(hv_ref, wdt_s, dtb_ref, al_ref, dsk_ref, wdt_ref)
+        fill_expand(expand, heads)
         hist[0:8, :] = jnp.zeros((8, hist.shape[1]), F32)
         hist_bc[0:8, :] = jnp.zeros((8, hist_bc.shape[1]), F32)
         segs[0:8, :] = jnp.full((8, 1), -1.0, F32)
@@ -625,12 +660,12 @@
     p_ref[...] = conv_taps(hist, cx_ref, same, rows) + bx
     pbc_ref[...] = conv_taps(hist_bc, cbc_ref, same, rows) + bbc
     g = g_ref[...]
-    g_s[lax.rem(block, 2)] = g
-    dn_ref[...] = dot_t(g, wo_ref[...])
+    g_s[lax.rem(block, RING)] = g
     dt_all = softplus(dtr + hv_ref[0:1, :])
     la_all = -jnp.exp(hv_ref[1:2, :]) * dt_all
-    dsk = spread(hv_ref[2:3, :], heads)
+    dsk = spread(hv_ref[...], expand)[2:3, :]
     row_i, lane_i = iotas(CHUNK, LANES)
+    squares = []
     for piece in range(PIECES):
         at = pl.ds(piece * CHUNK, CHUNK)
         span = slice(piece * CHUNK, (piece + 1) * CHUNK)
@@ -646,7 +681,13 @@
         n = bcu.shape[1] // 2
         b, c = bcu[:, :n], bcu[:, n:]
         scores = dot_t(c, b)
-        v = spread(dt, heads) * u
+        last = cum[CHUNK - 1 : CHUNK, :]
+        flows = [dt, jnp.exp(cum) * keep, jnp.exp(last - cum) * tail]
+        flows.append(jnp.broadcast_to(jnp.exp(last) * keep[CHUNK - 1 : CHUNK, :], (8, LANES)))
+        wide = spread(jnp.concatenate(flows, axis=0), expand)
+        dt_x, enter_x, end_x = (wide[k * CHUNK : (k + 1) * CHUNK, :] for k in range(3))
+        carry = wide[3 * CHUNK : 3 * CHUNK + 1, :]
+        v = dt_x * u
         v_low = v.astype(BF16)
         pieces = []
         for pair in range(heads // 2):
@@ -660,45 +701,47 @@
         old = state[...]
         old_low = old.astype(BF16)
         st_ref[piece] = old_low
-        entering = dot(c, old_low) * spread(jnp.exp(cum) * keep, heads)
-        last = cum[CHUNK - 1 : CHUNK, :]
-        to_end = spread(jnp.exp(last - cum) * tail, heads)
-        carry = spread(jnp.exp(last) * keep[CHUNK - 1 : CHUNK, :], heads)
-        state[...] = old * carry + tdot(b, (to_end * v).astype(BF16))
+        entering = dot(c, old_low) * enter_x
+        state[...] = old * carry + tdot(b, (end_x * v).astype(BF16))
         ys = inside + entering + dsk * u
         ys_ref[at, :] = ys
         z = z_ref[at, :]
         gated = ys * (z * sigmoid(z))
         scaled = gated * og
-        scaled_s[lax.rem(block, 2), at, :] = scaled
+        scaled_s[lax.rem(block, RING), at, :] = scaled
+        if piece == 0:
+
+            @pl.when(block == 0)
+            def _():
+                heard(everyone)
+                load.wait()
+
         y_part = dot(scaled.astype(BF16), wo_ref[...]).astype(BF16)
         for q in range(2):
-            yp_ref[0, 2 * piece + q] = y_part[q * 64 : q * 64 + 64, :]
-
-        @pl.when(block < part.shape[0])
+            yp_ref[piece, q] = y_part[q * ROWS : q * ROWS + ROWS, :]
+
+        @pl.when(block * PIECES + piece < part.shape[0])
         def _():
             for q in range(2):
-                part[jnp.minimum(block, part.shape[0] - 1), 2 * piece + q] = y_part[q * 64 : q * 64 + 64, :]
+                at_pair = jnp.minimum(block * PIECES + piece, part.shape[0] - 1)
+                part[at_pair, q] = y_part[q * ROWS : q * ROWS + ROWS, :]
 
         if piece == 0:
-
-            @pl.when((block >= 4) & (lax.rem(block, 2) == 0))
+            line.step(jnp.where(block < 4, 2 * block, block + 3))
+        else:
+
+            @pl.when((block < 3) | (block == blocks - 1))
             def _():
-                line.step(block // 2 + 1, 1)
-
-            @pl.when((block < 4) | (lax.rem(block, 2) == 1))
-            def _():
-                line.step(jnp.where(block < 4, block, (block + 3) // 2), 0)
-
-        else:
-
-            @pl.when(block < 3)
-            def _():
-                line.step(block, 1)
-
-        sums = jnp.sum(gated * gated, axis=1, keepdims=True)
-        across = jnp.sum(dn_ref[at, :] * scaled, axis=1, keepdims=True)
-        both = jnp.where(lane_i == 0, sums, jnp.where(lane_i == 1, across, 0.0))
+                line.step(jnp.where(block < 3, 2 * block + 1, steps - 1))
+
+        squares.append(jnp.sum(gated * gated, axis=1, keepdims=True))
+
+    dn = dot_t(g, wo_ref[...])
+    dn_ref[...] = dn
+    for piece in range(PIECES):
+        span = slice(piece * CHUNK, (piece + 1) * CHUNK)
+        across = jnp.sum(dn[span, :] * scaled_s[lax.rem(block, RING), span, :], axis=1, keepdims=True)
+        both = jnp.where(lane_i == 0, squares[piece], jnp.where(lane_i == 1, across, 0.0))
         stat_mine[block, piece] = both.T[0:8, :]
     hist[0:8, :] = hist[rows : rows + 8, :]
     hist_bc[0:8, :] = hist_bc[rows : rows + 8, :]
@@ -715,7 +758,7 @@
         for d in range(1, count):
             stat_copy(d, b).wait()
             total = total + stat_land[d - 1, b]
-        place = lax.rem(b, 2)
+        place = lax.rem(b, RING)
         low = []
         for piece in range(PIECES):
             r2 = lax.rsqrt(total[piece, 0:1, :] * (1.0 / (inner * count)) + EPS)
@@ -731,34 +774,34 @@
     for d in range(1, count):
         stat_copy(d, block).start()
 
-    @pl.when(block > 0)
+    @pl.when(block >= RING - 1)
     def _():
-        settle(block - 1)
+        settle(block - (RING - 1))
 
     @pl.when(block == blocks - 1)
     def _():
-        settle(block)
+        for b in range(1, RING):
+            settle(blocks - RING + b)
         for c in range(0, inner, 256):
             low = acc_out[c : c + 256, :].astype(BF16)
             wout_ref[c : c + 256, :] = low[:, 0 : width // 2]
             wout_ref[inner + c : inner + c + 256, :] = low[:, width // 2 :]
-        line.step(jnp.int32(steps - 1), 1)
         line.close(carry_out)
 
 
 def backward_kernel(
     heads, count, pairs, first, steps,
     z_ref, p_ref, xc_ref, ys_ref, pbc_ref, bc_ref, dtr_ref, dn_ref, st_ref, segp_ref, segr_ref, scal_ref, x_ref,
-    wz_ref, wx_ref, wbc_ref, wdt_ref, ng_ref, og_ref, cx_ref, cbc_ref, dtb_ref, al_ref, dsk_ref, y_ref, x_any, g_any, carry_ref, go_ref, res_y_in, res_x_in,
-    xp_ref, gz_ref, gx_ref, gb_ref, pack_ref, carry_out, go_sum, res_y, res_x,
-    hv_ref, wdt_s, ahead, ahead_bc, segs, d_state, dz_s, dx_s, ddt_s, dbc_s, acc_z, acc_x, acc_bc, acc_dt,
-    a1536, a768, a256, a128, rest, low_bc, stage, stage_sem, part, part_sem, rows_s, rows_sem, *scratch,
+    wz_any, wx_any, wbc_any, wdt_ref, ng_ref, og_ref, cx_ref, cbc_ref, dtb_ref, al_ref, dsk_ref, y_ref, x_any, g_any, carry_ref, go_ref, res_y_in, res_x_in,
+    xp_ref, gz_ref, gx_ref, gb_ref, pack_ref, shared_ref, carry_out, go_sum, res_y, res_x,
+    wz_ref, wx_ref, wbc_ref, w_sem, hv_ref, wdt_s, expand, ahead, ahead_bc, segs, d_state, dz_s, dx_s, ddt_s, dbc_s, acc_z, acc_x, acc_bc, acc_dt,
+    a1536, a768, a256, a128, rest, shared, stage, stage_sem, part, part_sem, rows_s, rows_sem, *scratch,
 ):
     del res_y_in, res_x_in
     rows, inner = z_ref.shape
     width = x_ref.shape[1]
     block = pl.program_id(0)
-    blocks = steps
+    blocks = steps // PIECES - 1
     half = pairs // 2
     me = lax.axis_index("tensor")
     ng, og = row_of(ng_ref), row_of(og_ref)
@@ -767,35 +810,47 @@
     line = Line(
         count, pairs, first, steps, (res_y, res_x, *scratch[6:]), lambda q, i: part.at[lax.rem(i, half), q], finals
     )
+    loads = [
+        pltpu.make_async_copy(src, dst, w_sem.at[j])
+        for j, (src, dst) in enumerate(((wz_any, wz_ref), (wx_any, wx_ref), (wbc_any, wbc_ref)))
+    ]
     cube = Cube(list(range(len(dp_bits()))), (go_ref, go_sum, *scratch[0:6]))
-    old = first - (count - 1)
+    old = first - LAG * (count - 1)
 
     @pl.when(block == 0)
     def _():
         terms = pltpu.make_async_copy(y_ref.at[pl.ds(old, half - old)], part.at[pl.ds(old, half - old)], part_sem)
+        everyone = neighbours(count), [partner for _, partner in dp_bits()]
+        hello(*everyone)
         terms.start()
-        greet(neighbours(count), [partner for _, partner in dp_bits()])
         line.open(carry_ref)
+        for load in loads:
+            load.start()
+        line.opened(carry_ref)
         terms.wait()
+        heard(*everyone)
+        line.step(0)
         fill_heads(hv_ref, wdt_s, dtb_ref, al_ref, dsk_ref, wdt_ref)
+        fill_expand(expand, heads)
         ahead[rows : rows + 8, :] = jnp.zeros((8, ahead.shape[1]), F32)
         ahead_bc[rows : rows + 8, :] = jnp.zeros((8, ahead_bc.shape[1]), F32)
         segs[rows : rows + 8, :] = jnp.full((8, 1), -1.0, F32)
-        for ref in (d_state, acc_z, acc_x, acc_bc, acc_dt, a1536, a768, a256, a128, rest):
+        for ref in (d_state, acc_z, acc_x, acc_bc, acc_dt, a1536, a768, a256, a128, rest, shared):
             ref[...] = jnp.zeros_like(ref)
 
-    line.step(block, 0)
+    @pl.when(block > 0)
+    def _():
+        line.step(2 * block + 1)
+
     seg_all = columns_of(segr_ref)
     segs[0:rows, :] = seg_all
     before = jnp.where(block == blocks - 1, -1.0, segp_ref[:, rows - 1 : rows].astype(F32))
     r, c_ = iotas(CHUNK, CHUNK)
-    upper = (r <= c_).astype(F32)
-    below = (r > c_).astype(F32)
-    seg_r, seg_l = iotas(inner, LANES)
-    to_head = (seg_r // (inner // heads) == seg_l).astype(BF16)
-    two_r, two_l = iotas(2 * CHUNK, LANES)
+    both_ways = jnp.concatenate([(r <= c_).astype(F32), (r > c_).astype(F32)], axis=1)
+    all_r, all_l = iotas(heads * CHUNK, LANES)
+    pick = (all_r // CHUNK == all_l).astype(BF16)
     decay_rate = -jnp.exp(hv_ref[1:2, :])
-    dsk = spread(hv_ref[2:3, :], heads)
+    dsk = spread(hv_ref[...], expand)[2:3, :]
     for piece in reversed(range(PIECES)):
         at = pl.ds(piece * CHUNK, CHUNK)
         span = slice(piece * CHUNK, (piece + 1) * CHUNK)
@@ -831,17 +886,21 @@
         n = bcu.shape[1] // 2
         b, c = bcu[:, :n], bcu[:, n:]
         scores = dot_t(c, b)
-        dt_x = spread(dt, heads)
+        last = cum[CHUNK - 1 : CHUNK, :]
+        flows = [dt, jnp.exp(cum) * keep, jnp.exp(last - cum) * tail]
+        flows.append(jnp.broadcast_to(jnp.exp(last) * keep[CHUNK - 1 : CHUNK, :], (8, LANES)))
+        wide = spread(jnp.concatenate(flows, axis=0), expand)
+        dt_x, enter_x, end_x = (wide[k * CHUNK : (k + 1) * CHUNK, :] for k in range(3))
+        carry = wide[3 * CHUNK : 3 * CHUNK + 1, :]
         v = dt_x * u
         v_low = v.astype(BF16)
         d_scores = jnp.zeros((CHUNK, CHUNK), F32)
-        d_cum = jnp.zeros((CHUNK, LANES), F32)
-        pieces = []
+        pieces, weighed = [], []
         for pair in range(heads // 2):
             lanes = slice(pair * LANES, (pair + 1) * LANES)
             dy_halves = jnp.concatenate(split_pair(dy_low[:, lanes]), axis=0)
             grads = dot_t(dy_halves, v_low[:, lanes])
-            mats, weighed = [], []
+            mats = []
             for k in range(2):
                 decay = decay_matrix(cum, cum_t, visible, 2 * pair + k)
                 grad = grads[k * CHUNK : (k + 1) * CHUNK, :]
@@ -850,14 +909,16 @@
                 weighed.append((grad * mat).astype(BF16))
                 mats.append(mat.astype(BF16))
             pieces.append(tdot(jnp.concatenate(mats, axis=0), dy_halves))
-            pick = (two_l == 2 * pair + two_r // CHUNK).astype(BF16)
-            d_cum = d_cum + dot(jnp.concatenate(weighed, axis=1), pick)
-            d_cum = d_cum - tdot(jnp.concatenate(weighed, axis=0), pick)
         old_low = st_ref[piece]
-        last = cum[CHUNK - 1 : CHUNK, :]
-        enter_x = spread(jnp.exp(cum) * keep, heads)
-        end_x = spread(jnp.exp(last - cum) * tail, heads)
-        carry = spread(jnp.exp(last) * keep[CHUNK - 1 : CHUNK, :], heads)
+        if piece == 0:
+            line.step(2 * block + 2)
+        else:
+
+            @pl.when(block == 0)
+            def _():
+                line.step(1)
+
+        d_cum = dot(jnp.concatenate(weighed, axis=1), pick) - tdot(jnp.concatenate(weighed, axis=0), pick)
         ds = d_state[...]
         ds_low = ds.astype(BF16)
         dv_state = end_x * dot(b, ds_low)
@@ -866,16 +927,18 @@
         dy_enter_low = dy_enter.astype(BF16)
         d_b = dot_t((end_x * v).astype(BF16), ds_low)
         d_c = dot_t(dy_enter_low, old_low)
-        e = dot((dy_enter * dot(c, old_low)).astype(BF16), to_head)
-        f = dot((dv_state * v).astype(BF16), to_head)
-        flow = jnp.sum(ds * old_low.astype(F32) * carry, axis=0, keepdims=True)
-        flow = dot(flow, to_head.astype(F32), HIGHEST)
+        flow = jnp.broadcast_to(jnp.sum(ds * old_low.astype(F32) * carry, axis=0, keepdims=True), (8, inner))
+        flow_low = flow.astype(BF16)
+        products = [dy_enter * dot(c, old_low), dv_state * v, dv * u, flow, flow - flow_low.astype(F32)]
+        sums = dot_t(jnp.concatenate(products, axis=0).astype(BF16), expand[0:LANES, :])
+        e, f, d_dt = (sums[k * CHUNK : (k + 1) * CHUNK, :] for k in range(3))
+        flow = sums[3 * CHUNK : 3 * CHUNK + 1, :] + sums[3 * CHUNK + 8 : 3 * CHUNK + 9, :]
         d_state[...] = carry * ds + tdot(c, dy_enter_low)
         d_scores_low = d_scores.astype(BF16)
         d_c = d_c + dot(d_scores_low, b)
         d_b = d_b + tdot(d_scores_low, c)
-        d_la = dot(upper, d_cum + e, HIGHEST) + dot(below, f, HIGHEST) + flow
-        d_dt = d_la * decay_rate + dot((dv * u).astype(BF16), to_head)
+        d_la = dot(both_ways, jnp.concatenate([d_cum + e, f], axis=0), HIGHEST) + flow
+        d_dt = d_la * decay_rate + d_dt
         d_pre = d_dt * sigmoid(pre)
         ddt_s[at, :] = d_pre.astype(BF16)
         a128[0:1, :] += jnp.sum(d_pre, axis=0, keepdims=True)
@@ -885,7 +948,6 @@
         d_bcu = jnp.concatenate([d_b, d_c], axis=1)
         ahead_bc[at, :] = d_bcu * (spbc * (1.0 + pbc * (1.0 - spbc)))
 
-    line.step(block, 1)
     for e in range(cube.events):
 
         @pl.when(block == min(e, blocks - 1))
@@ -909,17 +971,19 @@
         out[...] = total.astype(BF16)
         hist[rows : rows + 8, :] = hist[0:8, :]
     segs[rows : rows + 8, :] = segs[0:8, :]
+
+    @pl.when(block == 0)
+    def _():
+        for load in loads:
+            load.wait()
+
     partial = dot_t(dz_s[...], wz_ref[...]) + dot_t(dx_s[...], wx_ref[...])
     partial = partial + dot(ddt_s[...], wdt_s[...]) + dot_t(dbc_s[...], wbc_ref[...])
     for piece in range(PIECES):
         low = partial[piece * CHUNK : (piece + 1) * CHUNK, :].astype(BF16)
         for q in range(2):
-            xp_ref[0, 2 * piece + q] = low[q * 64 : q * 64 + 64, :]
-
-        @pl.when(first + block < pairs)
-        def _():
-            for q in range(2):
-                part[block, 2 * piece + q] = low[q * 64 : q * 64 + 64, :]
+            xp_ref[piece, q] = low[q * ROWS : q * ROWS + ROWS, :]
+            part[PIECES * block + PIECES - 1 - piece, q] = low[q * ROWS : q * ROWS + ROWS, :]
 
     x = x_ref[...].astype(F32)
     xr = x * inverse_rms(x)
@@ -942,28 +1006,29 @@
             stage[j % 2] = acc[w : w + 256, :].astype(BF16)
             copies.append(pltpu.make_async_copy(stage.at[j % 2], out.at[pl.ds(w, 256), :], stage_sem.at[j % 2]))
             copies[j].start()
+        line.step(steps - 1)
         copies[-2].wait()
         copies[-1].wait()
+        for j in range(width // LANES):
+            rest[16 * j : 16 * j + 16, :] = acc_dt[j * LANES : (j + 1) * LANES, :].T[0:16, :]
+        base = dt_rows(width)
+        for acc, out in ((a768, rest), (a128, rest), (a1536, shared), (a256, shared)):
+            if acc is a1536:
+                base = 0
+            for j in range(acc.shape[1] // LANES):
+                out[base : base + 8, :] = acc[:, j * LANES : (j + 1) * LANES]
+                base += 8
+        packed = [
+            pltpu.make_async_copy(rest, pack_ref, stage_sem.at[2]),
+            pltpu.make_async_copy(shared, shared_ref, stage_sem.at[3]),
+        ]
         for j in range(acc_bc.shape[0]):
-            low_bc[:, j * LANES : (j + 1) * LANES] = acc_bc[j].astype(BF16)
-        turned = pl.multiple_of(me * dt_rows(width), 8)
-        for j in range(width // LANES):
-            rest[pl.ds(turned + 16 * j, 16), :] = acc_dt[j * LANES : (j + 1) * LANES, :].T[0:16, :]
-        base = count * dt_rows(width)
-        for acc in (a1536, a256):
-            for j in range(acc.shape[1] // LANES):
-                rest[base : base + 8, :] = acc[:, j * LANES : (j + 1) * LANES]
-                base += 8
-        mine = pl.multiple_of(base + me * slot_rows(inner), 8)
-        for j in range(inner // LANES):
-            rest[pl.ds(mine + 8 * j, 8), :] = a768[:, j * LANES : (j + 1) * LANES]
-        rest[pl.ds(mine + inner // LANES * 8, 8), :] = a128[...]
-        first_copy = pltpu.make_async_copy(rest, pack_ref, stage_sem.at[2])
-        second_copy = pltpu.make_async_copy(low_bc, gb_ref, stage_sem.at[3])
-        first_copy.start()
-        second_copy.start()
-        first_copy.wait()
-        second_copy.wait()
+            there = gb_ref.at[:, pl.ds(j * LANES, LANES)]
+            packed.append(pltpu.make_async_copy(acc_bc.at[j], there, stage_sem.at[4 + j]))
+        for copy in packed:
+            copy.start()
+        for copy in packed:
+            copy.wait()
         line.close(carry_out)
 
 
@@ -1003,19 +1068,19 @@
     blocks = length // BLOCK
     chunks = length // CHUNK
     last = blocks - 1
-    pairs = 2 * blocks
-    all_steps = pairs + 2 * count - 3
-    n_fwd = (blocks + 4) // 2
-    n_bwd = blocks
+    pairs = 2 * chunks
+    all_steps = pairs + LAG * (2 * count - 3)
+    n_fwd = blocks + 4
+    n_bwd = chunks + 2
     rest = all_steps - n_fwd - n_bwd
     wdt = w_dt.T
     per_head = (dt_bias[None, :], a_log[None, :], d_skip[None, :])
-    x4 = x.reshape(blocks, 4, BLOCK // 4, width)
-    g4 = g.reshape(blocks, 4, BLOCK // 4, width)
+    x4 = x.reshape(chunks, 2, ROWS, width)
+    g4 = g.reshape(chunks, 2, ROWS, width)
     shape = jax.ShapeDtypeStruct
     anywhere = pl.BlockSpec(memory_space=pl.ANY)
-    pair_shape = (blocks, 4, BLOCK // 4, width)
-    carry_shape = shape((4, BLOCK // 4, width), BF16)
+    pair_shape = (chunks, 2, ROWS, width)
+    carry_shape = shape((LAG, 2, ROWS, width), BF16)
     res_shape = shape(pair_shape, BF16)
 
     def params(ident):
@@ -1034,7 +1099,7 @@
             rows_spec(BLOCK, width),
             rows_spec(BLOCK, width),
             pl.BlockSpec((1, BLOCK), lambda i: (0, i)),
-            *[whole_spec(w) for w in weights],
+            *[anywhere if w is w_out else whole_spec(w) for w in weights],
         ],
         out_specs=[
             rows_spec(BLOCK, inner),
@@ -1046,7 +1111,7 @@
             rows_spec(BLOCK, LANES),
             rows_spec(BLOCK, inner),
             pl.BlockSpec((PIECES, state_n, inner), lambda i: (i, 0, 0)),
-            pl.BlockSpec((1, 4, BLOCK // 4, width), lambda i: (i, 0, 0, 0)),
+            pl.BlockSpec((PIECES, 2, ROWS, width), lambda i: (i, 0, 0, 0)),
             fixed_spec(chunks, 8, CHUNK),
             fixed_spec(2 * inner, width // 2),
             anywhere,
@@ -1071,20 +1136,23 @@
             res_shape,
         ],
         scratch_shapes=[
+            pltpu.VMEM(w_out.shape, BF16),
+            pltpu.SemaphoreType.DMA,
             pltpu.VMEM((8, LANES), F32),
             pltpu.VMEM((LANES, width), BF16),
+            pltpu.VMEM((2 * LANES, inner), BF16),
             pltpu.VMEM((BLOCK + 8, inner), F32),
             pltpu.VMEM((BLOCK + 8, bcw), F32),
             pltpu.VMEM((BLOCK + 8, 1), F32),
             pltpu.VMEM((state_n, inner), F32),
-            pltpu.VMEM((2, BLOCK, inner), F32),
-            pltpu.VMEM((2, BLOCK, width), BF16),
+            pltpu.VMEM((RING, BLOCK, inner), F32),
+            pltpu.VMEM((RING, BLOCK, width), BF16),
             pltpu.VMEM((inner, width), F32),
             pltpu.VMEM((blocks, PIECES, 8, CHUNK), F32),
             pltpu.VMEM((count - 1, blocks, PIECES, 8, CHUNK), F32),
             pltpu.SemaphoreType.DMA((count - 1, blocks)),
             pltpu.SemaphoreType.DMA((count - 1, blocks)),
-            pltpu.VMEM((n_fwd, 4, BLOCK // 4, width), BF16),
+            pltpu.VMEM((n_fwd, 2, ROWS, width), BF16),
             *line_scratch(n_fwd, width),
         ],
         compiler_params=params(0),
@@ -1095,9 +1163,11 @@
     weights = (w_z, w_x, w_bc, wdt, norm_gain, out_gain, conv_x, conv_bc, *per_head)
     n_in = 13 + len(weights)
     bits = lax.axis_size("dp").bit_length() - 1
-    used = (width + bcw) // LANES * 8 + count * (slot_rows(inner) + dt_rows(width))
-    pack_rows = -(-used // 256) * 256
-    xp, gz, gx, gbc, pack, carry, gout, res_y, res_x = pl.pallas_call(
+    unit = 8 << bits
+    pack_rows = -(-(dt_rows(width) + slot_rows(inner)) // unit) * unit
+    shared_rows = -(-((width + bcw) // LANES * 8) // unit) * unit
+    kind = F32 if (width >> bits) % 16 else BF16
+    xp, gz, gx, gbc, pack, shared, carry, gout, res_y, res_x = pl.pallas_call(
         functools.partial(backward_kernel, heads, count, pairs, n_fwd, n_bwd),
         grid=(blocks,),
         in_specs=[
@@ -1114,27 +1184,32 @@
             pl.BlockSpec((1, BLOCK), lambda i: (0, last - i)),
             pl.BlockSpec((PIECES, 8, CHUNK), lambda i: (last - i, 0, 0)),
             rows_spec(BLOCK, width, last),
-            *[whole_spec(w) for w in weights],
+            *[anywhere] * 3,
+            *[whole_spec(w) for w in weights[3:]],
             *[anywhere] * 7,
         ],
         out_specs=[
-            pl.BlockSpec((1, 4, BLOCK // 4, width), lambda i: (last - i, 0, 0, 0)),
-            *[anywhere] * 8,
+            pl.BlockSpec((PIECES, 2, ROWS, width), lambda i: (last - i, 0, 0, 0)),
+            *[anywhere] * 9,
         ],
         out_shape=[
             shape(pair_shape, BF16),
             shape((width, inner), BF16),
             shape((width, inner), BF16),
-            shape((width, bcw), BF16),
+            shape((width, bcw), F32),
             shape((pack_rows, LANES), F32),
+            shape((shared_rows, LANES), F32),
             carry_shape,
             shape((2 * inner, width // 2), BF16),
             res_shape,
             res_shape,
         ],
         scratch_shapes=[
+            *[pltpu.VMEM(w.shape, BF16) for w in weights[:3]],
+            pltpu.SemaphoreType.DMA((3,)),
             pltpu.VMEM((8, LANES), F32),
             pltpu.VMEM((LANES, width), BF16),
+            pltpu.VMEM((2 * LANES, inner), BF16),
             pltpu.VMEM((BLOCK + 8, inner), F32),
             pltpu.VMEM((BLOCK + 8, bcw), F32),
             pltpu.VMEM((BLOCK + 8, 1), F32),
@@ -1152,57 +1227,59 @@
             pltpu.VMEM((8, bcw), F32),
             pltpu.VMEM((8, LANES), F32),
             pltpu.VMEM((pack_rows, LANES), F32),
-            pltpu.VMEM((width, bcw), BF16),
+            pltpu.VMEM((shared_rows, LANES), F32),
             pltpu.VMEM((2, 256, inner), BF16),
-            pltpu.SemaphoreType.DMA((4,)),
-            pltpu.VMEM((blocks, 4, BLOCK // 4, width), BF16),
+            pltpu.SemaphoreType.DMA((4 + bcw // LANES,)),
+            pltpu.VMEM((chunks, 2, ROWS, width), BF16),
             pltpu.SemaphoreType.DMA,
             *finals_scratch(width),
             *cube_scratch(2 * inner, width // 2, bits, BF16),
             *line_scratch(n_bwd, width),
         ],
-        input_output_aliases={n_in + 5: 7, n_in + 6: 8},
+        input_output_aliases={n_in + 5: 8, n_in + 6: 9},
         compiler_params=params(1),
         cost_estimate=cost(12 * 10**10, 10**8),
         name="backward_scan",
     )(z, p, xc, ys, pbc, bc, dtr, dn, st, segments, segments, scal, x, *weights, yp, x4, g4, carry, gout, res_y, res_x)
 
-    left = pairs - (n_fwd + n_bwd - (count - 1))
-    res_y, res_x, gz, gx, gbc, pack = pl.pallas_call(
+    left = pairs - (n_fwd + n_bwd - LAG * (count - 1))
+    res_y, res_x, gz, gx, gbc, pack, shared = pl.pallas_call(
         functools.partial(line_kernel, count, pairs, n_fwd + n_bwd, rest),
         grid=(rest,),
-        in_specs=[anywhere] * 3 + [whole_spec(norm_gain)] + [anywhere] * 7,
-        out_specs=[anywhere] * 6,
+        in_specs=[anywhere] * 3 + [whole_spec(norm_gain)] + [anywhere] * 8,
+        out_specs=[anywhere] * 7,
         out_shape=[
             res_shape,
             res_shape,
             shape((width, inner), BF16),
             shape((width, inner), BF16),
-            shape((width, bcw), BF16),
+            shape((width, bcw), kind),
             shape((pack_rows, LANES), F32),
+            shape((shared_rows, LANES), F32),
         ],
         scratch_shapes=[
-            pltpu.VMEM((left, 4, BLOCK // 4, width), BF16),
+            pltpu.VMEM((left, 2, ROWS, width), BF16),
             pltpu.SemaphoreType.DMA,
             *finals_scratch(width),
             *cube_scratch(width, inner, bits, BF16),
             *cube_scratch(width, inner, bits, BF16),
-            *cube_scratch(width, bcw, bits, BF16),
+            *cube_scratch(width, bcw, bits, F32),
             *cube_scratch(pack_rows, LANES, bits, F32),
-            *cross_scratch(count, width >> bits, bcw, BF16),
-            *cross_scratch(count, pack_rows >> bits, LANES, F32),
+            *cube_scratch(shared_rows, LANES, bits, F32),
+            *cross_scratch(count, width >> bits, bcw, kind),
+            *cross_scratch(count, shared_rows >> bits, LANES, F32),
             *line_scratch(rest, width),
         ],
-        input_output_aliases={9: 0, 10: 1},
+        input_output_aliases={10: 0, 11: 1},
         compiler_params=params(2),
         cost_estimate=cost(10**11, 3 * 10**8),
         name="line_sums",
-    )(xp, x4, g4, norm_gain, carry, gz, gx, gbc, pack, res_y, res_x)
+    )(xp, x4, g4, norm_gain, carry, gz, gx, gbc, pack, shared, res_y, res_x)
 
     wide = width // blocks
     tall = inner // blocks
     outs = pl.pallas_call(
-        functools.partial(finish_kernel, heads, count),
+        functools.partial(finish_kernel, heads),
         grid=(blocks,),
         in_specs=[
             rows_spec(BLOCK, width),
@@ -1215,6 +1292,7 @@
             pl.BlockSpec((tall, width // 2), lambda i: (i + blocks, 0)),
             rows_spec(wide, bcw),
             whole_spec(pack),
+            whole_spec(shared),
         ],
         out_specs=[
             rows_spec(BLOCK, width),
@@ -1254,7 +1332,7 @@
         ],
         compiler_params=pltpu.CompilerParams(vmem_limit_bytes=60 * 2**20, dimension_semantics=("arbitrary",)),
         name="finish",
-    )(x, res_y.reshape(length, width), res_x.reshape(length, width), scal, gz, gx, gout, gout, gbc, pack)
+    )(x, res_y.reshape(length, width), res_x.reshape(length, width), scal, gz, gx, gout, gout, gbc, pack, shared)
     result, grad_x, gz, gx, gout, grad_wbc, grad_wdt, ng, cx, bx, og, ds, cbc, bbc, dtb, al = outs
     return (
         result[None], grad_x[None], ng, gz, gx, grad_wbc, grad_wdt.T, cx, cbc, bx, bbc, dtb[0], al[0], ds[0],

time: 389 us -> 374 us (0.961)
  Pallas kernels: 387 us -> 373 us
    pallas_call x1, Pallas kernels: 114 us -> 88.5 us  [on_device(): pl.pallas_call(functools.partial(line_kernel, count, pairs, n_fwd + n_bwd...]
    pallas_call x1, Pallas kernels: 150 us -> 163 us  [on_device(): pl.pallas_call(functools.partial(backward_kernel, heads, count, pairs, n_...]
where the time goes in v3:
time: 374 us
  Pallas kernels  373 us (100%)
    pallas_call x1, Pallas kernels, on_device(): pl.pallas_call(functools.partial(backward_kernel, heads, count, pairs, n_...  163 us
    pallas_call x1, Pallas kernels, on_device(): pl.pallas_call(functools.partial(forward_kernel, heads, count, pairs, n_f...  99.9 us
    pallas_call x1, Pallas kernels, on_device(): pl.pallas_call(functools.partial(line_kernel, count, pairs, n_fwd + n_bwd...  88.5 us
    pallas_call x1, Pallas kernels, on_device(): pl.pallas_call(functools.partial(finish_kernel, heads), grid=(blocks,), i...  21.1 us

profile of v3, /device:TPU:0, one launch (start us, length us, event | category | flops | bytes accessed | tf_op | source)
XLA Modules:
  0.0 373.5 jit_solution(7476920074504177371)
XLA Ops:
  0.6 99.9 %forward_scan.1 = (f32[2048,768]{1,0:T(8,128)}, f32[2048,768]{1,0:T(8,128)}, bf16[2048,768]{1,0:T(8,128)(2,1)}, f32[2048,768]{1,0:T(8,128)}, f32[2048,256]{1,0:T...) custom-call(bf16[2048,1536]{1,0:T(8,128)(2,1)} %bitcast.16, ...), custom_call_target="tpu_custom_call" | custom-call | flops 89999998976 | bytes 100000000 | tf_op jit(solution)/shard_map/forward_scan/pallas_call | solution.py:1095
  100.5 163.1 %backward_scan.1 = (bf16[16,2,64,1536]{3,2,1,0:T(8,128)(2,1)}, bf16[1536,768]{1,0:T(8,128)(2,1)}, bf16[1536,768]{1,0:T(8,128)(2,1)}, f32[1536,256]{1,0:T(8,128)}...) custom-call(f32[2048,768]{1,0:T(8,128)} %get-tuple-element.64.z_ref,, ...), custom_call_target="tpu_custom_call", output_to_operand_aliasing={{8}: (29, {}), {9}: (30, {})} | custom-call | flops 120000004096 | bytes 100000000 | tf_op jit(solution)/shard_map/backward_scan/pallas_call | solution.py:1170
  263.7 88.5 %line_sums.1 = (bf16[16,2,64,1536]{3,2,1,0:T(8,128)(2,1)}, bf16[16,2,64,1536]{3,2,1,0:T(8,128)(2,1)}, bf16[1536,768]{1,0:T(8,128)(2,1)}, bf16[1536,768]{1,0:T(8,...) custom-call(bf16[16,2,64,1536]{3,2,1,0:T(8,128)(2,1)} %get-tuple-ele, ...), custom_call_target="tpu_custom_call", output_to_operand_aliasing={{0}: (10, {}), {1}: (11, {})} | custom-call | flops 99999997952 | bytes 300000000 | tf_op jit(solution)/shard_map/line_sums/pallas_call | solution.py:1246
  352.2 21.1 %finish.1 = (bf16[2048,1536]{1,0:T(8,128)(2,1)}, bf16[2048,1536]{1,0:T(8,128)(2,1)}, f32[1536,768]{1,0:T(8,128)}, f32[1536,768]{1,0:T(8,128)}, f32[768,1536]{1,0...) custom-call(bf16[2048,1536]{1,0:T(8,128)(2,1)} %bitcast.20, ...), custom_call_target="tpu_custom_call" | custom-call | tf_op jit(solution)/shard_map/finish/pallas_call | solution.py:1281

commit v4 on v3

--- a/solution.py
+++ b/solution.py
@@ -12,7 +12,8 @@
 BLOCK = 256
 PIECES = BLOCK // CHUNK
 LANES = 128
-ROWS = CHUNK // 2
+ROWS = CHUNK // 4
+PER = CHUNK // (2 * ROWS)
 LAG = 2
 RING = 4
 F32 = jnp.float32
@@ -524,13 +525,18 @@
     cubes = [
         Cube(order, (gz_ref, oz_ref, *scratch[0:6])),
         Cube(other, (gx_ref, ox_ref, *scratch[6:12])),
-        Cube(other, (gb_ref, ob_ref, *scratch[12:18]), (*scratch[30:34], peers)),
-        Cube(order, (pk_ref, op_ref, *scratch[18:24])),
-        Cube(order, (sh_ref, os_ref, *scratch[24:30]), (*scratch[34:38], peers)),
+        Cube(order, (pk_ref, op_ref, *scratch[12:18])),
+        Cube(order, (sh_ref, os_ref, *scratch[18:24]), (*scratch[24:28], peers)),
     ]
+    tall = gb_ref.shape[0] // 2
+    for j, way in enumerate((order, other)):
+        rows_j = pl.ds(j * tall, tall)
+        refs = scratch[28 + 10 * j : 38 + 10 * j]
+        cubes.append(Cube(way, (gb_ref.at[rows_j, :], ob_ref.at[rows_j, :], *refs[0:6]), (*refs[6:10], peers)))
+
     finals = Finals(pairs, x_any, g_any, row_of(ng_ref), rows, sems)
     line = Line(
-        count, pairs, first, steps, (res_y, res_x, *scratch[38:]), lambda q, i: part.at[2 * half - 1 - i, q], finals
+        count, pairs, first, steps, (res_y, res_x, *scratch[48:]), lambda q, i: part.at[2 * half - 1 - i, q], finals
     )
     at = pl.program_id(0)
 
@@ -546,10 +552,11 @@
         heard(*everyone)
 
     if len(order) == 3:
-        times = [0, 1, 4, 5, 6, 9, 10], [0, 1, 4, 5, 6, 9, 10], [0, 1, 4, 6, 8, 10, 11, 11]
+        times = [0, 2, 7, 9, 11, 15, 17], [0, 2, 7, 9, 12, 15, 17, 18]
     else:
-        times = (range(2 * len(order) + 2),) * 3
-    for cube, when in zip(cubes, (*times, times[0], times[2])):
+        times = (range(2 * len(order) + 2),) * 2
+    for cube in cubes:
+        when = times[0] if cube.across is None else times[1]
         for e in range(cube.events):
 
             @pl.when(at == min(when[e], steps - 1))
@@ -697,6 +704,12 @@
             ]
             halves = split_pair(v_low[:, pair * LANES : (pair + 1) * LANES])
             pieces.append(dot(jnp.concatenate(mats, axis=1), jnp.concatenate(halves, axis=0)))
+        if piece:
+
+            @pl.when(block < 2)
+            def _():
+                line.step(4 * block + 1)
+
         inside = jnp.concatenate(pieces, axis=1)
         old = state[...]
         old_low = old.astype(BF16)
@@ -717,22 +730,14 @@
                 load.wait()
 
         y_part = dot(scaled.astype(BF16), wo_ref[...]).astype(BF16)
-        for q in range(2):
-            yp_ref[piece, q] = y_part[q * ROWS : q * ROWS + ROWS, :]
-
-        @pl.when(block * PIECES + piece < part.shape[0])
-        def _():
+        for r in range(PER):
             for q in range(2):
-                at_pair = jnp.minimum(block * PIECES + piece, part.shape[0] - 1)
-                part[at_pair, q] = y_part[q * ROWS : q * ROWS + ROWS, :]
-
-        if piece == 0:
-            line.step(jnp.where(block < 4, 2 * block, block + 3))
-        else:
-
-            @pl.when((block < 3) | (block == blocks - 1))
-            def _():
-                line.step(jnp.where(block < 3, 2 * block + 1, steps - 1))
+                low = y_part[(2 * r + q) * ROWS : (2 * r + q + 1) * ROWS, :]
+                yp_ref[piece * PER + r, q] = low
+                part[(block * PIECES + piece) * PER + r, q] = low
+
+        later = jnp.where(block < 4, 3 * block + 2 + piece, 2 * block + 6 + piece)
+        line.step(jnp.where(block < 2, 4 * block + 2 * piece, later))
 
         squares.append(jnp.sum(gated * gated, axis=1, keepdims=True))
 
@@ -774,6 +779,10 @@
     for d in range(1, count):
         stat_copy(d, block).start()
 
+    @pl.when(block < 4)
+    def _():
+        line.step(jnp.where(block < 2, 4 * block + 3, 3 * block + 4))
+
     @pl.when(block >= RING - 1)
     def _():
         settle(block - (RING - 1))
@@ -801,7 +810,7 @@
     rows, inner = z_ref.shape
     width = x_ref.shape[1]
     block = pl.program_id(0)
-    blocks = steps // PIECES - 1
+    blocks = steps // (PIECES * PER)
     half = pairs // 2
     me = lax.axis_index("tensor")
     ng, og = row_of(ng_ref), row_of(og_ref)
@@ -840,7 +849,7 @@
 
     @pl.when(block > 0)
     def _():
-        line.step(2 * block + 1)
+        line.step(4 * block)
 
     seg_all = columns_of(segr_ref)
     segs[0:rows, :] = seg_all
@@ -910,14 +919,7 @@
                 mats.append(mat.astype(BF16))
             pieces.append(tdot(jnp.concatenate(mats, axis=0), dy_halves))
         old_low = st_ref[piece]
-        if piece == 0:
-            line.step(2 * block + 2)
-        else:
-
-            @pl.when(block == 0)
-            def _():
-                line.step(1)
-
+        line.step(4 * block + 2 - piece)
         d_cum = dot(jnp.concatenate(weighed, axis=1), pick) - tdot(jnp.concatenate(weighed, axis=0), pick)
         ds = d_state[...]
         ds_low = ds.astype(BF16)
@@ -981,10 +983,13 @@
     partial = partial + dot(ddt_s[...], wdt_s[...]) + dot_t(dbc_s[...], wbc_ref[...])
     for piece in range(PIECES):
         low = partial[piece * CHUNK : (piece + 1) * CHUNK, :].astype(BF16)
-        for q in range(2):
-            xp_ref[piece, q] = low[q * ROWS : q * ROWS + ROWS, :]
-            part[PIECES * block + PIECES - 1 - piece, q] = low[q * ROWS : q * ROWS + ROWS, :]
-
+        for r in range(PER):
+            for q in range(2):
+                part_low = low[(2 * r + q) * ROWS : (2 * r + q + 1) * ROWS, :]
+                xp_ref[piece * PER + r, q] = part_low
+                part[(block + 1) * PIECES * PER - 1 - piece * PER - r, q] = part_low
+
+    line.step(4 * block + 3)
     x = x_ref[...].astype(F32)
     xr = x * inverse_rms(x)
     a1536[0:1, :] += jnp.sum(partial * xr, axis=0, keepdims=True)
@@ -1006,7 +1011,6 @@
             stage[j % 2] = acc[w : w + 256, :].astype(BF16)
             copies.append(pltpu.make_async_copy(stage.at[j % 2], out.at[pl.ds(w, 256), :], stage_sem.at[j % 2]))
             copies[j].start()
-        line.step(steps - 1)
         copies[-2].wait()
         copies[-1].wait()
         for j in range(width // LANES):
@@ -1068,18 +1072,18 @@
     blocks = length // BLOCK
     chunks = length // CHUNK
     last = blocks - 1
-    pairs = 2 * chunks
+    pairs = length // ROWS
     all_steps = pairs + LAG * (2 * count - 3)
-    n_fwd = blocks + 4
-    n_bwd = chunks + 2
+    n_fwd = 2 * blocks + 6
+    n_bwd = pairs // 2
     rest = all_steps - n_fwd - n_bwd
     wdt = w_dt.T
     per_head = (dt_bias[None, :], a_log[None, :], d_skip[None, :])
-    x4 = x.reshape(chunks, 2, ROWS, width)
-    g4 = g.reshape(chunks, 2, ROWS, width)
+    x4 = x.reshape(pairs // 2, 2, ROWS, width)
+    g4 = g.reshape(pairs // 2, 2, ROWS, width)
     shape = jax.ShapeDtypeStruct
     anywhere = pl.BlockSpec(memory_space=pl.ANY)
-    pair_shape = (chunks, 2, ROWS, width)
+    pair_shape = (pairs // 2, 2, ROWS, width)
     carry_shape = shape((LAG, 2, ROWS, width), BF16)
     res_shape = shape(pair_shape, BF16)
 
@@ -1111,7 +1115,7 @@
             rows_spec(BLOCK, LANES),
             rows_spec(BLOCK, inner),
             pl.BlockSpec((PIECES, state_n, inner), lambda i: (i, 0, 0)),
-            pl.BlockSpec((PIECES, 2, ROWS, width), lambda i: (i, 0, 0, 0)),
+            pl.BlockSpec((PIECES * PER, 2, ROWS, width), lambda i: (i, 0, 0, 0)),
             fixed_spec(chunks, 8, CHUNK),
             fixed_spec(2 * inner, width // 2),
             anywhere,
@@ -1152,7 +1156,7 @@
             pltpu.VMEM((count - 1, blocks, PIECES, 8, CHUNK), F32),
             pltpu.SemaphoreType.DMA((count - 1, blocks)),
             pltpu.SemaphoreType.DMA((count - 1, blocks)),
-            pltpu.VMEM((n_fwd, 2, ROWS, width), BF16),
+            pltpu.VMEM(pair_shape, BF16),
             *line_scratch(n_fwd, width),
         ],
         compiler_params=params(0),
@@ -1166,7 +1170,7 @@
     unit = 8 << bits
     pack_rows = -(-(dt_rows(width) + slot_rows(inner)) // unit) * unit
     shared_rows = -(-((width + bcw) // LANES * 8) // unit) * unit
-    kind = F32 if (width >> bits) % 16 else BF16
+    kind = F32 if (width // 2 >> bits) % 16 else BF16
     xp, gz, gx, gbc, pack, shared, carry, gout, res_y, res_x = pl.pallas_call(
         functools.partial(backward_kernel, heads, count, pairs, n_fwd, n_bwd),
         grid=(blocks,),
@@ -1189,7 +1193,7 @@
             *[anywhere] * 7,
         ],
         out_specs=[
-            pl.BlockSpec((PIECES, 2, ROWS, width), lambda i: (last - i, 0, 0, 0)),
+            pl.BlockSpec((PIECES * PER, 2, ROWS, width), lambda i: (last - i, 0, 0, 0)),
             *[anywhere] * 9,
         ],
         out_shape=[
@@ -1230,7 +1234,7 @@
             pltpu.VMEM((shared_rows, LANES), F32),
             pltpu.VMEM((2, 256, inner), BF16),
             pltpu.SemaphoreType.DMA((4 + bcw // LANES,)),
-            pltpu.VMEM((chunks, 2, ROWS, width), BF16),
+            pltpu.VMEM(pair_shape, BF16),
             pltpu.SemaphoreType.DMA,
             *finals_scratch(width),
             *cube_scratch(2 * inner, width // 2, bits, BF16),
@@ -1263,11 +1267,13 @@
             *finals_scratch(width),
             *cube_scratch(width, inner, bits, BF16),
             *cube_scratch(width, inner, bits, BF16),
-            *cube_scratch(width, bcw, bits, F32),
             *cube_scratch(pack_rows, LANES, bits, F32),
             *cube_scratch(shared_rows, LANES, bits, F32),
-            *cross_scratch(count, width >> bits, bcw, kind),
             *cross_scratch(count, shared_rows >> bits, LANES, F32),
+            *cube_scratch(width // 2, bcw, bits, F32),
+            *cross_scratch(count, width // 2 >> bits, bcw, kind),
+            *cube_scratch(width // 2, bcw, bits, F32),
+            *cross_scratch(count, width // 2 >> bits, bcw, kind),
             *line_scratch(rest, width),
         ],
         input_output_aliases={10: 0, 11: 1},

time: 374 us -> 361 us (0.965)
  Pallas kernels: 373 us -> 360 us
    pallas_call x1, Pallas kernels: 163 us -> 150 us  [on_device(): pl.pallas_call(functools.partial(backward_kernel, heads, count, pairs, n_...]
    pallas_call x1, Pallas kernels: 99.9 us -> 105 us  [on_device(): pl.pallas_call(functools.partial(forward_kernel, heads, count, pairs, n_f...]
    pallas_call x1, Pallas kernels: 88.5 us -> 84 us  [on_device(): pl.pallas_call(functools.partial(line_kernel, count, pairs, n_fwd + n_bwd...]
where the time goes in v4:
time: 361 us
  Pallas kernels  360 us (100%)
    pallas_call x1, Pallas kernels, on_device(): pl.pallas_call(functools.partial(backward_kernel, heads, count, pairs, n_...  150 us
    pallas_call x1, Pallas kernels, on_device(): pl.pallas_call(functools.partial(forward_kernel, heads, count, pairs, n_f...  105 us
    pallas_call x1, Pallas kernels, on_device(): pl.pallas_call(functools.partial(line_kernel, count, pairs, n_fwd + n_bwd...  84 us
    pallas_call x1, Pallas kernels, on_device(): pl.pallas_call(functools.partial(finish_kernel, heads), grid=(blocks,), i...  21.1 us

profile of v4, /device:TPU:0, one launch (start us, length us, event | category | flops | bytes accessed | tf_op | source)
XLA Modules:
  0.0 360.9 jit_solution(4000077666911605863)
XLA Ops:
  0.6 104.7 %forward_scan.1 = (f32[2048,768]{1,0:T(8,128)}, f32[2048,768]{1,0:T(8,128)}, bf16[2048,768]{1,0:T(8,128)(2,1)}, f32[2048,768]{1,0:T(8,128)}, f32[2048,256]{1,0:T...) custom-call(bf16[2048,1536]{1,0:T(8,128)(2,1)} %bitcast.16, ...), custom_call_target="tpu_custom_call" | custom-call | flops 89999998976 | bytes 100000000 | tf_op jit(solution)/shard_map/forward_scan/pallas_call | solution.py:1099
  105.3 150.2 %backward_scan.1 = (bf16[32,2,32,1536]{3,2,1,0:T(8,128)(2,1)}, bf16[1536,768]{1,0:T(8,128)(2,1)}, bf16[1536,768]{1,0:T(8,128)(2,1)}, f32[1536,256]{1,0:T(8,128)}...) custom-call(f32[2048,768]{1,0:T(8,128)} %get-tuple-element.64.z_ref,, ...), custom_call_target="tpu_custom_call", output_to_operand_aliasing={{8}: (29, {}), {9}: (30, {})} | custom-call | flops 120000004096 | bytes 100000000 | tf_op jit(solution)/shard_map/backward_scan/pallas_call | solution.py:1174
  255.6 84.0 %line_sums.1 = (bf16[32,2,32,1536]{3,2,1,0:T(8,128)(2,1)}, bf16[32,2,32,1536]{3,2,1,0:T(8,128)(2,1)}, bf16[1536,768]{1,0:T(8,128)(2,1)}, bf16[1536,768]{1,0:T(8,...) custom-call(bf16[32,2,32,1536]{3,2,1,0:T(8,128)(2,1)} %get-tuple-ele, ...), custom_call_target="tpu_custom_call", output_to_operand_aliasing={{0}: (10, {}), {1}: (11, {})} | custom-call | flops 99999997952 | bytes 300000000 | tf_op jit(solution)/shard_map/line_sums/pallas_call | solution.py:1250
  339.6 21.1 %finish.1 = (bf16[2048,1536]{1,0:T(8,128)(2,1)}, bf16[2048,1536]{1,0:T(8,128)(2,1)}, f32[1536,768]{1,0:T(8,128)}, f32[1536,768]{1,0:T(8,128)}, f32[768,1536]{1,0...) custom-call(bf16[2048,1536]{1,0:T(8,128)(2,1)} %bitcast.20, ...), custom_call_target="tpu_custom_call" | custom-call | tf_op jit(solution)/shard_map/finish/pallas_call | solution.py:1287

commit v5 on v4

--- a/solution.py
+++ b/solution.py
@@ -426,7 +426,7 @@
     def crossing(self, d):
         mine, land, out_sem, in_sem, peers = self.across
         return pltpu.make_async_remote_copy(
-            src_ref=mine, dst_ref=land.at[d - 1], send_sem=out_sem.at[d - 1],
+            src_ref=mine, dst_ref=land.at[d], send_sem=out_sem.at[d - 1],
             recv_sem=in_sem.at[d - 1], device_id={"tensor": peers[d - 1]}, device_id_type=MESH,
         )
 
@@ -474,13 +474,17 @@
             return
         if self.across is not None:
             if e == count + 1:
-                size = self.rows >> count
-                total = self.total[self.span(self.inside(count), size), :]
-                for d in range(1, len(self.across[4]) + 1):
+                mine, land, _, _, peers = self.across
+                ranks = len(peers) + 1
+                for d in range(1, ranks):
                     self.crossing(d).wait()
-                    total = total + self.across[1][d - 1].astype(F32)
-                self.across[0][...] = total.astype(self.across[0].dtype)
-                self.turn(self.across[0])
+                land[0] = mine[...]
+                me = lax.axis_index("tensor")
+                total = land[me].astype(F32)
+                for rank in range(1, ranks):
+                    total = total + land[lax.rem(me - rank + ranks, ranks)].astype(F32)
+                mine[...] = total.astype(mine.dtype)
+                self.turn(mine)
                 return
             e = e - 1
         self.doubling(e - count - 1).wait()
@@ -502,7 +506,7 @@
 def cross_scratch(count, rows, cols, dtype):
     return [
         pltpu.VMEM((rows, cols), dtype),
-        pltpu.VMEM((count - 1, rows, cols), dtype),
+        pltpu.VMEM((count, rows, cols), dtype),
         pltpu.SemaphoreType.DMA((count - 1,)),
         pltpu.SemaphoreType.DMA((count - 1,)),
     ]
@@ -552,11 +556,14 @@
         heard(*everyone)
 
     if len(order) == 3:
-        times = [0, 2, 7, 9, 11, 15, 17], [0, 2, 7, 9, 12, 15, 17, 18]
+        first_times, other_times = [0, 2, 6, 8, 10, 14, 16], [0, 3, 7, 9, 11, 15, 17]
+        across_times = [0, 4, 8, 9, 12, 15, 16, 17]
     else:
-        times = (range(2 * len(order) + 2),) * 2
+        first_times = other_times = across_times = range(2 * len(order) + 2)
     for cube in cubes:
-        when = times[0] if cube.across is None else times[1]
+        when = other_times if cube is cubes[1] else first_times
+        if cube.across is not None:
+            when = across_times
         for e in range(cube.events):
 
             @pl.when(at == min(when[e], steps - 1))
@@ -621,11 +628,11 @@
 
 def forward_kernel(
     heads, count, pairs, steps, blocks,
-    x_ref, g_ref, segr_ref, wz_ref, wx_ref, wbc_ref, wdt_ref, wo_any, ng_ref, bx_ref, og_ref, bbc_ref, cx_ref, cbc_ref,
+    x_ref, g_ref, segr_ref, wz_any, wx_ref, wbc_ref, wdt_ref, wo_any, ng_ref, bx_ref, og_ref, bbc_ref, cx_ref, cbc_ref,
     dtb_ref, al_ref, dsk_ref,
     z_ref, p_ref, xc_ref, ys_ref, pbc_ref, bc_ref, dtr_ref, dn_ref, st_ref, yp_ref, scal_ref, wout_ref,
     carry_out, res_y, res_x,
-    wo_ref, w_sem, hv_ref, wdt_s, expand, hist, hist_bc, segs, state, scaled_s, g_s, acc_out, stat_mine, stat_land, stat_out, stat_in, part, *scratch,
+    wz_ref, wo_ref, w_sem, hv_ref, wdt_s, expand, hist, hist_bc, segs, state, scaled_s, g_s, acc_out, stat_mine, stat_land, stat_out, stat_in, part, *scratch,
 ):
     rows, width = x_ref.shape
     inner = z_ref.shape[1]
@@ -635,12 +642,14 @@
 
     line = Line(count, pairs, 0, steps, (res_y, res_x, *scratch), lambda q, i: part.at[i, q])
 
-    load = pltpu.make_async_copy(wo_any, wo_ref, w_sem)
+    load_z = pltpu.make_async_copy(wz_any, wz_ref, w_sem.at[0])
+    load = pltpu.make_async_copy(wo_any, wo_ref, w_sem.at[1])
     everyone = [(peer, peer >= 0) for peer in tensor_peers(count)]
 
     @pl.when(block == 0)
     def _():
         hello(everyone)
+        load_z.start()
         load.start()
         fill_heads(hv_ref, wdt_s, dtb_ref, al_ref, dsk_ref, wdt_ref)
         fill_expand(expand, heads)
@@ -652,7 +661,6 @@
 
     x = x_ref[...].astype(F32)
     xn = (x * inverse_rms(x) * ng).astype(BF16)
-    z_ref[...] = dot(xn, wz_ref[...])
     xc = dot(xn, wx_ref[...])
     bc = dot(xn, wbc_ref[...])
     dtr = dot_t(xn, wdt_s[...])
@@ -666,6 +674,11 @@
     same = [(segs[8 - k : 8 - k + rows, :] == seg_all).astype(F32) for k in range(1, 4)]
     p_ref[...] = conv_taps(hist, cx_ref, same, rows) + bx
     pbc_ref[...] = conv_taps(hist_bc, cbc_ref, same, rows) + bbc
+    @pl.when(block == 0)
+    def _():
+        load_z.wait()
+
+    z_ref[...] = dot(xn, wz_ref[...])
     g = g_ref[...]
     g_s[lax.rem(block, RING)] = g
     dt_all = softplus(dtr + hv_ref[0:1, :])
@@ -754,25 +767,29 @@
 
     def stat_copy(d, b):
         return pltpu.make_async_remote_copy(
-            src_ref=stat_mine.at[b], dst_ref=stat_land.at[d - 1, b], send_sem=stat_out.at[d - 1, b],
+            src_ref=stat_mine.at[b], dst_ref=stat_land.at[d, b], send_sem=stat_out.at[d - 1, b],
             recv_sem=stat_in.at[d - 1, b], device_id={"tensor": lax.rem(me + d, count)}, device_id_type=MESH,
         )
 
-    def settle(b):
-        total = stat_mine[b]
-        for d in range(1, count):
-            stat_copy(d, b).wait()
-            total = total + stat_land[d - 1, b]
-        place = lax.rem(b, RING)
-        low = []
-        for piece in range(PIECES):
-            r2 = lax.rsqrt(total[piece, 0:1, :] * (1.0 / (inner * count)) + EPS)
-            k2 = r2 * r2 * r2 * (total[piece, 1:2, :] * (1.0 / (inner * count)))
-            both = jnp.where(row_i == 0, r2, jnp.where(row_i == 1, k2, 0.0))
-            scal_ref[b * PIECES + piece] = both[0:8, :]
-            low.append((scaled_s[place, piece * CHUNK : (piece + 1) * CHUNK, :] * both.T[:, 0:1]).astype(BF16))
+    def settle(pair):
+        low, up = [], []
+        for b in (pair, pair + 1):
+            for d in range(1, count):
+                stat_copy(d, b).wait()
+            stat_land[0, b] = stat_mine[b]
+            total = stat_land[me, b]
+            for rank in range(1, count):
+                total = total + stat_land[lax.rem(me - rank + count, count), b]
+            place = lax.rem(b, RING)
+            for piece in range(PIECES):
+                r2 = lax.rsqrt(total[piece, 0:1, :] * (1.0 / (inner * count)) + EPS)
+                k2 = r2 * r2 * r2 * (total[piece, 1:2, :] * (1.0 / (inner * count)))
+                both = jnp.where(row_i == 0, r2, jnp.where(row_i == 1, k2, 0.0))
+                scal_ref[b * PIECES + piece] = both[0:8, :]
+                low.append((scaled_s[place, piece * CHUNK : (piece + 1) * CHUNK, :] * both.T[:, 0:1]).astype(BF16))
+            up.append(g_s[place])
         normed = jnp.concatenate(low, axis=0)
-        up = g_s[place]
+        up = jnp.concatenate(up, axis=0)
         for c in range(0, inner, 256):
             acc_out[c : c + 256, :] += tdot(normed[:, c : c + 256], up)
 
@@ -783,14 +800,13 @@
     def _():
         line.step(jnp.where(block < 2, 4 * block + 3, 3 * block + 4))
 
-    @pl.when(block >= RING - 1)
+    @pl.when((block >= RING - 1) & (lax.rem(block, 2) == 1))
     def _():
         settle(block - (RING - 1))
 
     @pl.when(block == blocks - 1)
     def _():
-        for b in range(1, RING):
-            settle(blocks - RING + b)
+        settle(blocks - 2)
         for c in range(0, inner, 256):
             low = acc_out[c : c + 256, :].astype(BF16)
             wout_ref[c : c + 256, :] = low[:, 0 : width // 2]
@@ -1004,6 +1020,7 @@
     @pl.when(block == blocks - 1)
     def _():
         bits = [(acc_z, gz_ref, w) for w in range(0, width, 256)] + [(acc_x, gx_ref, w) for w in range(0, width, 256)]
+        line.step(steps - 2)
         copies = []
         for j, (acc, out, w) in enumerate(bits):
             if j >= 2:
@@ -1011,6 +1028,7 @@
             stage[j % 2] = acc[w : w + 256, :].astype(BF16)
             copies.append(pltpu.make_async_copy(stage.at[j % 2], out.at[pl.ds(w, 256), :], stage_sem.at[j % 2]))
             copies[j].start()
+        line.step(steps - 1)
         copies[-2].wait()
         copies[-1].wait()
         for j in range(width // LANES):
@@ -1075,7 +1093,7 @@
     pairs = length // ROWS
     all_steps = pairs + LAG * (2 * count - 3)
     n_fwd = 2 * blocks + 6
-    n_bwd = pairs // 2
+    n_bwd = pairs // 2 + 2
     rest = all_steps - n_fwd - n_bwd
     wdt = w_dt.T
     per_head = (dt_bias[None, :], a_log[None, :], d_skip[None, :])
@@ -1103,7 +1121,7 @@
             rows_spec(BLOCK, width),
             rows_spec(BLOCK, width),
             pl.BlockSpec((1, BLOCK), lambda i: (0, i)),
-            *[anywhere if w is w_out else whole_spec(w) for w in weights],
+            *[anywhere if w is w_out or w is w_z else whole_spec(w) for w in weights],
         ],
         out_specs=[
             rows_spec(BLOCK, inner),
@@ -1140,8 +1158,9 @@
             res_shape,
         ],
         scratch_shapes=[
+            pltpu.VMEM(w_z.shape, BF16),
             pltpu.VMEM(w_out.shape, BF16),
-            pltpu.SemaphoreType.DMA,
+            pltpu.SemaphoreType.DMA((2,)),
             pltpu.VMEM((8, LANES), F32),
             pltpu.VMEM((LANES, width), BF16),
             pltpu.VMEM((2 * LANES, inner), BF16),
@@ -1153,7 +1172,7 @@
             pltpu.VMEM((RING, BLOCK, width), BF16),
             pltpu.VMEM((inner, width), F32),
             pltpu.VMEM((blocks, PIECES, 8, CHUNK), F32),
-            pltpu.VMEM((count - 1, blocks, PIECES, 8, CHUNK), F32),
+            pltpu.VMEM((count, blocks, PIECES, 8, CHUNK), F32),
             pltpu.SemaphoreType.DMA((count - 1, blocks)),
             pltpu.SemaphoreType.DMA((count - 1, blocks)),
             pltpu.VMEM(pair_shape, BF16),

time: 361 us -> 360 us (level)
    pallas_call x1, Pallas kernels: 84 us -> 78.2 us  [on_device(): pl.pallas_call(functools.partial(line_kernel, count, pairs, n_fwd + n_bwd...]
    pallas_call x1, Pallas kernels: 150 us -> 155 us  [on_device(): pl.pallas_call(functools.partial(backward_kernel, heads, count, pairs, n_...]
where the time goes in v5:
time: 360 us
  Pallas kernels  359 us (100%)
    pallas_call x1, Pallas kernels, on_device(): pl.pallas_call(functools.partial(backward_kernel, heads, count, pairs, n_...  155 us
    pallas_call x1, Pallas kernels, on_device(): pl.pallas_call(functools.partial(forward_kernel, heads, count, pairs, n_f...  105 us
    pallas_call x1, Pallas kernels, on_device(): pl.pallas_call(functools.partial(line_kernel, count, pairs, n_fwd + n_bwd...  78.2 us
    pallas_call x1, Pallas kernels, on_device(): pl.pallas_call(functools.partial(finish_kernel, heads), grid=(blocks,), i...  21.1 us

profile of v5, /device:TPU:0, one launch (start us, length us, event | category | flops | bytes accessed | tf_op | source)
XLA Modules:
  0.0 359.9 jit_solution(9079692622693787661)
XLA Ops:
  0.6 105.2 %forward_scan.1 = (f32[2048,768]{1,0:T(8,128)}, f32[2048,768]{1,0:T(8,128)}, bf16[2048,768]{1,0:T(8,128)(2,1)}, f32[2048,768]{1,0:T(8,128)}, f32[2048,256]{1,0:T...) custom-call(bf16[2048,1536]{1,0:T(8,128)(2,1)} %bitcast.16, ...), custom_call_target="tpu_custom_call" | custom-call | flops 89999998976 | bytes 100000000 | tf_op jit(solution)/shard_map/forward_scan/pallas_call | solution.py:1117
  105.8 154.5 %backward_scan.1 = (bf16[32,2,32,1536]{3,2,1,0:T(8,128)(2,1)}, bf16[1536,768]{1,0:T(8,128)(2,1)}, bf16[1536,768]{1,0:T(8,128)(2,1)}, f32[1536,256]{1,0:T(8,128)}...) custom-call(f32[2048,768]{1,0:T(8,128)} %get-tuple-element.64.z_ref,, ...), custom_call_target="tpu_custom_call", output_to_operand_aliasing={{8}: (29, {}), {9}: (30, {})} | custom-call | flops 120000004096 | bytes 100000000 | tf_op jit(solution)/shard_map/backward_scan/pallas_call | solution.py:1193
  260.4 78.2 %line_sums.1 = (bf16[32,2,32,1536]{3,2,1,0:T(8,128)(2,1)}, bf16[32,2,32,1536]{3,2,1,0:T(8,128)(2,1)}, bf16[1536,768]{1,0:T(8,128)(2,1)}, bf16[1536,768]{1,0:T(8,...) custom-call(bf16[32,2,32,1536]{3,2,1,0:T(8,128)(2,1)} %get-tuple-ele, ...), custom_call_target="tpu_custom_call", output_to_operand_aliasing={{0}: (10, {}), {1}: (11, {})} | custom-call | flops 99999997952 | bytes 300000000 | tf_op jit(solution)/shard_map/line_sums/pallas_call | solution.py:1269
  338.6 21.1 %finish.1 = (bf16[2048,1536]{1,0:T(8,128)(2,1)}, bf16[2048,1536]{1,0:T(8,128)(2,1)}, f32[1536,768]{1,0:T(8,128)}, f32[1536,768]{1,0:T(8,128)}, f32[768,1536]{1,0...) custom-call(bf16[2048,1536]{1,0:T(8,128)(2,1)} %bitcast.20, ...), custom_call_target="tpu_custom_call" | custom-call | tf_op jit(solution)/shard_map/finish/pallas_call | solution.py:1306

commit v6 on v5

--- a/solution.py
+++ b/solution.py
@@ -385,7 +385,8 @@
         (self.src, self.out, self.total, self.send, self.land, self.out_sem, self.in_sem, self.local) = refs
         self.rows = self.src.shape[0]
         self.bits = dp_bits()
-        self.events = 2 * len(order) + (1 if across is None else 2)
+        self.turns = 0 if across is None else len(across[4])
+        self.events = 2 * len(order) + 1 + self.turns
 
     def start_of(self, depth):
         at = 0
@@ -423,11 +424,11 @@
             device_id={"dp": partner}, device_id_type=MESH,
         )
 
-    def crossing(self, d):
-        mine, land, out_sem, in_sem, peers = self.across
+    def crossing(self, t):
+        mine, land, out_sem, in_sem, partners = self.across
         return pltpu.make_async_remote_copy(
-            src_ref=mine, dst_ref=land.at[d], send_sem=out_sem.at[d - 1],
-            recv_sem=in_sem.at[d - 1], device_id={"tensor": peers[d - 1]}, device_id_type=MESH,
+            src_ref=mine, dst_ref=land.at[t], send_sem=out_sem.at[t], recv_sem=in_sem.at[t],
+            device_id={"tensor": partners[t]}, device_id_type=MESH,
         )
 
     def turn(self, part):
@@ -463,8 +464,7 @@
             part = self.total[self.span(at, size), :]
             if e == count and self.across is not None:
                 self.across[0][...] = part.astype(self.across[0].dtype)
-                for d in range(1, len(self.across[4]) + 1):
-                    self.crossing(d).start()
+                self.crossing(0).start()
                 return
             self.send[0:size, :] = part.astype(self.send.dtype)
             if e < count:
@@ -473,20 +473,17 @@
                 self.turn(self.send.at[pl.ds(0, size), :])
             return
         if self.across is not None:
-            if e == count + 1:
-                mine, land, _, _, peers = self.across
-                ranks = len(peers) + 1
-                for d in range(1, ranks):
-                    self.crossing(d).wait()
-                land[0] = mine[...]
-                me = lax.axis_index("tensor")
-                total = land[me].astype(F32)
-                for rank in range(1, ranks):
-                    total = total + land[lax.rem(me - rank + ranks, ranks)].astype(F32)
-                mine[...] = total.astype(mine.dtype)
-                self.turn(mine)
+            t = e - count - 1
+            if t < self.turns:
+                mine, land = self.across[0], self.across[1]
+                self.crossing(t).wait()
+                mine[...] = (mine[...].astype(F32) + land[t].astype(F32)).astype(mine.dtype)
+                if t + 1 < self.turns:
+                    self.crossing(t + 1).start()
+                else:
+                    self.turn(mine)
                 return
-            e = e - 1
+            e = e - self.turns
         self.doubling(e - count - 1).wait()
         if e < 2 * count:
             self.doubling(e - count).start()
@@ -504,12 +501,18 @@
 
 
 def cross_scratch(count, rows, cols, dtype):
+    turns = count.bit_length() - 1
     return [
         pltpu.VMEM((rows, cols), dtype),
-        pltpu.VMEM((count, rows, cols), dtype),
-        pltpu.SemaphoreType.DMA((count - 1,)),
-        pltpu.SemaphoreType.DMA((count - 1,)),
+        pltpu.VMEM((turns, rows, cols), dtype),
+        pltpu.SemaphoreType.DMA((turns,)),
+        pltpu.SemaphoreType.DMA((turns,)),
     ]
+
+
+def tensor_partners(count):
+    me = lax.axis_index("tensor")
+    return [me + (1 - 2 * lax.rem(me // 2**b, 2)) * 2**b for b in range(count.bit_length() - 1)]
 
 
 def tensor_peers(count):
@@ -526,17 +529,18 @@
     order = list(range(len(dp_bits())))
     other = order[:1] + order[:0:-1]
     peers = tensor_peers(count)
+    partners = tensor_partners(count)
     cubes = [
         Cube(order, (gz_ref, oz_ref, *scratch[0:6])),
         Cube(other, (gx_ref, ox_ref, *scratch[6:12])),
         Cube(order, (pk_ref, op_ref, *scratch[12:18])),
-        Cube(order, (sh_ref, os_ref, *scratch[18:24]), (*scratch[24:28], peers)),
+        Cube(order, (sh_ref, os_ref, *scratch[18:24]), (*scratch[24:28], partners)),
     ]
     tall = gb_ref.shape[0] // 2
     for j, way in enumerate((order, other)):
         rows_j = pl.ds(j * tall, tall)
         refs = scratch[28 + 10 * j : 38 + 10 * j]
-        cubes.append(Cube(way, (gb_ref.at[rows_j, :], ob_ref.at[rows_j, :], *refs[0:6]), (*refs[6:10], peers)))
+        cubes.append(Cube(way, (gb_ref.at[rows_j, :], ob_ref.at[rows_j, :], *refs[0:6]), (*refs[6:10], partners)))
 
     finals = Finals(pairs, x_any, g_any, row_of(ng_ref), rows, sems)
     line = Line(
@@ -557,9 +561,9 @@
 
     if len(order) == 3:
         first_times, other_times = [0, 2, 6, 8, 10, 14, 16], [0, 3, 7, 9, 11, 15, 17]
-        across_times = [0, 4, 8, 9, 12, 15, 16, 17]
+        across_times = [0, 4, 8, 9, 10, 12, 15, 16, 17]
     else:
-        first_times = other_times = across_times = range(2 * len(order) + 2)
+        first_times = other_times = across_times = range(2 * len(order) + 4)
     for cube in cubes:
         when = other_times if cube is cubes[1] else first_times
         if cube.across is not None:

time: 360 us -> 359 us (level)
  no operation moved by 1% of the time
where the time goes in v6:
time: 359 us
  Pallas kernels  358 us (100%)
    pallas_call x1, Pallas kernels, on_device(): pl.pallas_call(functools.partial(backward_kernel, heads, count, pairs, n_...  155 us
    pallas_call x1, Pallas kernels, on_device(): pl.pallas_call(functools.partial(forward_kernel, heads, count, pairs, n_f...  105 us
    pallas_call x1, Pallas kernels, on_device(): pl.pallas_call(functools.partial(line_kernel, count, pairs, n_fwd + n_bwd...  77 us
    pallas_call x1, Pallas kernels, on_device(): pl.pallas_call(functools.partial(finish_kernel, heads), grid=(blocks,), i...  21.1 us

profile of v6, /device:TPU:0, one launch (start us, length us, event | category | flops | bytes accessed | tf_op | source)
XLA Modules:
  0.0 358.6 jit_solution(15518090965667432149)
XLA Ops:
  0.6 105.2 %forward_scan.1 = (f32[2048,768]{1,0:T(8,128)}, f32[2048,768]{1,0:T(8,128)}, bf16[2048,768]{1,0:T(8,128)(2,1)}, f32[2048,768]{1,0:T(8,128)}, f32[2048,256]{1,0:T...) custom-call(bf16[2048,1536]{1,0:T(8,128)(2,1)} %bitcast.16, ...), custom_call_target="tpu_custom_call" | custom-call | flops 89999998976 | bytes 100000000 | tf_op jit(solution)/shard_map/forward_scan/pallas_call | solution.py:1121
  105.8 154.5 %backward_scan.1 = (bf16[32,2,32,1536]{3,2,1,0:T(8,128)(2,1)}, bf16[1536,768]{1,0:T(8,128)(2,1)}, bf16[1536,768]{1,0:T(8,128)(2,1)}, f32[1536,256]{1,0:T(8,128)}...) custom-call(f32[2048,768]{1,0:T(8,128)} %get-tuple-element.64.z_ref,, ...), custom_call_target="tpu_custom_call", output_to_operand_aliasing={{8}: (29, {}), {9}: (30, {})} | custom-call | flops 120000004096 | bytes 100000000 | tf_op jit(solution)/shard_map/backward_scan/pallas_call | solution.py:1197
  260.4 77.0 %line_sums.1 = (bf16[32,2,32,1536]{3,2,1,0:T(8,128)(2,1)}, bf16[32,2,32,1536]{3,2,1,0:T(8,128)(2,1)}, bf16[1536,768]{1,0:T(8,128)(2,1)}, bf16[1536,768]{1,0:T(8,...) custom-call(bf16[32,2,32,1536]{3,2,1,0:T(8,128)(2,1)} %get-tuple-ele, ...), custom_call_target="tpu_custom_call", output_to_operand_aliasing={{0}: (10, {}), {1}: (11, {})} | custom-call | flops 99999997952 | bytes 300000000 | tf_op jit(solution)/shard_map/line_sums/pallas_call | solution.py:1273
  337.3 21.1 %finish.1 = (bf16[2048,1536]{1,0:T(8,128)(2,1)}, bf16[2048,1536]{1,0:T(8,128)(2,1)}, f32[1536,768]{1,0:T(8,128)}, f32[1536,768]{1,0:T(8,128)}, f32[768,1536]{1,0...) custom-call(bf16[2048,1536]{1,0:T(8,128)(2,1)} %bitcast.20, ...), custom_call_target="tpu_custom_call" | custom-call | tf_op jit(solution)/shard_map/finish/pallas_call | solution.py:1310
